TPU v7x, 256 devices: a whole 4x4x8 slice. The times are simulated.
256 devices in a mesh: inst: 16 (over z_lo, x), section: 2 (over z_hi), tensor: 8 (over y, core).
Axes of the slice: x: 4, y: 4, z: 8 (z_hi: 2, z_lo: 4; z = z_hi * 4 + z_lo), core: 2. Of those that a mesh axis runs over, the one named last changes fastest.
Arguments:
- query_rows: bfloat16 [512, 4096], P('inst', 'tensor'), may hold values from -6 to 6
- new_kv: bfloat16 [512, 2, 1024], P('inst', None, 'tensor'), may hold values from -6 to 6
- residual: bfloat16 [512, 4096], P('inst', 'tensor'), may hold values from -6 to 6
- kv_cache: bfloat16 [2, 2048, 2, 128, 1024], P('section', 'inst', None, None, 'tensor'), may hold values from -6 to 6
- page_table: int32 [512, 4], P('inst'), may hold values from 0 to 127, as said below
- lengths: int32 [512], P('inst'), may hold values from 1 to 512, 131072 in all
- migrate_ids: int32 [128], P('inst'), may hold values from 0 to 31, as said below
- projection: bfloat16 [2, 4096, 4096], P('section', None, 'tensor')
- kv_weight: bfloat16 [4096, 2, 1024], P(None, None, 'tensor')
- norm_gain: float32 [4096], replicated, may hold values from 0.5 to 1.5
Outputs:
- attention_out: bfloat16 [2, 512, 4096], P('section', 'inst', 'tensor')
- hidden_out: bfloat16 [512, 4096], P('inst', 'tensor')
- migrated: bfloat16 [2, 128, 4, 2, 128, 1024], P('section', 'inst', None, None, None, 'tensor')
Inputs may be any that keep to these rules, and one draw needn't show every extreme that they name: `page_table`: the 4 entries of a replica's 32 rows together name every page of its pool once. `migrate_ids`: the 8 ids of one replica are distinct requests of that replica.
All inputs are finite; a program needn't handle non-finite values. No bound on the sum of `lengths` on one device may be relied on, other than what follows from the above.
Results may differ from a plain program's by a relative error of at most 0.0065.
Values may be sent and summed in bfloat16 or wider, within the bound.
No kernel may reach another device: no remote copies, remote signals or barrier semaphores. Data moves between devices by JAX's collectives and lax.ppermute only.
A program may use at most 128 MiB of HBM per device.

v0:
```python
import jax
import jax.numpy as jnp
from jax import lax
from jax.sharding import PartitionSpec as P

HDIM = 128


def from_behind(array, axis, by):
    devices = lax.axis_size(axis)
    pairs = [(i, i + by) for i in range(devices) if 0 <= i + by < devices]
    return lax.ppermute(array, axis, pairs)


def from_behind_2(block, axis, distance):
    devices = range(lax.axis_size(axis))
    route = [((i - distance) % len(devices), i) for i in devices]
    return lax.ppermute(block, axis, route)


def attend(queries, fresh_rows, page_pool, table_rows, length_rows):
    count_rows = queries.shape[0]
    kv_width = page_pool.shape[-1]
    kv_heads = kv_width // HDIM
    group_size = queries.shape[1] // kv_width
    page_data = jnp.take(page_pool, table_rows, axis=0)
    span_len = page_data.shape[1] * page_data.shape[3]
    key_rows = page_data[:, :, 0].reshape(count_rows, span_len, kv_heads, HDIM)
    value_rows = page_data[:, :, 1].reshape(count_rows, span_len, kv_heads, HDIM)
    grouped = queries.reshape(count_rows, kv_heads, group_size, HDIM)
    score_scale = HDIM ** (-0.5)
    scores = (
        jnp.einsum("nkgd,ntkd->nkgt", grouped, key_rows, preferred_element_type=jnp.float32)
        * score_scale
    )
    fresh_key = fresh_rows[:, 0].reshape(count_rows, kv_heads, HDIM)
    fresh_value = fresh_rows[:, 1].reshape(count_rows, kv_heads, 1, HDIM).astype(jnp.float32)
    fresh_score = (
        jnp.einsum("nkgd,nkd->nkg", grouped, fresh_key, preferred_element_type=jnp.float32)
        * score_scale
    )
    positions = lax.broadcasted_iota(jnp.int32, (count_rows, span_len), 1)
    valid = positions < (length_rows - 1)[:, None]
    scores = jnp.where(valid[:, None, None, :], scores, jnp.float32(-1e30))
    highest = jnp.maximum(jnp.max(scores, axis=-1), fresh_score)
    weights = jnp.exp(scores - highest[..., None])
    fresh_weight = jnp.exp(fresh_score - highest)
    denominator = jnp.sum(weights, axis=-1) + fresh_weight
    summed = jnp.einsum(
        "nkgt,ntkd->nkgd",
        weights.astype(jnp.bfloat16),
        value_rows,
        preferred_element_type=jnp.float32,
    )
    summed = summed + fresh_weight.astype(jnp.bfloat16).astype(jnp.float32)[..., None] * fresh_value
    return (summed / denominator[..., None]).astype(jnp.bfloat16).reshape(count_rows, -1)


def gather_moved(page_pool, table_rows, length_rows, moved_ids):
    moved_table = jnp.take(table_rows, moved_ids, axis=0)
    moved_len = jnp.take(length_rows, moved_ids)
    page_data = jnp.take(page_pool, moved_table, axis=0)
    page_size = page_data.shape[3]
    page_used = (
        lax.broadcasted_iota(jnp.int32, moved_table.shape, 1) * page_size < moved_len[:, None]
    )
    kept = jnp.where(page_used[:, :, None, None, None], page_data, jnp.zeros_like(page_data))
    return (kept, moved_len)


def write_rows(kept, moved_len, moved_new):
    page_count = kept.shape[1]
    page_size = kept.shape[3]
    positions = lax.broadcasted_iota(jnp.int32, (page_count, page_size), 0) * page_size
    positions = positions + lax.broadcasted_iota(jnp.int32, (page_count, page_size), 1)
    write_mask = positions[None] == (moved_len - 1)[:, None, None]
    return jnp.where(write_mask[:, :, None, :, None], moved_new[:, None, :, None, :], kept)


def local(
    query_rows,
    new_kv,
    residual,
    kv_cache,
    page_table,
    lengths,
    migrate_ids,
    projection,
    kv_weight,
    norm_gain,
):
    leading = lax.axis_index("section") == 0
    tensor_index = lax.axis_index("tensor")
    page_pool = kv_cache[0]
    weight_local = projection[0]
    share_width = residual.shape[1]
    full_width = share_width * lax.axis_size("tensor")
    count_rows = query_rows.shape[0]
    col_start = tensor_index * share_width
    kept, moved_len = gather_moved(page_pool, page_table, lengths, migrate_ids)

    def first_layer():
        first_attn = attend(query_rows, new_kv, page_pool, page_table, lengths)
        partial_value = jnp.einsum(
            "nj,dj->nd", first_attn, weight_local, preferred_element_type=jnp.float32
        )
        own_cols = lax.dynamic_slice_in_dim(
            partial_value, col_start, share_width, 1
        ) + residual.astype(jnp.float32)
        return (first_attn, lax.dynamic_update_slice_in_dim(partial_value, own_cols, col_start, 1))

    def first_skipped():
        return (
            jnp.zeros(query_rows.shape, jnp.bfloat16),
            jnp.zeros((count_rows, full_width), jnp.float32),
        )

    first_attn, partial_value = lax.cond(leading, first_layer, first_skipped)
    summed_rows = lax.psum(partial_value, "tensor").astype(jnp.bfloat16)
    arrived = from_behind(summed_rows, "section", 1)
    held = jnp.where(leading, summed_rows, arrived)
    hidden_share = lax.dynamic_slice_in_dim(held, col_start, share_width, 1)
    hidden_float = arrived.astype(jnp.float32)
    mean_square = jnp.mean(hidden_float * hidden_float, axis=-1, keepdims=True)
    normed = (hidden_float * lax.rsqrt(mean_square + 1e-05) * norm_gain).astype(jnp.bfloat16)

    def second_layer():
        second_query = jnp.dot(normed, weight_local, preferred_element_type=jnp.float32).astype(
            jnp.bfloat16
        )
        second_kv = jnp.einsum(
            "nd,dck->nck", normed, kv_weight, preferred_element_type=jnp.float32
        ).astype(jnp.bfloat16)
        return (attend(second_query, second_kv, page_pool, page_table, lengths), second_kv)

    def second_skipped():
        return (jnp.zeros(query_rows.shape, jnp.bfloat16), jnp.zeros(new_kv.shape, jnp.bfloat16))

    second_attn, second_kv = lax.cond(leading, second_skipped, second_layer)
    attn_block = jnp.where(leading, first_attn, second_attn)[None]
    layer_rows = jnp.where(leading, new_kv, second_kv)
    moved_new = jnp.take(layer_rows, migrate_ids, axis=0)
    updated = write_rows(kept, moved_len, moved_new)
    moved_pages = from_behind_2(updated, "inst", 1)
    return (attn_block, hidden_share, moved_pages[None])


def solution(mesh):
    return jax.shard_map(
        local,
        mesh=mesh,
        in_specs=(
            P("inst", "tensor"),
            P("inst", None, "tensor"),
            P("inst", "tensor"),
            P("section", "inst", None, None, "tensor"),
            P("inst", None),
            P("inst"),
            P("inst"),
            P("section", None, "tensor"),
            P(None, None, "tensor"),
            P(),
        ),
        out_specs=(
            P("section", "inst", "tensor"),
            P("inst", "tensor"),
            P("section", "inst", None, None, None, "tensor"),
        ),
        check_vma=False,
    )
```

profile of v0, /device:TPU:216, one launch (start us, length us, event | category | flops | bytes accessed | tf_op | source)
XLA Modules:
  0.0 159.5 jit_solution(5151288596587853660)
XLA Ops:
  0.6 1.5 conditional.2
  0.7 0.6 broadcast.234
  1.3 0.8 broadcast.235
  2.1 28.8 %all-reduce.1 = bf16[32,4096]{1,0:T(8,128)(2,1)S(1)} all-reduce(f32[32,4096]{1,0:T(8,128)} %get-tuple-element.51), channel_id=1, replica_groups=mesh['inst'=16,'section'=2,'tensor'=8] {'tensor'}, use_global_device_ids=true, to_apply=%region_4.6 | all-reduce | flops 131072 | bytes 786432 | tf_op jit(solution)/shard_map/psum | solution.py:119
  30.9 1.3 collective-permute-start
  32.2 0.8 copy.34
  33.0 1.3 gather_fusion.2
  35.3 4.3 %gather_fusion.5 = bf16[32,2,128,128]{3,2,1,0:T(8,128)(2,1)S(1)} fusion(bf16[128,2,128,128]{3,2,1,0:T(8,128)(2,1)} %bitcast.64, s32[1024]{0:T(1024)S(1)} %pad_clamp_fusion.2), kind=kCustom, calls=%fused_computation.5 | custom fusion | bytes 4194432 | tf_op jit(solution)/shard_map/jit(_take)/gather | solution.py:62
  39.7 36.4 %collective-permute-done = bf16[32,4096]{1,0:T(8,128)(2,1)S(1)} collective-permute-done((bf16[32,4096]{1,0:T(8,128)(2,1)S(1)}, bf16[32,4096]{1,0:T(8,128)(2,1)S(1)}, u32[]{:S(2)}, u32[]{:S(2)}) %collective-permute-start) | collective-permute-done | bytes 262176 | tf_op jit(solution)/shard_map/ppermute | solution.py:12
  76.5 29.3 %conditional.3 = (bf16[32,512]{1,0:T(8,128)(2,1)S(1)}, bf16[32,2,128]{2,0,1:T(8,128)(2,1)S(1)}) conditional(s32[]{:T(128)} %convert_element_type.76, (s32[32]{0:T(128)S(1)}, bf16[32,4096]{1,0:T(8,128)(2,1)S(1)}, bf16[4096,512]{1,0:T(8,128)(2,1)}, bf16[128,2,128,128]{3,2,1,0:T(8,128)(2,1)}, s32[32,4]{0,1:T(4,128)S(1)}, ...), branch_computations={%region_6.10_spmd, %region_9.11_spmd} | conditional | flops 239680416 | bytes 66716304 | solution.py:139
  76.6 2.1 %fusion.17 = bf16[32,2,128]{2,0,1:T(8,128)(2,1)S(1)} fusion(bf16[4096,2,128]{2,1,0:T(2,128)(2,1)} %get-tuple-element.87, bf16[32,4096]{1,0:T(8,128)(2,1)S(1)} %get-tuple-element.38), kind=kOutput, calls=%fused_computation.42 | convolution fusion | flops 67117056 | bytes 2375680 | tf_op jit(solution)/shard_map/cond/branch_0_fun/nd,dck->nck/dot_general | solution.py:131
  78.7 3.0 %convolution_convert_fusion = bf16[32,512]{1,0:T(8,128)(2,1)S(1)} fusion(bf16[32,4096]{1,0:T(8,128)(2,1)S(1)} %get-tuple-element.38, bf16[4096,512]{1,0:T(8,128)(2,1)} %get-tuple-element.39), kind=kOutput, calls=%fused_computation.41 | convolution fusion | flops 134234112 | bytes 4489216 | tf_op jit(solution)/shard_map/cond/branch_0_fun/dot_general | solution.py:128
  82.1 10.0 %gather_fusion.1 = bf16[128,2,128,128]{3,2,1,0:T(8,128)(2,1)} fusion(bf16[128,2,128,128]{3,2,1,0:T(8,128)(2,1)} %get-tuple-element.40, s32[1024]{0:T(1024)S(1)} %pad_clamp_fusion.1), kind=kCustom, calls=%fused_computation.1.clone | custom fusion | bytes 16777728 | tf_op jit(solution)/shard_map/cond/branch_0_fun/jit(_take)/gather | solution.py:26
  92.1 7.4 %copy_select_fusion.1 = bf16[32,4,2,128,128]{4,3,1,0,2:T(8,128)(2,1)} fusion(bf16[32,4,2,128,128]{4,3,2,1,0:T(8,128)(2,1)} %bitcast.67, pred[32,4]{1,0:T(8,128)(4,1)S(1)} %compare_and_fusion.1), kind=kLoop, calls=%fused_computation.33 | loop fusion | flops 4194304 | bytes 16777344 | tf_op jit(solution)/shard_map/cond/branch_0_fun/jit(_take)/select_n | solution.py:26
  99.5 4.0 %fusion.34 = (bf16[32,4,1,128,128]{4,3,1,0,2:T(8,128)(2,1)S(1)}, bf16[32,4,1,128,128]{4,3,1,0,2:T(8,128)(2,1)S(1)}) fusion(bf16[32,4,2,128,128]{4,3,1,0,2:T(8,128)(2,1)} %copy_select_fusion.1), kind=kLoop, calls=%fused_computation.90 | loop fusion | bytes 16777216 | tf_op jit(solution)/shard_map/cond/branch_0_fun/slice | solution.py:28
  103.5 1.3 fusion.35
  105.0 0.7 fusion.16
  105.8 0.6 gather_fusion.3
  106.5 1.8 %select_select_fusion = bf16[8,4,2,128,128]{4,3,2,1,0:T(8,128)(2,1)} fusion(bf16[8,4,2,128,128]{4,3,2,1,0:T(8,128)(2,1)S(1)} %bitcast.72, pred[8,4]{1,0:T(8,128)(4,1)S(1)} %get-tuple-element.107, pred[8,4]{1,0:T(8,128)(4,1)S(1)} %get-tuple-element.108, pred[8,4,128]{2,1,0:T(4,128)(4,1)S(1)} %broadcast_compare_fusion, ...), kind=kLoop, calls=%fused_computation.63 | loop fusion | flops 3145728 | bytes 4202560 | tf_op jit(solution)/shard_map/jit(_where)/select_n | solution.py:77
  108.2 1.5 collective-permute-start.1
  109.7 0.6 dynamic-slice_select_fusion
  110.4 0.6 select_bitcast_fusion
  111.0 47.2 %collective-permute-done.1 = bf16[8,4,2,128,128]{4,3,2,1,0:T(8,128)(2,1)S(1)} collective-permute-done((bf16[8,4,2,128,128]{4,3,2,1,0:T(8,128)(2,1)}, bf16[8,4,2,128,128]{4,3,2,1,0:T(8,128)(2,1)S(1)}, u32[]{:S(2)}, u32[]{:S(2)}) %collective-permute-start.1) | collective-permute-done | bytes 2097184 | tf_op jit(solution)/shard_map/ppermute | solution.py:18
  158.2 1.3 copy.70
  (42 shorter events, 2.2 us)
Async XLA Ops:
  0.6 32.3 %copy-start.6 = (s32[8]{0:T(128)S(1)}, s32[8]{0:T(128)}, u32[]{:S(2)}) copy-start(s32[8]{0:T(128)} %param.22) | copy-start | bytes 100
  2.1 74.2 %copy-start.5 = (f32[4096]{0:T(1024)S(1)}, f32[4096]{0:T(1024)}, u32[]{:S(2)}) copy-start(f32[4096]{0:T(1024)} %param.25) | copy-start | bytes 49156
  2.1 74.3 %copy-start = (s32[32]{0:T(128)S(1)}, s32[32]{0:T(128)}, u32[]{:S(2)}) copy-start(s32[32]{0:T(128)} %param.21) | copy-start | bytes 388
  2.1 74.3 %copy-start.4 = (s32[32,4]{0,1:T(4,128)S(1)}, s32[32,4]{0,1:T(4,128)}, u32[]{:S(2)}) copy-start(s32[32,4]{0,1:T(4,128)} %param.20) | copy-start | bytes 1540
  30.9 45.2 %collective-permute-start = (bf16[32,4096]{1,0:T(8,128)(2,1)S(1)}, bf16[32,4096]{1,0:T(8,128)(2,1)S(1)}, u32[]{:S(2)}, u32[]{:S(2)}) collective-permute-start(bf16[32,4096]{1,0:T(8,128)(2,1)S(1)} %all-reduce.1), channel_id=1, source_target_pairs={{0,8},{1,9},{2,10},{3,11},{4,12},{5,13},{6,14},{7,15},{16,24},{17,... | collective-permute-start | bytes 786440 | tf_op jit(solution)/shard_map/ppermute | solution.py:12
  76.5 29.3 %copy-start.2 = (bf16[32,2,128]{2,1,0:T(2,128)(2,1)S(1)}, bf16[32,2,128]{2,1,0:T(2,128)(2,1)}, u32[]{:S(2)}) copy-start(bf16[32,2,128]{2,1,0:T(2,128)(2,1)} %param.17) | copy-start | bytes 49156
  108.2 50.0 %collective-permute-start.1 = (bf16[8,4,2,128,128]{4,3,2,1,0:T(8,128)(2,1)}, bf16[8,4,2,128,128]{4,3,2,1,0:T(8,128)(2,1)S(1)}, u32[]{:S(2)}, u32[]{:S(2)}) collective-permute-start(bf16[8,4,2,128,128]{4,3,2,1,0:T(8,128)(2,1)} %select_select_fusion), channel_id=1, source_target_pairs={{240,0},{0,16},{16,32},{32,48},{48,64},{64,80},{80,96},{96,112},{1... | collective-permute-start | bytes 6291464 | tf_op jit(solution)/shard_map/ppermute | solution.py:18
where the time goes:
time: 160 us
  waiting for transfers between devices  83.7 us (52%)
  blocking collectives  28.8 us (18%)
  local copies, waits for them, and re-layouts  24.8 us (16%)
  other arithmetic  11.5 us (7%)
  matrix products  7.22 us (5%)
  starting transfers between devices  2.78 us (2%)
    ppermute x1, waiting for transfers between devices, from_behind_2(): return lax.ppermute(block, axis, route)  47.2 us
    ppermute x1, waiting for transfers between devices, from_behind(): return lax.ppermute(array, axis, pairs)  36.4 us
    psum x1, blocking collectives, local(): summed_rows = lax.psum(partial_value, 'tensor').astype(jnp.bfloat16)  28.8 us
    gather x1, local copies, waits for them, and re-layouts, attend(): page_data = jnp.take(page_pool, table_rows, axis=0)  9.98 us
    select_n x2, other arithmetic, attend(): page_data = jnp.take(page_pool, table_rows, axis=0)  7.42 us
    gather x1, local copies, waits for them, and re-layouts, gather_moved(): page_data = jnp.take(page_pool, moved_table, axis=0)  4.33 us
    slice x1, local copies, waits for them, and re-layouts, attend(): key_rows = page_data[:, :, 0].reshape(count_rows, span_len, kv_heads, HDIM)  3.99 us
  transfers between devices with their start and end apart: 2, of which 2 were waited for; matrix products, arithmetic and copies ran while one was open for 5% of the time, Pallas kernels for 0%

commit v1 on v0

v1 whole, which is shorter than its diff:
```python
import functools

import jax
import jax.numpy as jnp
from jax import lax
from jax.experimental import pallas as pl
from jax.experimental.pallas import tpu as pltpu
from jax.sharding import PartitionSpec as P

HDIM = 128
PAGE = 128
PAGES = 4
REQ = 32
MIG = 8
HEADS = 4
SPAN = PAGES * PAGE
WIDTH = HEADS * HDIM
D = 4096
ROWS = REQ + MIG
GROUP = 8
PAD = 8
SCALE = HDIM ** (-0.5)
F32 = jnp.float32
BF16 = jnp.bfloat16
ANY = pl.BlockSpec(memory_space=pl.ANY)
SMEM = pl.BlockSpec(memory_space=pltpu.SMEM)
VMEM = pl.BlockSpec(memory_space=pltpu.VMEM)


def leading():
    return lax.axis_index("section") == 0


def place():
    index = lax.axis_index("tensor")
    return index // 2, index % 2


def page_starts(table, pool, pages, sem):
    def start(r, _):
        for p in range(PAGES):
            pltpu.make_async_copy(
                pool.at[table[r, p]], pages.at[r, :, p], sem.at[r // GROUP]
            ).start()
        return 0

    lax.fori_loop(0, REQ, start, 0)


def attend(lengths, qs, ks, vs, os, pages, sem):
    lane = lax.broadcasted_iota(jnp.int32, (PAD, SPAN), 1)
    for g in range(REQ // GROUP):
        block = pages.at[pl.ds(g * GROUP, GROUP)]
        pltpu.make_async_copy(block, block, sem.at[g]).wait()
        rows = slice(g * GROUP * PAD, (g + 1) * GROUP * PAD)
        q = qs[rows, :]
        fresh = jnp.sum(q * ks[rows, :], axis=-1, keepdims=True) * SCALE
        scores = []
        for i in range(GROUP):
            r = g * GROUP + i
            keys = pages[r, 0].reshape(SPAN, HDIM)
            s = lax.dot_general(
                q[i * PAD : (i + 1) * PAD].astype(BF16),
                keys,
                (((1,), (1,)), ((), ())),
                preferred_element_type=F32,
            )
            scores.append(jnp.where(lane < lengths[r] - 1, s * SCALE, F32(-1e30)))
        s = jnp.concatenate(scores, axis=0)
        top = jnp.maximum(jnp.max(s, axis=-1, keepdims=True), fresh)
        w = jnp.exp(s - top)
        fw = jnp.exp(fresh - top)
        total = jnp.sum(w, axis=-1, keepdims=True) + fw
        outs = []
        for i in range(GROUP):
            r = g * GROUP + i
            values = pages[r, 1].reshape(SPAN, HDIM)
            outs.append(
                jnp.dot(
                    w[i * PAD : (i + 1) * PAD].astype(BF16),
                    values,
                    preferred_element_type=F32,
                )
            )
        o = jnp.concatenate(outs, axis=0) + fw.astype(BF16).astype(F32) * vs[rows, :]
        os[rows, :] = o / total


def spread(dst, h, value):
    dst[pl.ds(h, REQ, stride=PAD), :] = value.astype(F32)


def collect(os, out):
    for h in range(HEADS):
        out[:, h * HDIM : (h + 1) * HDIM] = os[pl.ds(h, REQ, stride=PAD), :].astype(BF16)


def gather_kernel(table, lengths, ids, pool, out, zero, sem):
    zero[...] = jnp.zeros_like(zero)

    def each(j, _):
        r = ids[j]
        for p in range(PAGES):
            used = p * PAGE < lengths[r]

            @pl.when(used)
            def _():
                pltpu.make_async_copy(pool.at[table[r, p]], out.at[j, p], sem).start()

            @pl.when(jnp.logical_not(used))
            def _():
                pltpu.make_async_copy(zero, out.at[j, p], sem).start()

        return 0

    lax.fori_loop(0, MIG, each, 0)
    pltpu.make_async_copy(out, out, sem).wait()


def gather_pages(table, lengths, ids, pool):
    return pl.pallas_call(
        gather_kernel,
        out_shape=jax.ShapeDtypeStruct((MIG, PAGES) + pool.shape[1:], BF16),
        in_specs=[SMEM, SMEM, SMEM, ANY],
        out_specs=ANY,
        scratch_shapes=[
            pltpu.VMEM(pool.shape[1:], BF16),
            pltpu.SemaphoreType.DMA,
        ],
        compiler_params=pltpu.CompilerParams(vmem_limit_bytes=4 << 20),
        name="gather_pages",
    )(table, lengths, ids, pool)


ATTEND_SCRATCH = [
    pltpu.VMEM((REQ, 2, PAGES, PAGE, HDIM), BF16),
    pltpu.VMEM((REQ * PAD, HDIM), F32),
    pltpu.VMEM((REQ * PAD, HDIM), F32),
    pltpu.VMEM((REQ * PAD, HDIM), F32),
    pltpu.VMEM((REQ * PAD, HDIM), F32),
    pltpu.SemaphoreType.DMA((REQ // GROUP,)),
]


def first_kernel(
    table, lengths, query, fresh_key, fresh_value, pool, weight, attn, keep, give,
    pages, qs, ks, vs, os, sem, held, wsem,
):
    y, core = place()

    @pl.when(leading())
    def _():
        page_starts(table, pool, pages, sem)
        copy = pltpu.make_async_copy(weight, held, wsem)
        copy.start()
        qs[...] = jnp.zeros_like(qs)
        ks[...] = jnp.zeros_like(ks)
        vs[...] = jnp.zeros_like(vs)
        for h in range(HEADS):
            spread(qs, h, query[:, h * HDIM : (h + 1) * HDIM])
            spread(ks, h, fresh_key[...])
            spread(vs, h, fresh_value[...])
        attend(lengths, qs, ks, vs, os, pages, sem)
        collect(os, attn)
        a = attn[...]
        copy.wait()
        for k in range(4):
            for out, c in ((give, 1 - core), (keep, core)):
                block = lax.rem(y + k, 4) * 2 + c
                w = held[pl.ds(pl.multiple_of(block * WIDTH, WIDTH), WIDTH), :]
                out[k] = lax.dot_general(
                    a, w, (((1,), (1,)), ((), ())), preferred_element_type=F32
                ).astype(out.dtype)

    @pl.when(jnp.logical_not(leading()))
    def _():
        attn[...] = jnp.zeros_like(attn)
        keep[...] = jnp.zeros_like(keep)
        give[...] = jnp.zeros_like(give)


def first_layer(table, lengths, query, fresh_key, fresh_value, pool, weight):
    part = (4, REQ, WIDTH)
    return pl.pallas_call(
        first_kernel,
        out_shape=(
            jax.ShapeDtypeStruct((REQ, WIDTH), BF16),
            jax.ShapeDtypeStruct(part, F32),
            jax.ShapeDtypeStruct(part, F32),
        ),
        in_specs=[SMEM, SMEM, VMEM, VMEM, VMEM, ANY, ANY],
        out_specs=(VMEM, VMEM, VMEM),
        scratch_shapes=ATTEND_SCRATCH
        + [pltpu.VMEM((D, WIDTH), BF16), pltpu.SemaphoreType.DMA],
        compiler_params=pltpu.CompilerParams(vmem_limit_bytes=24 << 20),
        name="first_layer",
    )(table, lengths, query, fresh_key, fresh_value, pool, weight)


def pair_kernel(keep, got, residual, own, a, b, c):
    own[...] = keep[0] + got[0] + residual[...].astype(F32)
    for k, out in ((1, a), (2, b), (3, c)):
        out[...] = (keep[k] + got[k]).astype(BF16)


def pair_sum(keep, got, residual):
    share = (REQ, WIDTH)
    return pl.pallas_call(
        pair_kernel,
        out_shape=(jax.ShapeDtypeStruct(share, F32),)
        + (jax.ShapeDtypeStruct(share, BF16),) * 3,
        in_specs=[VMEM] * 3,
        out_specs=(VMEM,) * 4,
        compiler_params=pltpu.CompilerParams(vmem_limit_bytes=4 << 20),
        name="pair_sum",
    )(keep, got, residual)


def share_kernel(ids, own, a, b, c, share, moved, wide):
    total = own[...] + a[...].astype(F32) + b[...].astype(F32) + c[...].astype(F32)
    rounded = total.astype(BF16)
    share[...] = rounded
    wide[...] = rounded.astype(F32)
    for j in range(MIG):
        moved[pl.ds(j, 1), :] = wide[pl.ds(ids[j], 1), :]


def share_sum(ids, own, a, b, c):
    return pl.pallas_call(
        share_kernel,
        out_shape=(
            jax.ShapeDtypeStruct((REQ, WIDTH), BF16),
            jax.ShapeDtypeStruct((MIG, WIDTH), F32),
        ),
        in_specs=[SMEM] + [VMEM] * 4,
        out_specs=(VMEM, VMEM),
        scratch_shapes=[pltpu.VMEM((REQ, WIDTH), F32)],
        compiler_params=pltpu.CompilerParams(vmem_limit_bytes=4 << 20),
        name="share_sum",
    )(ids, own, a, b, c)


def second_kernel(
    table, lengths, m0, m1, m2, m3, n0, n1, n2, n3, gain, pool, weight, kv_weight,
    attn, moved_kv,
    pages, qs, ks, vs, os, sem, held, wsem, held_kv, kvsem,
):
    y, core = place()

    @pl.when(jnp.logical_not(leading()))
    def _():
        wcopy = pltpu.make_async_copy(weight, held, wsem)
        wcopy.start()
        kvcopy = pltpu.make_async_copy(kv_weight, held_kv, kvsem)
        kvcopy.start()
        page_starts(table, pool, pages, sem)
        blocks = []
        square = jnp.zeros((ROWS, 1), F32)
        for refs, c in (((m0, m1, m2, m3), core), ((n0, n1, n2, n3), 1 - core)):
            for k, ref in enumerate(refs):
                x = ref[...].astype(F32)
                square += jnp.sum(x * x, axis=-1, keepdims=True)
                blocks.append((x, lax.rem(y + 4 - k, 4) * 2 + c))
        factor = lax.rsqrt(square * (1.0 / D) + 1e-05)
        wcopy.wait()
        kvcopy.wait()
        q = jnp.zeros((ROWS, WIDTH), F32)
        kv = jnp.zeros((ROWS, 2 * HDIM), F32)
        for x, block in blocks:
            x = (x * factor * gain[pl.ds(block, 1), :]).astype(BF16)
            at = pl.ds(pl.multiple_of(block * WIDTH, WIDTH), WIDTH)
            q += jnp.dot(x, held[at, :], preferred_element_type=F32)
            kv += jnp.dot(x, held_kv[at, :], preferred_element_type=F32)
        q = q.astype(BF16)
        kv = kv.astype(BF16).astype(F32)
        moved_kv[...] = kv[REQ:]
        qs[...] = jnp.zeros_like(qs)
        ks[...] = jnp.zeros_like(ks)
        vs[...] = jnp.zeros_like(vs)
        for h in range(HEADS):
            spread(qs, h, q[:REQ, h * HDIM : (h + 1) * HDIM])
            spread(ks, h, kv[:REQ, :HDIM])
            spread(vs, h, kv[:REQ, HDIM:])
        attend(lengths, qs, ks, vs, os, pages, sem)
        collect(os, attn)

    @pl.when(leading())
    def _():
        attn[...] = jnp.zeros_like(attn)
        moved_kv[...] = jnp.zeros_like(moved_kv)


def second_layer(table, lengths, mine, other, gain, pool, weight, kv_weight):
    return pl.pallas_call(
        second_kernel,
        out_shape=(
            jax.ShapeDtypeStruct((REQ, WIDTH), BF16),
            jax.ShapeDtypeStruct((MIG, 2 * HDIM), F32),
        ),
        in_specs=[SMEM, SMEM] + [VMEM] * 9 + [ANY] * 3,
        out_specs=(VMEM, VMEM),
        scratch_shapes=ATTEND_SCRATCH
        + [
            pltpu.VMEM((D, WIDTH), BF16),
            pltpu.SemaphoreType.DMA,
            pltpu.VMEM((D, 2 * HDIM), BF16),
            pltpu.SemaphoreType.DMA,
        ],
        compiler_params=pltpu.CompilerParams(vmem_limit_bytes=28 << 20),
        name="second_layer",
    )(table, lengths, *mine, *other, gain, pool, weight, kv_weight)


def patch_kernel(length, first_rows, second_rows, bulk, out, held, insem, outsem):
    for j in range(MIG):
        pltpu.make_async_copy(bulk.at[j], held.at[j], insem.at[j]).start()
    lead = leading()
    row = lax.broadcasted_iota(jnp.int32, (16, HDIM), 0)
    for j in range(MIG):
        pltpu.make_async_copy(bulk.at[j], held.at[j], insem.at[j]).wait()
        last = length[j] - 1
        page = last // PAGE
        base = pl.multiple_of((last % PAGE) // 16 * 16, 16)
        hit = row == last % 16
        for c in range(2):
            cols = slice(c * HDIM, (c + 1) * HDIM)
            new = jnp.where(lead, first_rows[pl.ds(j, 1), cols], second_rows[pl.ds(j, 1), cols])
            old = held[j, page, c, pl.ds(base, 16), :].astype(F32)
            held[j, page, c, pl.ds(base, 16), :] = jnp.where(hit, new, old).astype(BF16)
        pltpu.make_async_copy(held.at[j], out.at[j], outsem.at[j]).start()
    for j in range(MIG):
        pltpu.make_async_copy(held.at[j], out.at[j], outsem.at[j]).wait()


def patch(length, first_rows, second_rows, bulk):
    return pl.pallas_call(
        patch_kernel,
        out_shape=jax.ShapeDtypeStruct(bulk.shape, BF16),
        in_specs=[SMEM, VMEM, VMEM, ANY],
        out_specs=ANY,
        scratch_shapes=[
            pltpu.VMEM(bulk.shape, BF16),
            pltpu.SemaphoreType.DMA((MIG,)),
            pltpu.SemaphoreType.DMA((MIG,)),
        ],
        compiler_params=pltpu.CompilerParams(vmem_limit_bytes=8 << 20),
        name="patch",
    )(length, first_rows, second_rows, bulk)


def after(value, *others):
    return lax.optimization_barrier((value,) + others)[0]


def local(
    query_rows, new_kv, residual, kv_cache, page_table, lengths, migrate_ids,
    projection, kv_weight, norm_gain,
):
    replicas = lax.axis_size("inst")
    lead = leading()
    pool = kv_cache[0]
    weight = projection[0]

    def across(value, by):
        return lax.ppermute(value, "tensor", [(i, (i + 2 * by) % 8) for i in range(8)])

    def to_twin(value):
        return lax.ppermute(value, "tensor", [(i, i ^ 1) for i in range(8)])

    def to_next(value):
        return lax.ppermute(
            value, "inst", [(i, (i + 1) % replicas) for i in range(replicas)]
        )

    bulk = to_next(gather_pages(page_table, lengths, migrate_ids, pool))

    attn, keep, give = first_layer(
        page_table, lengths, query_rows, new_kv[:, 0], new_kv[:, 1], pool, weight
    )
    got = to_twin(give)
    own, a, b, c = pair_sum(keep, got, residual)
    share, moved = share_sum(migrate_ids, own, across(a, 1), across(b, 2), across(c, 3))
    moved = moved.astype(BF16)
    arrived = lax.ppermute(share, "section", [(0, 1)])
    moved_in = lax.ppermute(
        moved,
        ("inst", "section"),
        [(2 * i, 2 * ((i + 1) % replicas) + 1) for i in range(replicas)],
    )
    hidden = jnp.where(lead, share, arrived)

    ids = after(migrate_ids, moved)
    pick = (ids[:, None] == jnp.arange(REQ)[None, :]).astype(F32)
    side = jnp.concatenate(
        [new_kv.reshape(REQ, 2 * HDIM).astype(F32), jnp.broadcast_to(lengths.astype(F32)[:, None], (REQ, HDIM))],
        axis=1,
    )
    side = to_next(jnp.dot(pick, side, precision=lax.Precision.HIGHEST))
    first_rows = side[:, : 2 * HDIM]
    moved_len = side[:, 2 * HDIM].astype(jnp.int32)
    flat_kv = after(kv_weight, moved).reshape(D, 2 * HDIM)

    rows = jnp.concatenate([arrived, moved_in], axis=0)
    mine = [rows] + [across(rows, k) for k in (1, 2, 3)]
    other = [to_twin(m) for m in mine]
    second_attn, second_rows = second_layer(
        page_table, lengths, mine, other, norm_gain.reshape(8, WIDTH), pool, weight, flat_kv
    )
    migrated = patch(moved_len, first_rows, second_rows, bulk)
    attn = jnp.where(lead, attn, second_attn)
    return attn[None], hidden, migrated[None]


def solution(mesh):
    return jax.shard_map(
        local,
        mesh=mesh,
        in_specs=(
            P("inst", "tensor"),
            P("inst", None, "tensor"),
            P("inst", "tensor"),
            P("section", "inst", None, None, "tensor"),
            P("inst", None),
            P("inst"),
            P("inst"),
            P("section", None, "tensor"),
            P(None, None, "tensor"),
            P(),
        ),
        out_specs=(
            P("section", "inst", "tensor"),
            P("inst", "tensor"),
            P("section", "inst", None, None, None, "tensor"),
        ),
        check_vma=False,
    )
```

time: 160 us -> 91.8 us (0.57)
  the two profiles are of different devices: /device:TPU:216 before, /device:TPU:201 now
where the time goes in v1:
time: 91.8 us; the launch traced here: 91.6 us
  waiting for transfers between devices  41.3 us (45%)
  Pallas kernels  17.6 us (19%)
  starting transfers between devices  16.3 us (18%)
  local copies, waits for them, and re-layouts  13.8 us (15%)
  other arithmetic  1.37 us (1%)
  between operations  0.95 us (1%)
    ppermute x1, waiting for transfers between devices, local(): lax.ppermute(moved, ('inst', 'section'), [(2 * i, 2 * ((i + 1) % replicas...  24.4 us
    unnamed x29, local copies, waits for them, and re-layouts  13.7 us
    pallas_call x1, Pallas kernels, second_layer(): pl.pallas_call(second_kernel, out_shape=(jax.ShapeDtypeStruct((REQ, WIDTH...  11.8 us
    ppermute x1, waiting for transfers between devices, local(): arrived = lax.ppermute(share, 'section', [(0, 1)])  10.4 us
    ppermute x6, starting transfers between devices, across(): lax.ppermute(value, 'tensor', [(i, (i + 2 * by) % 8) for i in range(8)])  8.25 us
    ppermute x5, starting transfers between devices, to_twin(): return lax.ppermute(value, 'tensor', [(i, i ^ 1) for i in range(8)])  4.14 us
    ppermute x2, waiting for transfers between devices, to_next(): lax.ppermute(value, 'inst', [(i, (i + 1) % replicas) for i in range(repli...  2.61 us
    ppermute x5, waiting for transfers between devices, to_twin(): return lax.ppermute(value, 'tensor', [(i, i ^ 1) for i in range(8)])  2.17 us
  transfers between devices with their start and end apart: 15, of which 9 were waited for; matrix products, arithmetic and copies ran while one was open for 4% of the time, Pallas kernels for 15%

profile of v1, /device:TPU:201, one launch (start us, length us, event | category | flops | bytes accessed | tf_op | source)
XLA Modules:
  0.0 91.6 jit_solution(5200414698279167388)
XLA Ops:
  0.6 0.8 copy.20.table
  1.4 3.4 %copy-done = bf16[1,128,2,128,128]{4,3,2,1,0:T(8,128)(2,1)S(1)} copy-done((bf16[1,128,2,128,128]{4,3,2,1,0:T(8,128)(2,1)S(1)}, bf16[1,128,2,128,128]{4,3,2,1,0:T(8,128)(2,1)}, u32[]{:S(2)}) %copy-start) | copy-done | bytes 8388632
  6.1 2.1 %gather_pages.1 = bf16[8,4,2,128,128]{4,3,2,1,0:T(8,128)(2,1)} custom-call(s32[32,4]{1,0:T(8,128)S(1)} %copy.20.table, s32[32]{0:T(128)S(1)} %copy-done.7, s32[8]{0:T(128)S(1)} %copy-done.9, bf16[128,2,128,128]{3,2,1,0:T(8,128)(2,1)S(1)} %bitcast.18), custom_call_target="tpu_custom_call" | custom-call | tf_op jit(solution)/shard_map/gather_pages/pallas_call | solution.py:121
  8.2 1.3 %collective-permute-start.14 = (bf16[8,4,2,128,128]{4,3,2,1,0:T(8,128)(2,1)}, bf16[8,4,2,128,128]{4,3,2,1,0:T(8,128)(2,1)S(1)}, u32[]{:S(2)}, u32[]{:S(2)}) collective-permute-start(bf16[8,4,2,128,128]{4,3,2,1,0:T(8,128)(2,1)} %gather_pages.1), channel_id=1, source_target_pairs={{0,16},{16,32},{32,48},{48,64},{64,80},{80,96},{96,112},{112,128},... | collective-permute-start | bytes 6291464 | tf_op jit(solution)/shard_map/ppermute | solution.py:371
  10.2 2.2 %copy-done.3 = bf16[1,4096,512]{2,1,0:T(8,128)(2,1)S(1)} copy-done((bf16[1,4096,512]{2,1,0:T(8,128)(2,1)S(1)}, bf16[1,4096,512]{2,1,0:T(8,128)(2,1)}, u32[]{:S(2)}) %copy-start.3) | copy-done | bytes 4194328
  12.4 0.9 first_layer.1
  13.3 0.8 collective-permute-start
  14.1 1.2 %collective-permute-done.got = f32[4,32,512]{2,1,0:T(8,128)S(1)} collective-permute-done((f32[4,32,512]{2,1,0:T(8,128)S(1)}, f32[4,32,512]{2,1,0:T(8,128)S(1)}, u32[]{:S(2)}, u32[]{:S(2)}) %collective-permute-start) | collective-permute-done | bytes 262176 | tf_op jit(solution)/shard_map/ppermute | solution.py:368
  15.3 1.4 %collective-permute-start.1 = (bf16[32,512]{1,0:T(8,128)(2,1)S(1)}, bf16[32,512]{1,0:T(8,128)(2,1)S(1)}, u32[]{:S(2)}, u32[]{:S(2)}) collective-permute-start(bf16[32,512]{1,0:T(8,128)(2,1)S(1)} %get-tuple-element.20), channel_id=1, source_target_pairs={{0,2},{1,3},{2,4},{3,5},{4,6},{5,7},{6,0},{7,1},{8,10},{9,11},{10,... | collective-permute-start | bytes 98312 | tf_op jit(solution)/shard_map/ppermute | solution.py:365
  16.7 0.8 collective-permute-start.2
  17.5 2.0 %collective-permute-start.3 = (bf16[32,512]{1,0:T(8,128)(2,1)S(1)}, bf16[32,512]{1,0:T(8,128)(2,1)S(1)}, u32[]{:S(2)}, u32[]{:S(2)}) collective-permute-start(bf16[32,512]{1,0:T(8,128)(2,1)S(1)} %get-tuple-element.22), channel_id=1, source_target_pairs={{0,6},{1,7},{2,0},{3,1},{4,2},{5,3},{6,4},{7,5},{8,14},{9,15},{10,... | collective-permute-start | bytes 98312 | tf_op jit(solution)/shard_map/ppermute | solution.py:365
  19.5 1.8 %collective-permute-done.2.b = bf16[32,512]{1,0:T(8,128)(2,1)S(1)} collective-permute-done((bf16[32,512]{1,0:T(8,128)(2,1)S(1)}, bf16[32,512]{1,0:T(8,128)(2,1)S(1)}, u32[]{:S(2)}, u32[]{:S(2)}) %collective-permute-start.2) | collective-permute-done | bytes 32800 | tf_op jit(solution)/shard_map/ppermute | solution.py:365
  21.8 1.3 %collective-permute-start.4 = (bf16[32,512]{1,0:T(8,128)(2,1)S(1)}, bf16[32,512]{1,0:T(8,128)(2,1)S(1)}, u32[]{:S(2)}, u32[]{:S(2)}) collective-permute-start(bf16[32,512]{1,0:T(8,128)(2,1)S(1)} %get-tuple-element.23), channel_id=1, source_target_pairs={{0,8},{1,9},{2,10},{3,11},{4,12},{5,13},{6,14},{7,15},{16,24},{17,... | collective-permute-start | bytes 98312 | tf_op jit(solution)/shard_map/ppermute | solution.py:384
  23.2 1.3 %collective-permute-start.5 = (bf16[8,512]{1,0:T(8,128)(2,1)S(1)}, bf16[8,512]{1,0:T(8,128)(2,1)S(1)}, u32[]{:S(2)}, u32[]{:S(2)}) collective-permute-start(bf16[8,512]{1,0:T(8,128)(2,1)S(1)} %convert_element_type.18), channel_id=1, source_target_pairs={{0,24},{16,40},{32,56},{48,72},{64,88},{80,104},{96,120},{112,136}... | collective-permute-start | bytes 24584 | tf_op jit(solution)/shard_map/ppermute | solution.py:385
  24.5 10.4 %collective-permute-done.4 = bf16[32,512]{1,0:T(8,128)(2,1)S(1)} collective-permute-done((bf16[32,512]{1,0:T(8,128)(2,1)S(1)}, bf16[32,512]{1,0:T(8,128)(2,1)S(1)}, u32[]{:S(2)}, u32[]{:S(2)}) %collective-permute-start.4) | collective-permute-done | bytes 32800 | tf_op jit(solution)/shard_map/ppermute | solution.py:384
  35.5 24.4 %collective-permute-done.5 = bf16[8,512]{1,0:T(8,128)(2,1)S(1)} collective-permute-done((bf16[8,512]{1,0:T(8,128)(2,1)S(1)}, bf16[8,512]{1,0:T(8,128)(2,1)S(1)}, u32[]{:S(2)}, u32[]{:S(2)}) %collective-permute-start.5) | collective-permute-done | bytes 8224 | tf_op jit(solution)/shard_map/ppermute | solution.py:385
  60.1 2.3 %collective-permute-start.7 = (bf16[40,512]{1,0:T(8,128)(2,1)S(1)}, bf16[40,512]{1,0:T(8,128)(2,1)S(1)}, u32[]{:S(2)}, u32[]{:S(2)}) collective-permute-start(bf16[40,512]{1,0:T(8,128)(2,1)S(1)} %constant_dynamic-update-slice_fusion.m0), channel_id=1, source_target_pairs={{0,4},{1,5},{2,6},{3,7},{4,0},{5,1},{6,2},{7,3},{8,12},{9,13},{10,... | collective-permute-start | bytes 122888 | tf_op jit(solution)/shard_map/ppermute | solution.py:365
  62.4 1.6 %collective-permute-start.6 = (bf16[40,512]{1,0:T(8,128)(2,1)S(1)}, bf16[40,512]{1,0:T(8,128)(2,1)S(1)}, u32[]{:S(2)}, u32[]{:S(2)}) collective-permute-start(bf16[40,512]{1,0:T(8,128)(2,1)S(1)} %constant_dynamic-update-slice_fusion.m0), channel_id=1, source_target_pairs={{0,2},{1,3},{2,4},{3,5},{4,6},{5,7},{6,0},{7,1},{8,10},{9,11},{10,... | collective-permute-start | bytes 122888 | tf_op jit(solution)/shard_map/ppermute | solution.py:365
  64.3 2.0 %copy.31 = bf16[512,8,2,128]{3,1,2,0:T(8,128)(2,1)S(1)} copy(bf16[512,8,2,128]{3,2,1,0:T(2,128)(2,1)} %bitcast.24) | data formatting | bytes 4194304
  66.3 2.6 %collective-permute-done.13 = f32[8,384]{1,0:T(8,128)S(1)} collective-permute-done((f32[8,384]{1,0:T(8,128)S(1)}, f32[8,384]{1,0:T(8,128)S(1)}, u32[]{:S(2)}, u32[]{:S(2)}) %collective-permute-start.13) | collective-permute-done | bytes 12320 | tf_op jit(solution)/shard_map/ppermute | solution.py:371
  68.9 2.8 %collective-permute-start.9 = (bf16[40,512]{1,0:T(8,128)(2,1)S(1)}, bf16[40,512]{1,0:T(8,128)(2,1)S(1)}, u32[]{:S(2)}, u32[]{:S(2)}) collective-permute-start(bf16[40,512]{1,0:T(8,128)(2,1)S(1)} %constant_dynamic-update-slice_fusion.m0), channel_id=1, source_target_pairs={{0,1},{1,0},{2,3},{3,2},{4,5},{5,4},{6,7},{7,6},{8,9},{9,8},{10,11... | collective-permute-start | bytes 122888 | tf_op jit(solution)/shard_map/ppermute | solution.py:368
  73.4 3.4 %copy-done.2 = bf16[1,128,2,128,128]{4,3,2,1,0:T(8,128)(2,1)S(1)} copy-done((bf16[1,128,2,128,128]{4,3,2,1,0:T(8,128)(2,1)S(1)}, bf16[1,128,2,128,128]{4,3,2,1,0:T(8,128)(2,1)}, u32[]{:S(2)}) %copy-start.2) | copy-done | bytes 8388632
  76.8 11.8 %second_layer.1 = (bf16[32,512]{1,0:T(8,128)(2,1)S(1)}, f32[8,256]{1,0:T(8,128)S(1)}) custom-call(s32[32,4]{1,0:T(8,128)S(1)} %copy.20.table, s32[32]{0:T(128)S(1)} %copy-done.8, bf16[40,512]{1,0:T(8,128)(2,1)S(1)} %constant_dynamic-update-slice_fusion.m0, bf16[40,512]{1,0:T(8,128)(2,1)S(1)} %collective-permute-done.6.m1, ...), custom_call_target="tpu_custom_call" | custom-call | tf_op jit(solution)/shard_map/second_layer/pallas_call | solution.py:294
  89.2 2.2 %patch.1 = bf16[8,4,2,128,128]{4,3,2,1,0:T(8,128)(2,1)} custom-call(s32[8]{0:T(128)S(1)} %fusion.4.length, f32[8,256]{1,0:T(8,128)S(1)} %slice.17.first_rows, f32[8,256]{1,0:T(8,128)S(1)} %get-tuple-element.28.second_rows, bf16[8,4,2,128,128]{4,3,2,1,0:T(8,128)(2,1)S(1)} %collective-permute-done.14.bulk), custom_call_target="tpu_custom_call" | custom-call | tf_op jit(solution)/shard_map/patch/pallas_call | solution.py:336
  (53 shorter events, 6.1 us)
Async XLA Ops:
  1.4 3.4 %copy-start = (bf16[1,128,2,128,128]{4,3,2,1,0:T(8,128)(2,1)S(1)}, bf16[1,128,2,128,128]{4,3,2,1,0:T(8,128)(2,1)}, u32[]{:S(2)}) copy-start(bf16[1,128,2,128,128]{4,3,2,1,0:T(8,128)(2,1)} %param.13) | copy-start | bytes 25165828
  6.1 3.4 %copy-start.11 = (bf16[32,2,128]{2,1,0:T(2,128)(2,1)S(1)}, bf16[32,2,128]{2,1,0:T(2,128)(2,1)}, u32[]{:S(2)}) copy-start(bf16[32,2,128]{2,1,0:T(2,128)(2,1)} %param.11) | copy-start | bytes 49156
  6.1 4.1 %copy-start.1 = (bf16[1,128,2,128,128]{4,3,2,1,0:T(8,128)(2,1)S(1)}, bf16[1,128,2,128,128]{4,3,2,1,0:T(8,128)(2,1)}, u32[]{:S(2)}) copy-start(bf16[1,128,2,128,128]{4,3,2,1,0:T(8,128)(2,1)} %param.13) | copy-start | bytes 25165828
  6.1 4.1 %copy-start.5 = (bf16[32,512]{1,0:T(8,128)(2,1)S(1)}, bf16[32,512]{1,0:T(8,128)(2,1)}, u32[]{:S(2)}) copy-start(bf16[32,512]{1,0:T(8,128)(2,1)} %query.1) | copy-start | bytes 98308
  6.1 4.1 %copy-start.8 = (s32[32]{0:T(128)S(1)}, s32[32]{0:T(128)}, u32[]{:S(2)}) copy-start(s32[32]{0:T(128)} %lengths.5) | copy-start | bytes 388
  8.2 81.0 %collective-permute-start.14 = (bf16[8,4,2,128,128]{4,3,2,1,0:T(8,128)(2,1)}, bf16[8,4,2,128,128]{4,3,2,1,0:T(8,128)(2,1)S(1)}, u32[]{:S(2)}, u32[]{:S(2)}) collective-permute-start(bf16[8,4,2,128,128]{4,3,2,1,0:T(8,128)(2,1)} %gather_pages.1), channel_id=1, source_target_pairs={{0,16},{16,32},{32,48},{48,64},{64,80},{80,96},{96,112},{112,128},... | collective-permute-start | bytes 6291464 | tf_op jit(solution)/shard_map/ppermute | solution.py:371
  12.4 8.8 %copy-start.10 = (s32[8]{0:T(128)S(1)}, s32[8]{0:T(128)}, u32[]{:S(2)}) copy-start(s32[8]{0:T(128)} %ids.3) | copy-start | bytes 100
  12.4 51.8 %copy-start.12 = (f32[4096]{0:T(1024)S(1)}, f32[4096]{0:T(1024)}, u32[]{:S(2)}) copy-start(f32[4096]{0:T(1024)} %param.19) | copy-start | bytes 49156
  13.3 1.9 %collective-permute-start = (f32[4,32,512]{2,1,0:T(8,128)S(1)}, f32[4,32,512]{2,1,0:T(8,128)S(1)}, u32[]{:S(2)}, u32[]{:S(2)}) collective-permute-start(f32[4,32,512]{2,1,0:T(8,128)S(1)} %get-tuple-element.18), channel_id=1, source_target_pairs={{0,1},{1,0},{2,3},{3,2},{4,5},{5,4},{6,7},{7,6},{8,9},{9,8},{10,11... | collective-permute-start | bytes 786440 | tf_op jit(solution)/shard_map/ppermute | solution.py:368
  15.3 4.2 %collective-permute-start.1 = (bf16[32,512]{1,0:T(8,128)(2,1)S(1)}, bf16[32,512]{1,0:T(8,128)(2,1)S(1)}, u32[]{:S(2)}, u32[]{:S(2)}) collective-permute-start(bf16[32,512]{1,0:T(8,128)(2,1)S(1)} %get-tuple-element.20), channel_id=1, source_target_pairs={{0,2},{1,3},{2,4},{3,5},{4,6},{5,7},{6,0},{7,1},{8,10},{9,11},{10,... | collective-permute-start | bytes 98312 | tf_op jit(solution)/shard_map/ppermute | solution.py:365
  16.7 4.6 %collective-permute-start.2 = (bf16[32,512]{1,0:T(8,128)(2,1)S(1)}, bf16[32,512]{1,0:T(8,128)(2,1)S(1)}, u32[]{:S(2)}, u32[]{:S(2)}) collective-permute-start(bf16[32,512]{1,0:T(8,128)(2,1)S(1)} %get-tuple-element.21), channel_id=1, source_target_pairs={{0,4},{1,5},{2,6},{3,7},{4,0},{5,1},{6,2},{7,3},{8,12},{9,13},{10,... | collective-permute-start | bytes 98312 | tf_op jit(solution)/shard_map/ppermute | solution.py:365
  17.5 3.7 %collective-permute-start.3 = (bf16[32,512]{1,0:T(8,128)(2,1)S(1)}, bf16[32,512]{1,0:T(8,128)(2,1)S(1)}, u32[]{:S(2)}, u32[]{:S(2)}) collective-permute-start(bf16[32,512]{1,0:T(8,128)(2,1)S(1)} %get-tuple-element.22), channel_id=1, source_target_pairs={{0,6},{1,7},{2,0},{3,1},{4,2},{5,3},{6,4},{7,5},{8,14},{9,15},{10,... | collective-permute-start | bytes 98312 | tf_op jit(solution)/shard_map/ppermute | solution.py:365
  21.8 13.1 %collective-permute-start.4 = (bf16[32,512]{1,0:T(8,128)(2,1)S(1)}, bf16[32,512]{1,0:T(8,128)(2,1)S(1)}, u32[]{:S(2)}, u32[]{:S(2)}) collective-permute-start(bf16[32,512]{1,0:T(8,128)(2,1)S(1)} %get-tuple-element.23), channel_id=1, source_target_pairs={{0,8},{1,9},{2,10},{3,11},{4,12},{5,13},{6,14},{7,15},{16,24},{17,... | collective-permute-start | bytes 98312 | tf_op jit(solution)/shard_map/ppermute | solution.py:384
  23.2 36.7 %collective-permute-start.5 = (bf16[8,512]{1,0:T(8,128)(2,1)S(1)}, bf16[8,512]{1,0:T(8,128)(2,1)S(1)}, u32[]{:S(2)}, u32[]{:S(2)}) collective-permute-start(bf16[8,512]{1,0:T(8,128)(2,1)S(1)} %convert_element_type.18), channel_id=1, source_target_pairs={{0,24},{16,40},{32,56},{48,72},{64,88},{80,104},{96,120},{112,136}... | collective-permute-start | bytes 24584 | tf_op jit(solution)/shard_map/ppermute | solution.py:385
  59.9 11.8 %collective-permute-start.8 = (bf16[40,512]{1,0:T(8,128)(2,1)S(1)}, bf16[40,512]{1,0:T(8,128)(2,1)S(1)}, u32[]{:S(2)}, u32[]{:S(2)}) collective-permute-start(bf16[40,512]{1,0:T(8,128)(2,1)S(1)} %constant_dynamic-update-slice_fusion.m0), channel_id=1, source_target_pairs={{0,6},{1,7},{2,0},{3,1},{4,2},{5,3},{6,4},{7,5},{8,14},{9,15},{10,... | collective-permute-start | bytes 122888 | tf_op jit(solution)/shard_map/ppermute | solution.py:365
  60.1 11.6 %collective-permute-start.7 = (bf16[40,512]{1,0:T(8,128)(2,1)S(1)}, bf16[40,512]{1,0:T(8,128)(2,1)S(1)}, u32[]{:S(2)}, u32[]{:S(2)}) collective-permute-start(bf16[40,512]{1,0:T(8,128)(2,1)S(1)} %constant_dynamic-update-slice_fusion.m0), channel_id=1, source_target_pairs={{0,4},{1,5},{2,6},{3,7},{4,0},{5,1},{6,2},{7,3},{8,12},{9,13},{10,... | collective-permute-start | bytes 122888 | tf_op jit(solution)/shard_map/ppermute | solution.py:365
  62.4 9.8 %collective-permute-start.6 = (bf16[40,512]{1,0:T(8,128)(2,1)S(1)}, bf16[40,512]{1,0:T(8,128)(2,1)S(1)}, u32[]{:S(2)}, u32[]{:S(2)}) collective-permute-start(bf16[40,512]{1,0:T(8,128)(2,1)S(1)} %constant_dynamic-update-slice_fusion.m0), channel_id=1, source_target_pairs={{0,2},{1,3},{2,4},{3,5},{4,6},{5,7},{6,0},{7,1},{8,10},{9,11},{10,... | collective-permute-start | bytes 122888 | tf_op jit(solution)/shard_map/ppermute | solution.py:365
  64.2 4.7 %collective-permute-start.13 = (f32[8,384]{1,0:T(8,128)S(1)}, f32[8,384]{1,0:T(8,128)S(1)}, u32[]{:S(2)}, u32[]{:S(2)}) collective-permute-start(f32[8,384]{1,0:T(8,128)S(1)} %fusion), channel_id=1, source_target_pairs={{0,16},{16,32},{32,48},{48,64},{64,80},{80,96},{96,112},{112,128},... | collective-permute-start | bytes 36872 | tf_op jit(solution)/shard_map/ppermute | solution.py:371
  64.3 9.2 %copy-start.4 = (bf16[1,4096,512]{2,1,0:T(8,128)(2,1)S(1)}, bf16[1,4096,512]{2,1,0:T(8,128)(2,1)}, u32[]{:S(2)}) copy-start(bf16[1,4096,512]{2,1,0:T(8,128)(2,1)} %param.17) | copy-start | bytes 12582916
  68.9 3.6 %collective-permute-start.9 = (bf16[40,512]{1,0:T(8,128)(2,1)S(1)}, bf16[40,512]{1,0:T(8,128)(2,1)S(1)}, u32[]{:S(2)}, u32[]{:S(2)}) collective-permute-start(bf16[40,512]{1,0:T(8,128)(2,1)S(1)} %constant_dynamic-update-slice_fusion.m0), channel_id=1, source_target_pairs={{0,1},{1,0},{2,3},{3,2},{4,5},{5,4},{6,7},{7,6},{8,9},{9,8},{10,11... | collective-permute-start | bytes 122888 | tf_op jit(solution)/shard_map/ppermute | solution.py:368
  71.7 1.2 %collective-permute-start.12 = (bf16[40,512]{1,0:T(8,128)(2,1)S(1)}, bf16[40,512]{1,0:T(8,128)(2,1)S(1)}, u32[]{:S(2)}, u32[]{:S(2)}) collective-permute-start(bf16[40,512]{1,0:T(8,128)(2,1)S(1)} %collective-permute-done.8.m3), channel_id=1, source_target_pairs={{0,1},{1,0},{2,3},{3,2},{4,5},{5,4},{6,7},{7,6},{8,9},{9,8},{10,11... | collective-permute-start | bytes 122888 | tf_op jit(solution)/shard_map/ppermute | solution.py:368
  71.7 1.4 %collective-permute-start.11 = (bf16[40,512]{1,0:T(8,128)(2,1)S(1)}, bf16[40,512]{1,0:T(8,128)(2,1)S(1)}, u32[]{:S(2)}, u32[]{:S(2)}) collective-permute-start(bf16[40,512]{1,0:T(8,128)(2,1)S(1)} %collective-permute-done.7.m2), channel_id=1, source_target_pairs={{0,1},{1,0},{2,3},{3,2},{4,5},{5,4},{6,7},{7,6},{8,9},{9,8},{10,11... | collective-permute-start | bytes 122888 | tf_op jit(solution)/shard_map/ppermute | solution.py:368
  72.2 1.2 %collective-permute-start.10 = (bf16[40,512]{1,0:T(8,128)(2,1)S(1)}, bf16[40,512]{1,0:T(8,128)(2,1)S(1)}, u32[]{:S(2)}, u32[]{:S(2)}) collective-permute-start(bf16[40,512]{1,0:T(8,128)(2,1)S(1)} %collective-permute-done.6.m1), channel_id=1, source_target_pairs={{0,1},{1,0},{2,3},{3,2},{4,5},{5,4},{6,7},{7,6},{8,9},{9,8},{10,11... | collective-permute-start | bytes 122888 | tf_op jit(solution)/shard_map/ppermute | solution.py:368
  73.4 3.4 %copy-start.2 = (bf16[1,128,2,128,128]{4,3,2,1,0:T(8,128)(2,1)S(1)}, bf16[1,128,2,128,128]{4,3,2,1,0:T(8,128)(2,1)}, u32[]{:S(2)}) copy-start(bf16[1,128,2,128,128]{4,3,2,1,0:T(8,128)(2,1)} %param.13) | copy-start | bytes 25165828
  (4 other events, 6.3 us)

commit v2 on v1

v2 whole, which is shorter than its diff:
```python
import functools

import jax
import jax.numpy as jnp
from jax import lax
from jax.experimental import pallas as pl
from jax.experimental.pallas import tpu as pltpu
from jax.sharding import PartitionSpec as P

HDIM = 128
PAGE = 128
PAGES = 4
REQ = 32
MIG = 8
HEADS = 4
SPAN = PAGES * PAGE
WIDTH = HEADS * HDIM
D = 4096
POOL = 128
ROWS = REQ + MIG
SENT = 16
GROUP = 16
PAD = 8
PARTS = (8, 15, 9)
SCALE = HDIM ** (-0.5)
F32 = jnp.float32
BF16 = jnp.bfloat16
HBM = pl.BlockSpec(memory_space=pltpu.HBM)
VMEM = pl.BlockSpec(memory_space=pltpu.VMEM)
DMA = pltpu.SemaphoreType.DMA
KV = (2, PAGE, HDIM)


def in_hbm(*values):
    return [pltpu.with_memory_space_constraint(v, pltpu.HBM) for v in values]


def in_vmem(*values):
    return [pltpu.with_memory_space_constraint(v, pltpu.VMEM) for v in values]


def leading():
    return lax.axis_index("section") == 0


def place():
    index = lax.axis_index("tensor")
    return index // 2, index % 2


def started(*copies):
    made = [pltpu.make_async_copy(*c) for c in copies]
    for c in made:
        c.start()
    return made


def scores(lengths, table, qs, ks, pages, ss, g):
    lane = lax.broadcasted_iota(jnp.int32, (PAD, SPAN), 1)
    rows = slice(g * GROUP * PAD, (g + 1) * GROUP * PAD)
    q = qs[rows, :]
    for i in range(GROUP):
        r = g * GROUP + i
        own = q[i * PAD : (i + 1) * PAD].astype(BF16)
        s = jnp.concatenate(
            [
                lax.dot_general(
                    own,
                    pages[table[p, r], 0],
                    (((1,), (1,)), ((), ())),
                    preferred_element_type=F32,
                )
                for p in range(PAGES)
            ],
            axis=1,
        )
        ss[r * PAD : (r + 1) * PAD, :] = jnp.where(
            lane < lengths[r] - 1, s * SCALE, F32(-1e30)
        )


def mix(table, qs, ks, vs, os, pages, ss, g):
    rows = slice(g * GROUP * PAD, (g + 1) * GROUP * PAD)
    fresh = jnp.sum(qs[rows, :] * ks[rows, :], axis=-1, keepdims=True) * SCALE
    s = ss[rows, :]
    top = jnp.maximum(jnp.max(s, axis=-1, keepdims=True), fresh)
    w = jnp.exp(s - top)
    fw = jnp.exp(fresh - top)
    total = jnp.sum(w, axis=-1, keepdims=True) + fw
    outs = []
    for i in range(GROUP):
        r = g * GROUP + i
        rounded = w[i * PAD : (i + 1) * PAD].astype(BF16)
        values = jnp.concatenate([pages[table[p, r], 1] for p in range(PAGES)], axis=0)
        outs.append(jnp.dot(rounded, values, preferred_element_type=F32))
    o = jnp.concatenate(outs, axis=0) + fw.astype(BF16).astype(F32) * vs[rows, :]
    os[rows, :] = o / total


def spread(qs, ks, vs, q, k, v):
    for dst in (qs, ks, vs):
        dst[...] = jnp.zeros_like(dst)
    for h in range(HEADS):
        at = pl.ds(h, REQ, stride=PAD)
        qs[at, :] = q[:, h * HDIM : (h + 1) * HDIM]
        ks[at, :] = k
        vs[at, :] = v


def collect(os, out):
    for h in range(HEADS):
        out[:, h * HDIM : (h + 1) * HDIM] = os[pl.ds(h, REQ, stride=PAD), :].astype(BF16)


ROW_SCRATCH = [pltpu.VMEM((REQ * PAD, HDIM), F32)] * 4 + [pltpu.VMEM((REQ * PAD, SPAN), F32)]
TABLE_SCRATCH = [pltpu.SMEM((PAGES, REQ), jnp.int32), pltpu.SMEM((REQ,), jnp.int32)]


def write_row(ref, index, row, key, value):
    base = pl.multiple_of(row // 16 * 16, 16)
    hit = lax.broadcasted_iota(jnp.int32, (16, HDIM), 0) == row - base
    for c, new in ((0, key), (1, value)):
        old = ref[index, c, pl.ds(base, 16), :].astype(F32)
        ref[index, c, pl.ds(base, 16), :] = jnp.where(hit, new, old).astype(BF16)


def page_slots(refs):
    return [(ref, i) for ref, count in zip(refs, PARTS) for i in range(count)]


def gather_kernel(
    table_in, lengths_in, ids_in, fresh_in, pool, back, ahead, later,
    table, lengths, ids, fresh, small, sems,
):
    small_copies = started(
        (table_in, table, small.at[0]),
        (lengths_in, lengths, small.at[1]),
        (ids_in, ids, small.at[2]),
        (fresh_in, fresh, small.at[3]),
    )
    for c in small_copies[:3]:
        c.wait()
    slots = page_slots((back, ahead, later))

    def each(act):
        for j in range(MIG):
            r = ids[j]
            for p in range(PAGES):
                ref, index = slots[j * PAGES + p]
                act(r, p, ref.at[index], sems.at[j * PAGES + p])

    def start(r, p, slot, sem):
        used = p * PAGE < lengths[r]

        @pl.when(used)
        def _():
            pltpu.make_async_copy(pool.at[table[p, r]], slot, sem).start()

        @pl.when(jnp.logical_not(used))
        def _():
            slot[...] = jnp.zeros(KV, BF16)

    def wait(r, p, slot, sem):
        @pl.when(p * PAGE < lengths[r])
        def _():
            pltpu.make_async_copy(pool.at[0], slot, sem).wait()

    each(start)
    small_copies[3].wait()
    each(wait)

    @pl.when(leading())
    def _():
        for j in range(MIG):
            r = ids[j]
            last = lengths[r] - 1
            row = fresh[r].astype(F32)
            for p in range(PAGES):
                ref, index = slots[j * PAGES + p]

                @pl.when(last // PAGE == p)
                def _():
                    write_row(ref, index, last % PAGE, row[0:1], row[1:2])


def gather_pages(table, lengths, ids, fresh, pool):
    return pl.pallas_call(
        gather_kernel,
        out_shape=[jax.ShapeDtypeStruct((count,) + KV, BF16) for count in PARTS],
        in_specs=[HBM] * 5,
        out_specs=[VMEM] * 3,
        scratch_shapes=TABLE_SCRATCH
        + [
            pltpu.SMEM((MIG,), jnp.int32),
            pltpu.VMEM((REQ, 2, HDIM), BF16),
            DMA((4,)),
            DMA((MIG * PAGES,)),
        ],
        compiler_params=pltpu.CompilerParams(vmem_limit_bytes=4 << 20),
        name="gather_pages",
    )(*in_hbm(table, lengths, ids, fresh, pool))


def first_kernel(
    table_in, lengths_in, query_in, fresh_in, pages, weight_in,
    attn, keep, give, weight,
    qs, ks, vs, os, ss, table, lengths, query, fresh, small, wsem,
):
    y, core = place()
    lead = leading()
    [weight_copy] = started((weight_in, weight, wsem))

    @pl.when(lead)
    def _():
        copies = started(
            (table_in, table, small.at[0]),
            (lengths_in, lengths, small.at[1]),
            (query_in, query, small.at[2]),
            (fresh_in, fresh, small.at[3]),
        )
        for c in copies:
            c.wait()
        spread(
            qs, ks, vs,
            query[...].astype(F32), fresh[:, 0, :].astype(F32), fresh[:, 1, :].astype(F32),
        )
        for g in range(REQ // GROUP):
            scores(lengths, table, qs, ks, pages, ss, g)
        for g in range(REQ // GROUP):
            mix(table, qs, ks, vs, os, pages, ss, g)
        collect(os, attn)

    weight_copy.wait()

    @pl.when(lead)
    def _():
        a = attn[...]
        for out, c in ((give, 1 - core), (keep, core)):
            for k in range(4):
                block = lax.rem(y + k, 4) * 2 + c
                w = weight[pl.ds(pl.multiple_of(block * WIDTH, WIDTH), WIDTH), :]
                out[k] = lax.dot_general(
                    a, w, (((1,), (1,)), ((), ())), preferred_element_type=F32
                )

    @pl.when(jnp.logical_not(lead))
    def _():
        attn[...] = jnp.zeros_like(attn)
        keep[...] = jnp.zeros_like(keep)
        give[...] = jnp.zeros_like(give)


def first_layer(table, lengths, query, fresh, pages, weight):
    part = (4, REQ, WIDTH)
    return pl.pallas_call(
        first_kernel,
        out_shape=(
            jax.ShapeDtypeStruct((REQ, WIDTH), BF16),
            jax.ShapeDtypeStruct(part, F32),
            jax.ShapeDtypeStruct(part, F32),
            pltpu.VMEM((D, WIDTH), BF16),
        ),
        in_specs=[HBM] * 4 + [VMEM, HBM],
        out_specs=(VMEM,) * 4,
        scratch_shapes=ROW_SCRATCH
        + TABLE_SCRATCH
        + [
            pltpu.VMEM((REQ, WIDTH), BF16),
            pltpu.VMEM((REQ, 2, HDIM), BF16),
            DMA((4,)),
            DMA,
        ],
        compiler_params=pltpu.CompilerParams(vmem_limit_bytes=8 << 20),
        name="first_layer",
    )(*in_hbm(table, lengths, query, fresh), *in_vmem(pages), *in_hbm(weight))


def pair_kernel(keep, got, residual, own, a, b, c):
    own[...] = keep[0] + got[0] + residual[...].astype(F32)
    for k, out in ((1, a), (2, b), (3, c)):
        out[...] = (keep[k] + got[k]).astype(BF16)


def pair_sum(keep, got, residual):
    share = (REQ, WIDTH)
    return pl.pallas_call(
        pair_kernel,
        out_shape=(jax.ShapeDtypeStruct(share, F32),)
        + (jax.ShapeDtypeStruct(share, BF16),) * 3,
        in_specs=[VMEM] * 3,
        out_specs=(VMEM,) * 4,
        compiler_params=pltpu.CompilerParams(vmem_limit_bytes=4 << 20),
        name="pair_sum",
    )(keep, got, residual)


def share_kernel(ids_in, lengths_in, own, a, b, c, share, moved, wide, sent, ids, lengths, small):
    copies = started((ids_in, ids, small.at[0]), (lengths_in, lengths, small.at[1]))
    total = own[...] + a[...].astype(F32) + b[...].astype(F32) + c[...].astype(F32)
    rounded = total.astype(BF16)
    share[...] = rounded
    wide[...] = rounded.astype(F32)
    for copy in copies:
        copy.wait()
    lane = lax.broadcasted_iota(jnp.int32, (1, WIDTH), 1)
    for j in range(MIG):
        r = ids[j]
        sent[pl.ds(j, 1), :] = wide[pl.ds(r, 1), :]
        last = lengths[r] - 1
        sent[pl.ds(MIG + j, 1), :] = jnp.where(
            lane < HDIM, last // PAGE, last % PAGE
        ).astype(F32)
    moved[...] = sent[...].astype(BF16)


def share_sum(ids, lengths, own, a, b, c):
    return pl.pallas_call(
        share_kernel,
        out_shape=(
            jax.ShapeDtypeStruct((REQ, WIDTH), BF16),
            jax.ShapeDtypeStruct((SENT, WIDTH), BF16),
        ),
        in_specs=[HBM] * 2 + [VMEM] * 4,
        out_specs=(VMEM, VMEM),
        scratch_shapes=[
            pltpu.VMEM((REQ, WIDTH), F32),
            pltpu.VMEM((SENT, WIDTH), F32),
            pltpu.SMEM((MIG,), jnp.int32),
            pltpu.SMEM((REQ,), jnp.int32),
            DMA((2,)),
        ],
        compiler_params=pltpu.CompilerParams(vmem_limit_bytes=4 << 20),
        name="share_sum",
    )(*in_hbm(ids, lengths), own, a, b, c)


def join_kernel(share, arrived, moved_in, hidden, rows, last):
    lead = leading()

    @pl.when(lead)
    def _():
        hidden[...] = share[...]

    @pl.when(jnp.logical_not(lead))
    def _():
        hidden[...] = arrived[...]

    rows[:REQ, :] = arrived[...]
    rows[REQ:, :] = moved_in[:MIG, :]
    last[...] = moved_in[MIG:, : 2 * HDIM].astype(F32).astype(jnp.int32)


def join(share, arrived, moved_in):
    return pl.pallas_call(
        join_kernel,
        out_shape=(
            jax.ShapeDtypeStruct((REQ, WIDTH), BF16),
            jax.ShapeDtypeStruct((ROWS, WIDTH), BF16),
            jax.ShapeDtypeStruct((MIG, 2 * HDIM), jnp.int32),
        ),
        in_specs=[VMEM] * 3,
        out_specs=(VMEM,) * 3,
        compiler_params=pltpu.CompilerParams(vmem_limit_bytes=4 << 20),
        name="join",
    )(share, arrived, moved_in)


def second_kernel(
    table_in, lengths_in, first_attn, m0, m1, m2, m3, n0, n1, n2, n3, gain, pages, weight,
    kv_weight, attn, moved_kv,
    qs, ks, vs, os, ss, table, lengths, small,
):
    y, core = place()

    @pl.when(jnp.logical_not(leading()))
    def _():
        copies = started((table_in, table, small.at[0]), (lengths_in, lengths, small.at[1]))
        blocks = []
        square = jnp.zeros((ROWS, 1), F32)
        for refs, c in (((m0, m1, m2, m3), core), ((n0, n1, n2, n3), 1 - core)):
            for k, ref in enumerate(refs):
                x = ref[...].astype(F32)
                square += jnp.sum(x * x, axis=-1, keepdims=True)
                blocks.append((x, lax.rem(y + 4 - k, 4) * 2 + c))
        factor = lax.rsqrt(square * (1.0 / D) + 1e-05)
        q = jnp.zeros((ROWS, WIDTH), F32)
        kv = jnp.zeros((ROWS, 2 * HDIM), F32)
        for x, block in blocks:
            at = pl.ds(pl.multiple_of(block * WIDTH, WIDTH), WIDTH)
            x = (x * factor * gain[at].reshape(1, WIDTH)).astype(BF16)
            q += jnp.dot(x, weight[at, :], preferred_element_type=F32)
            kv += jnp.dot(x, kv_weight[at, :], preferred_element_type=F32)
        q = q.astype(BF16).astype(F32)
        kv = kv.astype(BF16).astype(F32)
        moved_kv[...] = kv[REQ:]
        spread(qs, ks, vs, q[:REQ], kv[:REQ, :HDIM], kv[:REQ, HDIM:])
        for copy in copies:
            copy.wait()
        for g in range(REQ // GROUP):
            scores(lengths, table, qs, ks, pages, ss, g)
        for g in range(REQ // GROUP):
            mix(table, qs, ks, vs, os, pages, ss, g)
        collect(os, attn)

    @pl.when(leading())
    def _():
        attn[...] = first_attn[...]
        moved_kv[...] = jnp.zeros_like(moved_kv)


def second_layer(table, lengths, first_attn, mine, other, gain, pages, weight, kv_weight):
    return pl.pallas_call(
        second_kernel,
        out_shape=(
            jax.ShapeDtypeStruct((REQ, WIDTH), BF16),
            jax.ShapeDtypeStruct((MIG, 2 * HDIM), F32),
        ),
        in_specs=[HBM] * 2 + [VMEM] * 13,
        out_specs=(VMEM, VMEM),
        scratch_shapes=ROW_SCRATCH + TABLE_SCRATCH + [DMA((2,))],
        compiler_params=pltpu.CompilerParams(vmem_limit_bytes=24 << 20),
        name="second_layer",
    )(*in_hbm(table, lengths), first_attn, *mine, *other, gain, *in_vmem(pages, weight, kv_weight))


def patch_kernel(last_in, rows, back, ahead, later, out, held, last, small, insem, outsem):
    [last_copy] = started((last_in, last, small))
    begin = [sum(PARTS[:i]) for i in range(3)]
    copies = started(
        *[
            (ref, held.at[pl.ds(begin[i], PARTS[i])], insem.at[i])
            for i, ref in enumerate((back, ahead, later))
        ]
    )
    last_copy.wait()
    for c in copies:
        c.wait()
    lead = leading()
    leave = []
    for j in range(MIG):

        @pl.when(jnp.logical_not(lead))
        def _():
            write_row(
                held,
                j * PAGES + last[j, 0],
                last[j, HDIM],
                rows[pl.ds(j, 1), :HDIM],
                rows[pl.ds(j, 1), HDIM:],
            )

        at = pl.ds(j * PAGES, PAGES)
        leave += started((held.at[at], out.at[at], outsem.at[j]))
    for c in leave:
        c.wait()


def patch(last, rows, *parts):
    shape = (MIG * PAGES,) + KV
    return pl.pallas_call(
        patch_kernel,
        out_shape=jax.ShapeDtypeStruct(shape, BF16),
        in_specs=[HBM, VMEM] + [pl.BlockSpec(memory_space=pl.ANY)] * 3,
        out_specs=HBM,
        scratch_shapes=[
            pltpu.VMEM(shape, BF16),
            pltpu.SMEM((MIG, 2 * HDIM), jnp.int32),
            DMA,
            DMA((3,)),
            DMA((MIG,)),
        ],
        compiler_params=pltpu.CompilerParams(vmem_limit_bytes=8 << 20),
        name="patch",
    )(last, rows, *parts)


def after(value, *others):
    return lax.optimization_barrier((value,) + others)[0]


def local(
    query_rows, new_kv, residual, kv_cache, page_table, lengths, migrate_ids,
    projection, kv_weight, norm_gain,
):
    replicas = lax.axis_size("inst")
    table = page_table.T

    def across(value, by):
        return lax.ppermute(value, "tensor", [(i, (i + 2 * by) % 8) for i in range(8)])

    def to_twin(value):
        return lax.ppermute(value, "tensor", [(i, i ^ 1) for i in range(8)])

    down = [(i, i // 4 * 4 + (i + 3) % 4) for i in range(replicas)]
    turn = [(i, (i + 3) % replicas) if i % 4 == 1 else pair for i, pair in enumerate(down)]

    def to_next(value):
        return lax.ppermute(
            value, "inst", [(i, (i + 1) % replicas) for i in range(replicas)]
        )

    pool = kv_cache[0]
    back, ahead, later = gather_pages(table, lengths, migrate_ids, new_kv, pool)
    ahead = to_next(ahead)
    back = lax.ppermute(back, "inst", down)

    attn, keep, give, weight = first_layer(
        table, lengths, query_rows, new_kv, pool, projection[0]
    )
    own, a, b, c = pair_sum(keep, to_twin(give), residual)
    share, moved = share_sum(
        migrate_ids, lengths, own, across(a, 1), across(b, 2), across(c, 3)
    )
    arrived = lax.ppermute(share, "section", [(0, 1), (1, 0)])
    links = [(2 * i, 2 * ((i + 1) % replicas) + 1) for i in range(replicas)]
    moved_in = lax.ppermute(
        moved, ("inst", "section"), links + [(b, a) for a, b in links]
    )
    flat_kv = after(kv_weight, share).reshape(D, 2 * HDIM)
    back = lax.ppermute(after(back, flat_kv), "inst", down)
    arrived = after(arrived, flat_kv)
    later = to_next(after(later, arrived, moved_in, ahead))

    hidden, rows, last = join(share, arrived, moved_in)
    mine = [rows] + [across(rows, k) for k in (1, 2, 3)]
    other = [to_twin(after(rows, mine[1]))] + [to_twin(m) for m in mine[1:]]
    back = lax.ppermute(after(back, rows), "inst", turn)
    attn, second_rows = second_layer(
        table, lengths, attn, mine, other, norm_gain, pool, weight, flat_kv
    )
    migrated = patch(last, second_rows, back, ahead, later)
    return attn[None], hidden, migrated.reshape((1, MIG, PAGES) + KV)


def solution(mesh):
    return jax.shard_map(
        local,
        mesh=mesh,
        in_specs=(
            P("inst", "tensor"),
            P("inst", None, "tensor"),
            P("inst", "tensor"),
            P("section", "inst", None, None, "tensor"),
            P("inst", None),
            P("inst"),
            P("inst"),
            P("section", None, "tensor"),
            P(None, None, "tensor"),
            P(),
        ),
        out_specs=(
            P("section", "inst", "tensor"),
            P("inst", "tensor"),
            P("section", "inst", None, None, None, "tensor"),
        ),
        check_vma=False,
    )
```

time: 91.8 us -> 60.3 us (0.66)
  the two profiles are of different devices: /device:TPU:201 before, /device:TPU:161 now
where the time goes in v2:
time: 60.3 us; the launch traced here: 60 us
  starting transfers between devices  31.7 us (53%)
  Pallas kernels  13.8 us (23%)
  waiting for transfers between devices  13.2 us (22%)
  between operations  0.91 us (2%)
    ppermute x5, starting transfers between devices, to_twin(): return lax.ppermute(value, 'tensor', [(i, i ^ 1) for i in range(8)])  8.76 us
    ppermute x6, starting transfers between devices, across(): lax.ppermute(value, 'tensor', [(i, (i + 2 * by) % 8) for i in range(8)])  8.45 us
    ppermute x1, waiting for transfers between devices, local(): lax.ppermute(moved, ('inst', 'section'), links + [(b, a) for a, b in links])  5.84 us
    pallas_call x1, Pallas kernels, second_layer(): pl.pallas_call(second_kernel, out_shape=(jax.ShapeDtypeStruct((REQ, WIDTH...  5.29 us
    ppermute x1, starting transfers between devices, local(): arrived = lax.ppermute(share, 'section', [(0, 1), (1, 0)])  4.58 us
    ppermute x1, starting transfers between devices, local(): back = lax.ppermute(after(back, rows), 'inst', turn)  3.75 us
    ppermute x1, starting transfers between devices, local(): back = lax.ppermute(after(back, flat_kv), 'inst', down)  3.57 us
    ppermute x6, waiting for transfers between devices, across(): lax.ppermute(value, 'tensor', [(i, (i + 2 * by) % 8) for i in range(8)])  2.97 us
  transfers between devices with their start and end apart: 18, of which 8 were waited for; matrix products, arithmetic and copies ran while one was open for 0% of the time, Pallas kernels for 15%

profile of v2, /device:TPU:161, one launch (start us, length us, event | category | flops | bytes accessed | tf_op | source)
XLA Modules:
  0.0 60.0 jit_solution(8115180526773597170)
XLA Ops:
  0.6 2.6 %gather_pages.1 = (bf16[8,2,128,128]{3,2,1,0:T(8,128)(2,1)S(1)}, bf16[15,2,128,128]{3,2,1,0:T(8,128)(2,1)S(1)}, bf16[9,2,128,128]{3,2,1,0:T(8,128)(2,1)S(1)}) custom-call(s32[4,32]{1,0:T(4,128)} %bitcast.16, s32[32]{0:T(128)} %lengths_in.7, s32[8]{0:T(128)} %ids_in.3, bf16[32,2,128]{2,1,0:T(2,128)(2,1)} %fresh_in.3, bf16[128,2,128,128]{3,2,1,0:T(8,128)(2,1)} %bitcast.9), custom_call_target="tpu_custom_call" | custom-call | tf_op jit(solution)/shard_map/gather_pages/pallas_call | solution.py:187
  3.3 2.6 %collective-permute-start.13 = (bf16[8,2,128,128]{3,2,1,0:T(8,128)(2,1)S(1)}, bf16[8,2,128,128]{3,2,1,0:T(8,128)(2,1)S(1)}, u32[]{:S(2)}, u32[]{:S(2)}) collective-permute-start(bf16[8,2,128,128]{3,2,1,0:T(8,128)(2,1)S(1)} %get-tuple-element.45), channel_id=1, source_target_pairs={{0,48},{16,0},{32,16},{48,32},{64,112},{80,64},{96,80},{112,96},{1... | collective-permute-start | bytes 1572872 | tf_op jit(solution)/shard_map/ppermute | solution.py:505
  5.8 2.4 %first_layer.1 = (bf16[32,512]{1,0:T(8,128)(2,1)S(1)}, f32[4,32,512]{2,1,0:T(8,128)S(1)}, f32[4,32,512]{2,1,0:T(8,128)S(1)}, bf16[4096,512]{1,0:T(8,128)(2,1)S(1)}) custom-call(s32[4,32]{1,0:T(4,128)} %bitcast.17, s32[32]{0:T(128)} %lengths_in.7, bf16[32,512]{1,0:T(8,128)(2,1)} %query_in.1, bf16[32,2,128]{2,1,0:T(2,128)(2,1)} %fresh_in.3, ...), custom_call_target="tpu_custom_call" | custom-call | tf_op jit(solution)/shard_map/first_layer/pallas_call | solution.py:255
  8.3 1.0 %collective-permute-start = (f32[4,32,512]{2,1,0:T(8,128)S(1)}, f32[4,32,512]{2,1,0:T(8,128)S(1)}, u32[]{:S(2)}, u32[]{:S(2)}) collective-permute-start(f32[4,32,512]{2,1,0:T(8,128)S(1)} %get-tuple-element.29), channel_id=1, source_target_pairs={{0,1},{1,0},{2,3},{3,2},{4,5},{5,4},{6,7},{7,6},{8,9},{9,8},{10,11... | collective-permute-start | bytes 786440 | tf_op jit(solution)/shard_map/ppermute | solution.py:492
  9.3 1.2 %collective-permute-done.got = f32[4,32,512]{2,1,0:T(8,128)S(1)} collective-permute-done((f32[4,32,512]{2,1,0:T(8,128)S(1)}, f32[4,32,512]{2,1,0:T(8,128)S(1)}, u32[]{:S(2)}, u32[]{:S(2)}) %collective-permute-start) | collective-permute-done | bytes 262176 | tf_op jit(solution)/shard_map/ppermute | solution.py:492
  10.5 1.4 %collective-permute-start.1 = (bf16[32,512]{1,0:T(8,128)(2,1)S(1)}, bf16[32,512]{1,0:T(8,128)(2,1)S(1)}, u32[]{:S(2)}, u32[]{:S(2)}) collective-permute-start(bf16[32,512]{1,0:T(8,128)(2,1)S(1)} %get-tuple-element.31), channel_id=1, source_target_pairs={{0,2},{1,3},{2,4},{3,5},{4,6},{5,7},{6,0},{7,1},{8,10},{9,11},{10,... | collective-permute-start | bytes 98312 | tf_op jit(solution)/shard_map/ppermute | solution.py:489
  11.9 2.6 %collective-permute-start.2 = (bf16[32,512]{1,0:T(8,128)(2,1)S(1)}, bf16[32,512]{1,0:T(8,128)(2,1)S(1)}, u32[]{:S(2)}, u32[]{:S(2)}) collective-permute-start(bf16[32,512]{1,0:T(8,128)(2,1)S(1)} %get-tuple-element.32), channel_id=1, source_target_pairs={{0,4},{1,5},{2,6},{3,7},{4,0},{5,1},{6,2},{7,3},{8,12},{9,13},{10,... | collective-permute-start | bytes 98312 | tf_op jit(solution)/shard_map/ppermute | solution.py:489
  14.5 1.1 %collective-permute-start.3 = (bf16[32,512]{1,0:T(8,128)(2,1)S(1)}, bf16[32,512]{1,0:T(8,128)(2,1)S(1)}, u32[]{:S(2)}, u32[]{:S(2)}) collective-permute-start(bf16[32,512]{1,0:T(8,128)(2,1)S(1)} %get-tuple-element.33), channel_id=1, source_target_pairs={{0,6},{1,7},{2,0},{3,1},{4,2},{5,3},{6,4},{7,5},{8,14},{9,15},{10,... | collective-permute-start | bytes 98312 | tf_op jit(solution)/shard_map/ppermute | solution.py:489
  15.6 0.9 %collective-permute-done.2.b = bf16[32,512]{1,0:T(8,128)(2,1)S(1)} collective-permute-done((bf16[32,512]{1,0:T(8,128)(2,1)S(1)}, bf16[32,512]{1,0:T(8,128)(2,1)S(1)}, u32[]{:S(2)}, u32[]{:S(2)}) %collective-permute-start.2) | collective-permute-done | bytes 32800 | tf_op jit(solution)/shard_map/ppermute | solution.py:489
  16.5 1.1 %collective-permute-done.3.c = bf16[32,512]{1,0:T(8,128)(2,1)S(1)} collective-permute-done((bf16[32,512]{1,0:T(8,128)(2,1)S(1)}, bf16[32,512]{1,0:T(8,128)(2,1)S(1)}, u32[]{:S(2)}, u32[]{:S(2)}) %collective-permute-start.3) | collective-permute-done | bytes 32800 | tf_op jit(solution)/shard_map/ppermute | solution.py:489
  17.6 0.8 %share_sum.1 = (bf16[32,512]{1,0:T(8,128)(2,1)S(1)}, bf16[16,512]{1,0:T(8,128)(2,1)S(1)}) custom-call(s32[8]{0:T(128)} %ids_in.3, s32[32]{0:T(128)} %lengths_in.7, f32[32,512]{1,0:T(8,128)S(1)} %get-tuple-element.30.own, bf16[32,512]{1,0:T(8,128)(2,1)S(1)} %collective-permute-done.1.a, bf16[32,512]{1,0:T(8,128)(2,1)S(1)} %collective-permute-done.2.b, ...), custom_call_target="tpu_custom_call" | custom-call | tf_op jit(solution)/shard_map/share_sum/pallas_call | solution.py:317
  18.6 3.6 %collective-permute-start.14 = (bf16[8,2,128,128]{3,2,1,0:T(8,128)(2,1)S(1)}, bf16[8,2,128,128]{3,2,1,0:T(8,128)(2,1)S(1)}, u32[]{:S(2)}, u32[]{:S(2)}) collective-permute-start(bf16[8,2,128,128]{3,2,1,0:T(8,128)(2,1)S(1)} %collective-permute-done.13), channel_id=1, source_target_pairs={{0,48},{16,0},{32,16},{48,32},{64,112},{80,64},{96,80},{112,96},{1... | collective-permute-start | bytes 1572872 | tf_op jit(solution)/shard_map/ppermute | solution.py:520
  22.2 4.6 %collective-permute-start.4 = (bf16[32,512]{1,0:T(8,128)(2,1)S(1)}, bf16[32,512]{1,0:T(8,128)(2,1)S(1)}, u32[]{:S(2)}, u32[]{:S(2)}) collective-permute-start(bf16[32,512]{1,0:T(8,128)(2,1)S(1)} %get-tuple-element.34.share), channel_id=1, source_target_pairs={{0,8},{8,0},{1,9},{9,1},{2,10},{10,2},{3,11},{11,3},{4,12},{12,4},... | collective-permute-start | bytes 98312 | tf_op jit(solution)/shard_map/ppermute | solution.py:514
  26.9 2.0 %collective-permute-done.4.arrived = bf16[32,512]{1,0:T(8,128)(2,1)S(1)} collective-permute-done((bf16[32,512]{1,0:T(8,128)(2,1)S(1)}, bf16[32,512]{1,0:T(8,128)(2,1)S(1)}, u32[]{:S(2)}, u32[]{:S(2)}) %collective-permute-start.4) | collective-permute-done | bytes 32800 | tf_op jit(solution)/shard_map/ppermute | solution.py:514
  28.9 5.8 %collective-permute-done.5.moved_in = bf16[16,512]{1,0:T(8,128)(2,1)S(1)} collective-permute-done((bf16[16,512]{1,0:T(8,128)(2,1)S(1)}, bf16[16,512]{1,0:T(8,128)(2,1)S(1)}, u32[]{:S(2)}, u32[]{:S(2)}) %collective-permute-start.5) | collective-permute-done | bytes 16416 | tf_op jit(solution)/shard_map/ppermute | solution.py:516
  35.4 3.8 %collective-permute-start.15 = (bf16[8,2,128,128]{3,2,1,0:T(8,128)(2,1)S(1)}, bf16[8,2,128,128]{3,2,1,0:T(8,128)(2,1)S(1)}, u32[]{:S(2)}, u32[]{:S(2)}) collective-permute-start(bf16[8,2,128,128]{3,2,1,0:T(8,128)(2,1)S(1)} %collective-permute-done.14), channel_id=1, source_target_pairs={{0,48},{16,64},{32,16},{48,32},{64,112},{80,128},{96,80},{112,96},... | collective-permute-start | bytes 1572872 | tf_op jit(solution)/shard_map/ppermute | solution.py:527
  39.1 3.2 %collective-permute-start.7 = (bf16[40,512]{1,0:T(8,128)(2,1)S(1)}, bf16[40,512]{1,0:T(8,128)(2,1)S(1)}, u32[]{:S(2)}, u32[]{:S(2)}) collective-permute-start(bf16[40,512]{1,0:T(8,128)(2,1)S(1)} %get-tuple-element.39.m0), channel_id=1, source_target_pairs={{0,4},{1,5},{2,6},{3,7},{4,0},{5,1},{6,2},{7,3},{8,12},{9,13},{10,... | collective-permute-start | bytes 122888 | tf_op jit(solution)/shard_map/ppermute | solution.py:489
  42.5 1.0 %collective-permute-done.6.m1 = bf16[40,512]{1,0:T(8,128)(2,1)S(1)} collective-permute-done((bf16[40,512]{1,0:T(8,128)(2,1)S(1)}, bf16[40,512]{1,0:T(8,128)(2,1)S(1)}, u32[]{:S(2)}, u32[]{:S(2)}) %collective-permute-start.6) | collective-permute-done | bytes 40992 | tf_op jit(solution)/shard_map/ppermute | solution.py:489
  43.5 5.0 %collective-permute-start.9 = (bf16[40,512]{1,0:T(8,128)(2,1)S(1)}, bf16[40,512]{1,0:T(8,128)(2,1)S(1)}, u32[]{:S(2)}, u32[]{:S(2)}) collective-permute-start(bf16[40,512]{1,0:T(8,128)(2,1)S(1)} %get-tuple-element.39.m0), channel_id=1, source_target_pairs={{0,1},{1,0},{2,3},{3,2},{4,5},{5,4},{6,7},{7,6},{8,9},{9,8},{10,11... | collective-permute-start | bytes 122888 | tf_op jit(solution)/shard_map/ppermute | solution.py:492
  48.5 1.1 %collective-permute-start.10 = (bf16[40,512]{1,0:T(8,128)(2,1)S(1)}, bf16[40,512]{1,0:T(8,128)(2,1)S(1)}, u32[]{:S(2)}, u32[]{:S(2)}) collective-permute-start(bf16[40,512]{1,0:T(8,128)(2,1)S(1)} %collective-permute-done.6.m1), channel_id=1, source_target_pairs={{0,1},{1,0},{2,3},{3,2},{4,5},{5,4},{6,7},{7,6},{8,9},{9,8},{10,11... | collective-permute-start | bytes 122888 | tf_op jit(solution)/shard_map/ppermute | solution.py:492
  49.6 1.6 %collective-permute-start.11 = (bf16[40,512]{1,0:T(8,128)(2,1)S(1)}, bf16[40,512]{1,0:T(8,128)(2,1)S(1)}, u32[]{:S(2)}, u32[]{:S(2)}) collective-permute-start(bf16[40,512]{1,0:T(8,128)(2,1)S(1)} %collective-permute-done.7.m2), channel_id=1, source_target_pairs={{0,1},{1,0},{2,3},{3,2},{4,5},{5,4},{6,7},{7,6},{8,9},{9,8},{10,11... | collective-permute-start | bytes 122888 | tf_op jit(solution)/shard_map/ppermute | solution.py:492
  51.2 0.9 %collective-permute-done.11.n2 = bf16[40,512]{1,0:T(8,128)(2,1)S(1)} collective-permute-done((bf16[40,512]{1,0:T(8,128)(2,1)S(1)}, bf16[40,512]{1,0:T(8,128)(2,1)S(1)}, u32[]{:S(2)}, u32[]{:S(2)}) %collective-permute-start.11) | collective-permute-done | bytes 40992 | tf_op jit(solution)/shard_map/ppermute | solution.py:492
  52.4 5.3 %second_layer.1 = (bf16[32,512]{1,0:T(8,128)(2,1)}, f32[8,256]{1,0:T(8,128)S(1)}) custom-call(s32[4,32]{1,0:T(4,128)} %bitcast.18, s32[32]{0:T(128)} %lengths_in.7, bf16[32,512]{1,0:T(8,128)(2,1)S(1)} %get-tuple-element.27.first_attn, bf16[40,512]{1,0:T(8,128)(2,1)S(1)} %get-tuple-element.39.m0, bf16[40,512]{1,0:T(8,128)(2,1)S(1)} %collective-permute-done.6.m1, ...), custom_call_target="tpu_custom_call" | custom-call | tf_op jit(solution)/shard_map/second_layer/pallas_call | solution.py:412
  57.7 2.1 %patch.1 = bf16[32,2,128,128]{3,2,1,0:T(8,128)(2,1)} custom-call(s32[8,256]{1,0:T(8,128)S(1)} %get-tuple-element.43.last_in, f32[8,256]{1,0:T(8,128)S(1)} %get-tuple-element.44.rows, bf16[8,2,128,128]{3,2,1,0:T(8,128)(2,1)S(1)} %collective-permute-done.15.back, bf16[15,2,128,128]{3,2,1,0:T(8,128)(2,1)S(1)} %collective-permute-done.16.ahead, ...), custom_call_target="tpu_custom_call" | custom-call | tf_op jit(solution)/shard_map/patch/pallas_call | solution.py:460
  (28 shorter events, 1.6 us)
Async XLA Ops:
  0.6 5.2 %copy-start = (bf16[1,128,2,128,128]{4,3,2,1,0:T(8,128)(2,1)S(1)}, bf16[1,128,2,128,128]{4,3,2,1,0:T(8,128)(2,1)}, u32[]{:S(2)}) copy-start(bf16[1,128,2,128,128]{4,3,2,1,0:T(8,128)(2,1)} %param.13) | copy-start | bytes 25165828
  3.3 15.4 %collective-permute-start.13 = (bf16[8,2,128,128]{3,2,1,0:T(8,128)(2,1)S(1)}, bf16[8,2,128,128]{3,2,1,0:T(8,128)(2,1)S(1)}, u32[]{:S(2)}, u32[]{:S(2)}) collective-permute-start(bf16[8,2,128,128]{3,2,1,0:T(8,128)(2,1)S(1)} %get-tuple-element.45), channel_id=1, source_target_pairs={{0,48},{16,0},{32,16},{48,32},{64,112},{80,64},{96,80},{112,96},{1... | collective-permute-start | bytes 1572872 | tf_op jit(solution)/shard_map/ppermute | solution.py:505
  5.8 28.9 %collective-permute-start.16 = (bf16[15,2,128,128]{3,2,1,0:T(8,128)(2,1)S(1)}, bf16[15,2,128,128]{3,2,1,0:T(8,128)(2,1)S(1)}, u32[]{:S(2)}, u32[]{:S(2)}) collective-permute-start(bf16[15,2,128,128]{3,2,1,0:T(8,128)(2,1)S(1)} %get-tuple-element.48), channel_id=1, source_target_pairs={{0,16},{16,32},{32,48},{48,64},{64,80},{80,96},{96,112},{112,128},... | collective-permute-start | bytes 2949128 | tf_op jit(solution)/shard_map/ppermute | solution.py:498
  5.8 4.7 %copy-start.1 = (bf16[32,512]{1,0:T(8,128)(2,1)S(1)}, bf16[32,512]{1,0:T(8,128)(2,1)}, u32[]{:S(2)}) copy-start(bf16[32,512]{1,0:T(8,128)(2,1)} %residual.1) | copy-start | bytes 98308
  5.8 12.5 %copy-start.3 = (bf16[4096,2,128]{2,1,0:T(2,128)(2,1)S(1)}, bf16[4096,2,128]{2,1,0:T(2,128)(2,1)}, u32[]{:S(2)}) copy-start(bf16[4096,2,128]{2,1,0:T(2,128)(2,1)} %param.18) | copy-start | bytes 6291460
  8.3 44.2 %copy-start.2 = (f32[4096]{0:T(1024)S(1)}, f32[4096]{0:T(1024)}, u32[]{:S(2)}) copy-start(f32[4096]{0:T(1024)} %gain.1) | copy-start | bytes 49156
  8.3 2.2 %collective-permute-start = (f32[4,32,512]{2,1,0:T(8,128)S(1)}, f32[4,32,512]{2,1,0:T(8,128)S(1)}, u32[]{:S(2)}, u32[]{:S(2)}) collective-permute-start(f32[4,32,512]{2,1,0:T(8,128)S(1)} %get-tuple-element.29), channel_id=1, source_target_pairs={{0,1},{1,0},{2,3},{3,2},{4,5},{5,4},{6,7},{7,6},{8,9},{9,8},{10,11... | collective-permute-start | bytes 786440 | tf_op jit(solution)/shard_map/ppermute | solution.py:492
  10.5 5.1 %collective-permute-start.1 = (bf16[32,512]{1,0:T(8,128)(2,1)S(1)}, bf16[32,512]{1,0:T(8,128)(2,1)S(1)}, u32[]{:S(2)}, u32[]{:S(2)}) collective-permute-start(bf16[32,512]{1,0:T(8,128)(2,1)S(1)} %get-tuple-element.31), channel_id=1, source_target_pairs={{0,2},{1,3},{2,4},{3,5},{4,6},{5,7},{6,0},{7,1},{8,10},{9,11},{10,... | collective-permute-start | bytes 98312 | tf_op jit(solution)/shard_map/ppermute | solution.py:489
  11.9 4.6 %collective-permute-start.2 = (bf16[32,512]{1,0:T(8,128)(2,1)S(1)}, bf16[32,512]{1,0:T(8,128)(2,1)S(1)}, u32[]{:S(2)}, u32[]{:S(2)}) collective-permute-start(bf16[32,512]{1,0:T(8,128)(2,1)S(1)} %get-tuple-element.32), channel_id=1, source_target_pairs={{0,4},{1,5},{2,6},{3,7},{4,0},{5,1},{6,2},{7,3},{8,12},{9,13},{10,... | collective-permute-start | bytes 98312 | tf_op jit(solution)/shard_map/ppermute | solution.py:489
  14.5 3.1 %collective-permute-start.3 = (bf16[32,512]{1,0:T(8,128)(2,1)S(1)}, bf16[32,512]{1,0:T(8,128)(2,1)S(1)}, u32[]{:S(2)}, u32[]{:S(2)}) collective-permute-start(bf16[32,512]{1,0:T(8,128)(2,1)S(1)} %get-tuple-element.33), channel_id=1, source_target_pairs={{0,6},{1,7},{2,0},{3,1},{4,2},{5,3},{6,4},{7,5},{8,14},{9,15},{10,... | collective-permute-start | bytes 98312 | tf_op jit(solution)/shard_map/ppermute | solution.py:489
  18.6 16.7 %collective-permute-start.14 = (bf16[8,2,128,128]{3,2,1,0:T(8,128)(2,1)S(1)}, bf16[8,2,128,128]{3,2,1,0:T(8,128)(2,1)S(1)}, u32[]{:S(2)}, u32[]{:S(2)}) collective-permute-start(bf16[8,2,128,128]{3,2,1,0:T(8,128)(2,1)S(1)} %collective-permute-done.13), channel_id=1, source_target_pairs={{0,48},{16,0},{32,16},{48,32},{64,112},{80,64},{96,80},{112,96},{1... | collective-permute-start | bytes 1572872 | tf_op jit(solution)/shard_map/ppermute | solution.py:520
  22.2 6.7 %collective-permute-start.4 = (bf16[32,512]{1,0:T(8,128)(2,1)S(1)}, bf16[32,512]{1,0:T(8,128)(2,1)S(1)}, u32[]{:S(2)}, u32[]{:S(2)}) collective-permute-start(bf16[32,512]{1,0:T(8,128)(2,1)S(1)} %get-tuple-element.34.share), channel_id=1, source_target_pairs={{0,8},{8,0},{1,9},{9,1},{2,10},{10,2},{3,11},{11,3},{4,12},{12,4},... | collective-permute-start | bytes 98312 | tf_op jit(solution)/shard_map/ppermute | solution.py:514
  26.8 7.9 %collective-permute-start.5 = (bf16[16,512]{1,0:T(8,128)(2,1)S(1)}, bf16[16,512]{1,0:T(8,128)(2,1)S(1)}, u32[]{:S(2)}, u32[]{:S(2)}) collective-permute-start(bf16[16,512]{1,0:T(8,128)(2,1)S(1)} %get-tuple-element.37), channel_id=1, source_target_pairs={{0,24},{16,40},{32,56},{48,72},{64,88},{80,104},{96,120},{112,136}... | collective-permute-start | bytes 49160 | tf_op jit(solution)/shard_map/ppermute | solution.py:516
  34.7 23.0 %collective-permute-start.17 = (bf16[9,2,128,128]{3,2,1,0:T(8,128)(2,1)S(1)}, bf16[9,2,128,128]{3,2,1,0:T(8,128)(2,1)S(1)}, u32[]{:S(2)}, u32[]{:S(2)}) collective-permute-start(bf16[9,2,128,128]{3,2,1,0:T(8,128)(2,1)S(1)} %get-tuple-element.50), channel_id=1, source_target_pairs={{0,16},{16,32},{32,48},{48,64},{64,80},{80,96},{96,112},{112,128},... | collective-permute-start | bytes 1769480 | tf_op jit(solution)/shard_map/ppermute | solution.py:498
  35.4 22.4 %collective-permute-start.15 = (bf16[8,2,128,128]{3,2,1,0:T(8,128)(2,1)S(1)}, bf16[8,2,128,128]{3,2,1,0:T(8,128)(2,1)S(1)}, u32[]{:S(2)}, u32[]{:S(2)}) collective-permute-start(bf16[8,2,128,128]{3,2,1,0:T(8,128)(2,1)S(1)} %collective-permute-done.14), channel_id=1, source_target_pairs={{0,48},{16,64},{32,16},{48,32},{64,112},{80,128},{96,80},{112,96},... | collective-permute-start | bytes 1572872 | tf_op jit(solution)/shard_map/ppermute | solution.py:527
  39.1 4.4 %collective-permute-start.6 = (bf16[40,512]{1,0:T(8,128)(2,1)S(1)}, bf16[40,512]{1,0:T(8,128)(2,1)S(1)}, u32[]{:S(2)}, u32[]{:S(2)}) collective-permute-start(bf16[40,512]{1,0:T(8,128)(2,1)S(1)} %get-tuple-element.39.m0), channel_id=1, source_target_pairs={{0,2},{1,3},{2,4},{3,5},{4,6},{5,7},{6,0},{7,1},{8,10},{9,11},{10,... | collective-permute-start | bytes 122888 | tf_op jit(solution)/shard_map/ppermute | solution.py:489
  39.1 9.4 %collective-permute-start.7 = (bf16[40,512]{1,0:T(8,128)(2,1)S(1)}, bf16[40,512]{1,0:T(8,128)(2,1)S(1)}, u32[]{:S(2)}, u32[]{:S(2)}) collective-permute-start(bf16[40,512]{1,0:T(8,128)(2,1)S(1)} %get-tuple-element.39.m0), channel_id=1, source_target_pairs={{0,4},{1,5},{2,6},{3,7},{4,0},{5,1},{6,2},{7,3},{8,12},{9,13},{10,... | collective-permute-start | bytes 122888 | tf_op jit(solution)/shard_map/ppermute | solution.py:489
  42.3 7.3 %collective-permute-start.8 = (bf16[40,512]{1,0:T(8,128)(2,1)S(1)}, bf16[40,512]{1,0:T(8,128)(2,1)S(1)}, u32[]{:S(2)}, u32[]{:S(2)}) collective-permute-start(bf16[40,512]{1,0:T(8,128)(2,1)S(1)} %get-tuple-element.39.m0), channel_id=1, source_target_pairs={{0,6},{1,7},{2,0},{3,1},{4,2},{5,3},{6,4},{7,5},{8,14},{9,15},{10,... | collective-permute-start | bytes 122888 | tf_op jit(solution)/shard_map/ppermute | solution.py:489
  43.5 7.7 %collective-permute-start.9 = (bf16[40,512]{1,0:T(8,128)(2,1)S(1)}, bf16[40,512]{1,0:T(8,128)(2,1)S(1)}, u32[]{:S(2)}, u32[]{:S(2)}) collective-permute-start(bf16[40,512]{1,0:T(8,128)(2,1)S(1)} %get-tuple-element.39.m0), channel_id=1, source_target_pairs={{0,1},{1,0},{2,3},{3,2},{4,5},{5,4},{6,7},{7,6},{8,9},{9,8},{10,11... | collective-permute-start | bytes 122888 | tf_op jit(solution)/shard_map/ppermute | solution.py:492
  48.5 2.7 %collective-permute-start.10 = (bf16[40,512]{1,0:T(8,128)(2,1)S(1)}, bf16[40,512]{1,0:T(8,128)(2,1)S(1)}, u32[]{:S(2)}, u32[]{:S(2)}) collective-permute-start(bf16[40,512]{1,0:T(8,128)(2,1)S(1)} %collective-permute-done.6.m1), channel_id=1, source_target_pairs={{0,1},{1,0},{2,3},{3,2},{4,5},{5,4},{6,7},{7,6},{8,9},{9,8},{10,11... | collective-permute-start | bytes 122888 | tf_op jit(solution)/shard_map/ppermute | solution.py:492
  49.6 2.5 %collective-permute-start.11 = (bf16[40,512]{1,0:T(8,128)(2,1)S(1)}, bf16[40,512]{1,0:T(8,128)(2,1)S(1)}, u32[]{:S(2)}, u32[]{:S(2)}) collective-permute-start(bf16[40,512]{1,0:T(8,128)(2,1)S(1)} %collective-permute-done.7.m2), channel_id=1, source_target_pairs={{0,1},{1,0},{2,3},{3,2},{4,5},{5,4},{6,7},{7,6},{8,9},{9,8},{10,11... | collective-permute-start | bytes 122888 | tf_op jit(solution)/shard_map/ppermute | solution.py:492
  51.2 1.2 %collective-permute-start.12 = (bf16[40,512]{1,0:T(8,128)(2,1)S(1)}, bf16[40,512]{1,0:T(8,128)(2,1)S(1)}, u32[]{:S(2)}, u32[]{:S(2)}) collective-permute-start(bf16[40,512]{1,0:T(8,128)(2,1)S(1)} %collective-permute-done.8.m3), channel_id=1, source_target_pairs={{0,1},{1,0},{2,3},{3,2},{4,5},{5,4},{6,7},{7,6},{8,9},{9,8},{10,11... | collective-permute-start | bytes 122888 | tf_op jit(solution)/shard_map/ppermute | solution.py:492

commit v3 on v2

--- a/solution.py
+++ b/solution.py
@@ -17,11 +17,10 @@
 WIDTH = HEADS * HDIM
 D = 4096
 POOL = 128
-ROWS = REQ + MIG
-SENT = 16
+SENT = 2 * MIG
 GROUP = 16
 PAD = 8
-PARTS = (8, 15, 9)
+PARTS = (6, 14, 12)
 SCALE = HDIM ** (-0.5)
 F32 = jnp.float32
 BF16 = jnp.bfloat16
@@ -294,106 +293,101 @@
     )(keep, got, residual)
 
 
-def share_kernel(ids_in, lengths_in, own, a, b, c, share, moved, wide, sent, ids, lengths, small):
-    copies = started((ids_in, ids, small.at[0]), (lengths_in, lengths, small.at[1]))
+def share_kernel(own, a, b, c, share):
     total = own[...] + a[...].astype(F32) + b[...].astype(F32) + c[...].astype(F32)
-    rounded = total.astype(BF16)
-    share[...] = rounded
-    wide[...] = rounded.astype(F32)
-    for copy in copies:
-        copy.wait()
-    lane = lax.broadcasted_iota(jnp.int32, (1, WIDTH), 1)
-    for j in range(MIG):
-        r = ids[j]
-        sent[pl.ds(j, 1), :] = wide[pl.ds(r, 1), :]
-        last = lengths[r] - 1
-        sent[pl.ds(MIG + j, 1), :] = jnp.where(
-            lane < HDIM, last // PAGE, last % PAGE
-        ).astype(F32)
-    moved[...] = sent[...].astype(BF16)
-
-
-def share_sum(ids, lengths, own, a, b, c):
+    share[...] = total.astype(BF16)
+
+
+def share_sum(own, a, b, c):
     return pl.pallas_call(
         share_kernel,
-        out_shape=(
-            jax.ShapeDtypeStruct((REQ, WIDTH), BF16),
-            jax.ShapeDtypeStruct((SENT, WIDTH), BF16),
-        ),
-        in_specs=[HBM] * 2 + [VMEM] * 4,
-        out_specs=(VMEM, VMEM),
-        scratch_shapes=[
-            pltpu.VMEM((REQ, WIDTH), F32),
-            pltpu.VMEM((SENT, WIDTH), F32),
-            pltpu.SMEM((MIG,), jnp.int32),
-            pltpu.SMEM((REQ,), jnp.int32),
-            DMA((2,)),
-        ],
+        out_shape=jax.ShapeDtypeStruct((REQ, WIDTH), BF16),
+        in_specs=[VMEM] * 4,
+        out_specs=VMEM,
         compiler_params=pltpu.CompilerParams(vmem_limit_bytes=4 << 20),
         name="share_sum",
-    )(*in_hbm(ids, lengths), own, a, b, c)
-
-
-def join_kernel(share, arrived, moved_in, hidden, rows, last):
-    lead = leading()
-
-    @pl.when(lead)
-    def _():
-        hidden[...] = share[...]
-
-    @pl.when(jnp.logical_not(lead))
-    def _():
-        hidden[...] = arrived[...]
-
-    rows[:REQ, :] = arrived[...]
-    rows[REQ:, :] = moved_in[:MIG, :]
-    last[...] = moved_in[MIG:, : 2 * HDIM].astype(F32).astype(jnp.int32)
-
-
-def join(share, arrived, moved_in):
-    return pl.pallas_call(
-        join_kernel,
-        out_shape=(
-            jax.ShapeDtypeStruct((REQ, WIDTH), BF16),
-            jax.ShapeDtypeStruct((ROWS, WIDTH), BF16),
-            jax.ShapeDtypeStruct((MIG, 2 * HDIM), jnp.int32),
-        ),
-        in_specs=[VMEM] * 3,
-        out_specs=(VMEM,) * 3,
-        compiler_params=pltpu.CompilerParams(vmem_limit_bytes=4 << 20),
-        name="join",
-    )(share, arrived, moved_in)
-
-
-def second_kernel(
-    table_in, lengths_in, first_attn, m0, m1, m2, m3, n0, n1, n2, n3, gain, pages, weight,
-    kv_weight, attn, moved_kv,
-    qs, ks, vs, os, ss, table, lengths, small,
+    )(own, a, b, c)
+
+
+def project_kernel(
+    ids_in, lengths_in, share, m0, m1, m2, m3, n0, n1, n2, n3, gain, weight, kv_weight,
+    hidden, query, fresh, moved,
+    sent, ids, lengths, small,
 ):
     y, core = place()
-
-    @pl.when(jnp.logical_not(leading()))
-    def _():
-        copies = started((table_in, table, small.at[0]), (lengths_in, lengths, small.at[1]))
+    lead = leading()
+
+    @pl.when(lead)
+    def _():
+        hidden[...] = share[...]
+        query[...] = jnp.zeros_like(query)
+        fresh[...] = jnp.zeros_like(fresh)
+        moved[...] = jnp.zeros_like(moved)
+
+    @pl.when(jnp.logical_not(lead))
+    def _():
+        copies = started((ids_in, ids, small.at[0]), (lengths_in, lengths, small.at[1]))
+        hidden[...] = m0[...]
         blocks = []
-        square = jnp.zeros((ROWS, 1), F32)
+        square = jnp.zeros((REQ, 1), F32)
         for refs, c in (((m0, m1, m2, m3), core), ((n0, n1, n2, n3), 1 - core)):
             for k, ref in enumerate(refs):
                 x = ref[...].astype(F32)
                 square += jnp.sum(x * x, axis=-1, keepdims=True)
                 blocks.append((x, lax.rem(y + 4 - k, 4) * 2 + c))
         factor = lax.rsqrt(square * (1.0 / D) + 1e-05)
-        q = jnp.zeros((ROWS, WIDTH), F32)
-        kv = jnp.zeros((ROWS, 2 * HDIM), F32)
+        q = jnp.zeros((REQ, WIDTH), F32)
+        kv = jnp.zeros((REQ, 2 * HDIM), F32)
         for x, block in blocks:
             at = pl.ds(pl.multiple_of(block * WIDTH, WIDTH), WIDTH)
             x = (x * factor * gain[at].reshape(1, WIDTH)).astype(BF16)
             q += jnp.dot(x, weight[at, :], preferred_element_type=F32)
             kv += jnp.dot(x, kv_weight[at, :], preferred_element_type=F32)
-        q = q.astype(BF16).astype(F32)
-        kv = kv.astype(BF16).astype(F32)
-        moved_kv[...] = kv[REQ:]
-        spread(qs, ks, vs, q[:REQ], kv[:REQ, :HDIM], kv[:REQ, HDIM:])
+        query[...] = q.astype(BF16)
+        fresh[...] = kv.astype(BF16).astype(F32)
+        for copy in copies:
+            copy.wait()
+        lane = lax.broadcasted_iota(jnp.int32, (1, 2 * HDIM), 1)
+        for j in range(MIG):
+            r = ids[j]
+            sent[pl.ds(j, 1), :] = fresh[pl.ds(r, 1), :]
+            last = lengths[r] - 1
+            sent[pl.ds(MIG + j, 1), :] = jnp.where(
+                lane < HDIM, last // PAGE, last % PAGE
+            ).astype(F32)
+        moved[...] = sent[...].astype(BF16)
+
+
+def project(ids, lengths, share, mine, other, gain, weight, kv_weight):
+    return pl.pallas_call(
+        project_kernel,
+        out_shape=(
+            jax.ShapeDtypeStruct((REQ, WIDTH), BF16),
+            jax.ShapeDtypeStruct((REQ, WIDTH), BF16),
+            jax.ShapeDtypeStruct((REQ, 2 * HDIM), F32),
+            jax.ShapeDtypeStruct((SENT, 2 * HDIM), BF16),
+        ),
+        in_specs=[HBM] * 2 + [VMEM] * 12,
+        out_specs=(VMEM,) * 4,
+        scratch_shapes=[
+            pltpu.VMEM((SENT, 2 * HDIM), F32),
+            pltpu.SMEM((MIG,), jnp.int32),
+            pltpu.SMEM((REQ,), jnp.int32),
+            DMA((2,)),
+        ],
+        compiler_params=pltpu.CompilerParams(vmem_limit_bytes=8 << 20),
+        name="project",
+    )(*in_hbm(ids, lengths), share, *mine, *other, gain, *in_vmem(weight, kv_weight))
+
+
+def second_kernel(
+    table_in, lengths_in, first_attn, query, fresh, pages, attn,
+    qs, ks, vs, os, ss, table, lengths, small,
+):
+    @pl.when(jnp.logical_not(leading()))
+    def _():
+        copies = started((table_in, table, small.at[0]), (lengths_in, lengths, small.at[1]))
+        spread(qs, ks, vs, query[...].astype(F32), fresh[:, :HDIM], fresh[:, HDIM:])
         for copy in copies:
             copy.wait()
         for g in range(REQ // GROUP):
@@ -405,36 +399,43 @@
     @pl.when(leading())
     def _():
         attn[...] = first_attn[...]
-        moved_kv[...] = jnp.zeros_like(moved_kv)
-
-
-def second_layer(table, lengths, first_attn, mine, other, gain, pages, weight, kv_weight):
+
+
+def second_layer(table, lengths, first_attn, query, fresh, pages):
     return pl.pallas_call(
         second_kernel,
-        out_shape=(
-            jax.ShapeDtypeStruct((REQ, WIDTH), BF16),
-            jax.ShapeDtypeStruct((MIG, 2 * HDIM), F32),
+        out_shape=jax.ShapeDtypeStruct((REQ, WIDTH), BF16),
+        in_specs=[HBM] * 2 + [VMEM] * 4,
+        out_specs=VMEM,
+        scratch_shapes=ROW_SCRATCH + TABLE_SCRATCH + [DMA((2,))],
+        compiler_params=pltpu.CompilerParams(vmem_limit_bytes=8 << 20),
+        cost_estimate=pl.CostEstimate(
+            flops=1 << 30, bytes_accessed=16 << 20, transcendentals=1 << 20
         ),
-        in_specs=[HBM] * 2 + [VMEM] * 13,
-        out_specs=(VMEM, VMEM),
-        scratch_shapes=ROW_SCRATCH + TABLE_SCRATCH + [DMA((2,))],
-        compiler_params=pltpu.CompilerParams(vmem_limit_bytes=24 << 20),
         name="second_layer",
-    )(*in_hbm(table, lengths), first_attn, *mine, *other, gain, *in_vmem(pages, weight, kv_weight))
-
-
-def patch_kernel(last_in, rows, back, ahead, later, out, held, last, small, insem, outsem):
-    [last_copy] = started((last_in, last, small))
-    begin = [sum(PARTS[:i]) for i in range(3)]
-    copies = started(
-        *[
-            (ref, held.at[pl.ds(begin[i], PARTS[i])], insem.at[i])
-            for i, ref in enumerate((back, ahead, later))
-        ]
-    )
+    )(*in_hbm(table, lengths), first_attn, query, fresh, *in_vmem(pages))
+
+
+def patch_kernel(moved, back, ahead, soon, late, out, held, whole, last, rows, small, outsem):
+    whole[...] = moved[MIG:, :].astype(F32).astype(jnp.int32)
+    rows[...] = moved[:MIG, :].astype(F32)
+    [last_copy] = started((whole, last, small))
+    for i, (ref, index) in enumerate(page_slots((back, ahead))):
+        held[i] = ref[index]
+    turned = jnp.logical_and(leading(), lax.rem(lax.axis_index("inst"), 4) == 0)
+    first = PARTS[0] + PARTS[1]
+
+    @pl.when(turned)
+    def _():
+        for i in range(PARTS[2]):
+            held[first + i] = late[i]
+
+    @pl.when(jnp.logical_not(turned))
+    def _():
+        for i in range(PARTS[2]):
+            held[first + i] = soon[i]
+
     last_copy.wait()
-    for c in copies:
-        c.wait()
     lead = leading()
     leave = []
     for j in range(MIG):
@@ -455,23 +456,24 @@
         c.wait()
 
 
-def patch(last, rows, *parts):
+def patch(moved, *parts):
     shape = (MIG * PAGES,) + KV
     return pl.pallas_call(
         patch_kernel,
         out_shape=jax.ShapeDtypeStruct(shape, BF16),
-        in_specs=[HBM, VMEM] + [pl.BlockSpec(memory_space=pl.ANY)] * 3,
+        in_specs=[VMEM] * 5,
         out_specs=HBM,
         scratch_shapes=[
             pltpu.VMEM(shape, BF16),
+            pltpu.VMEM((MIG, 2 * HDIM), jnp.int32),
             pltpu.SMEM((MIG, 2 * HDIM), jnp.int32),
+            pltpu.VMEM((MIG, 2 * HDIM), F32),
             DMA,
-            DMA((3,)),
             DMA((MIG,)),
         ],
         compiler_params=pltpu.CompilerParams(vmem_limit_bytes=8 << 20),
         name="patch",
-    )(last, rows, *parts)
+    )(moved, *parts)
 
 
 def after(value, *others):
@@ -508,27 +510,34 @@
         table, lengths, query_rows, new_kv, pool, projection[0]
     )
     own, a, b, c = pair_sum(keep, to_twin(give), residual)
-    share, moved = share_sum(
-        migrate_ids, lengths, own, across(a, 1), across(b, 2), across(c, 3)
+    share = share_sum(own, across(a, 1), across(b, 2), across(c, 3))
+    across_z = [(2 * i, 2 * i + 1) for i in range(replicas)]
+    across_z += [(b, a) for a, b in across_z if a % 8 != 6]
+    arrived = lax.ppermute(share, ("inst", "section"), across_z)
+    back = lax.ppermute(after(back, share), "inst", down)
+    flat_kv = after(kv_weight, share).reshape(D, 2 * HDIM)
+    steps = [
+        (2 * i + k, 2 * ((i + 1) % replicas) + k) for i in range(replicas) for k in range(2)
+    ]
+    turns = [(a, b) for a, b in steps if a % 8 == 6]
+    later = after(later, share)
+    soon = lax.ppermute(later, ("inst", "section"), [p for p in steps if p not in turns])
+    arrived = after(arrived, flat_kv, ahead)
+    late = lax.ppermute(after(later, arrived), ("inst", "section"), turns)
+
+    mine = [arrived] + [across(arrived, k) for k in (1, 2, 3)]
+    other = [to_twin(after(arrived, mine[1]))] + [to_twin(m) for m in mine[1:]]
+    back = lax.ppermute(after(back, *mine), "inst", turn)
+    hidden, query, fresh, moved = project(
+        migrate_ids, lengths, share, mine, other, norm_gain, weight, flat_kv
     )
-    arrived = lax.ppermute(share, "section", [(0, 1), (1, 0)])
-    links = [(2 * i, 2 * ((i + 1) % replicas) + 1) for i in range(replicas)]
-    moved_in = lax.ppermute(
-        moved, ("inst", "section"), links + [(b, a) for a, b in links]
+    moved = lax.ppermute(
+        moved,
+        ("inst", "section"),
+        [(2 * i + 1, 2 * ((i + 1) % replicas) + 1) for i in range(replicas)],
     )
-    flat_kv = after(kv_weight, share).reshape(D, 2 * HDIM)
-    back = lax.ppermute(after(back, flat_kv), "inst", down)
-    arrived = after(arrived, flat_kv)
-    later = to_next(after(later, arrived, moved_in, ahead))
-
-    hidden, rows, last = join(share, arrived, moved_in)
-    mine = [rows] + [across(rows, k) for k in (1, 2, 3)]
-    other = [to_twin(after(rows, mine[1]))] + [to_twin(m) for m in mine[1:]]
-    back = lax.ppermute(after(back, rows), "inst", turn)
-    attn, second_rows = second_layer(
-        table, lengths, attn, mine, other, norm_gain, pool, weight, flat_kv
-    )
-    migrated = patch(last, second_rows, back, ahead, later)
+    attn = second_layer(table, lengths, attn, query, fresh, pool)
+    migrated = patch(moved, back, ahead, soon, late)
     return attn[None], hidden, migrated.reshape((1, MIG, PAGES) + KV)
 
 

time: 60.3 us -> 59.4 us (0.985)
  the two profiles are of different devices: /device:TPU:161 before, /device:TPU:24 now
where the time goes in v3:
time: 59.4 us; the launch traced here: 59.1 us
  starting transfers between devices  24.7 us (42%)
  waiting for transfers between devices  20.4 us (34%)
  Pallas kernels  12.8 us (22%)
  between operations  0.93 us (2%)
    ppermute x6, waiting for transfers between devices, across(): lax.ppermute(value, 'tensor', [(i, (i + 2 * by) % 8) for i in range(8)])  10.2 us
    pallas_call x1, Pallas kernels, first_layer(): pl.pallas_call(first_kernel, out_shape=(jax.ShapeDtypeStruct((REQ, WIDTH)...  6.43 us
    ppermute x1, starting transfers between devices, local(): back = lax.ppermute(after(back, *mine), 'inst', turn)  4.59 us
    ppermute x6, starting transfers between devices, across(): lax.ppermute(value, 'tensor', [(i, (i + 2 * by) % 8) for i in range(8)])  4.55 us
    ppermute x1, starting transfers between devices, local(): arrived = lax.ppermute(share, ('inst', 'section'), across_z)  3.87 us
    ppermute x1, waiting for transfers between devices, local(): late = lax.ppermute(after(later, arrived), ('inst', 'section'), turns)  3.5 us
    ppermute x1, starting transfers between devices, local(): back = lax.ppermute(back, 'inst', down)  3.14 us
    ppermute x5, waiting for transfers between devices, to_twin(): return lax.ppermute(value, 'tensor', [(i, i ^ 1) for i in range(8)])  3.08 us
  transfers between devices with their start and end apart: 19, of which 14 were waited for; matrix products, arithmetic and copies ran while one was open for 0% of the time, Pallas kernels for 13%

profile of v3, /device:TPU:24, one launch (start us, length us, event | category | flops | bytes accessed | tf_op | source)
XLA Modules:
  0.0 59.1 jit_solution(16023797460811345574)
XLA Ops:
  0.6 3.0 %gather_pages.1 = (bf16[6,2,128,128]{3,2,1,0:T(8,128)(2,1)S(1)}, bf16[14,2,128,128]{3,2,1,0:T(8,128)(2,1)S(1)}, bf16[12,2,128,128]{3,2,1,0:T(8,128)(2,1)S(1)}) custom-call(s32[4,32]{1,0:T(4,128)} %bitcast.17, s32[32]{0:T(128)} %lengths_in.7, s32[8]{0:T(128)} %ids_in.3, bf16[32,2,128]{2,1,0:T(2,128)(2,1)} %fresh_in.3, bf16[128,2,128,128]{3,2,1,0:T(8,128)(2,1)} %bitcast.9), custom_call_target="tpu_custom_call" | custom-call | tf_op jit(solution)/shard_map/gather_pages/pallas_call | solution.py:186
  3.6 1.5 %collective-permute-start.5 = (bf16[14,2,128,128]{3,2,1,0:T(8,128)(2,1)S(1)}, bf16[14,2,128,128]{3,2,1,0:T(8,128)(2,1)S(1)}, u32[]{:S(2)}, u32[]{:S(2)}) collective-permute-start(bf16[14,2,128,128]{3,2,1,0:T(8,128)(2,1)S(1)} %get-tuple-element.33), channel_id=1, source_target_pairs={{0,16},{16,32},{32,48},{48,64},{64,80},{80,96},{96,112},{112,128},... | collective-permute-start | bytes 2752520 | tf_op jit(solution)/shard_map/ppermute | solution.py:500
  5.1 3.1 %collective-permute-start.14 = (bf16[6,2,128,128]{3,2,1,0:T(8,128)(2,1)S(1)}, bf16[6,2,128,128]{3,2,1,0:T(8,128)(2,1)S(1)}, u32[]{:S(2)}, u32[]{:S(2)}) collective-permute-start(bf16[6,2,128,128]{3,2,1,0:T(8,128)(2,1)S(1)} %get-tuple-element.41), channel_id=1, source_target_pairs={{0,48},{16,0},{32,16},{48,32},{64,112},{80,64},{96,80},{112,96},{1... | collective-permute-start | bytes 1179656 | tf_op jit(solution)/shard_map/ppermute | solution.py:507
  8.2 6.4 %first_layer.1 = (bf16[32,512]{1,0:T(8,128)(2,1)S(1)}, f32[4,32,512]{2,1,0:T(8,128)S(1)}, f32[4,32,512]{2,1,0:T(8,128)S(1)}, bf16[4096,512]{1,0:T(8,128)(2,1)S(1)}) custom-call(s32[4,32]{1,0:T(4,128)} %bitcast.18, s32[32]{0:T(128)} %lengths_in.7, bf16[32,512]{1,0:T(8,128)(2,1)} %query_in.1, bf16[32,2,128]{2,1,0:T(2,128)(2,1)} %fresh_in.3, ...), custom_call_target="tpu_custom_call" | custom-call | tf_op jit(solution)/shard_map/first_layer/pallas_call | solution.py:254
  14.8 1.5 %collective-permute-done.got = f32[4,32,512]{2,1,0:T(8,128)S(1)} collective-permute-done((f32[4,32,512]{2,1,0:T(8,128)S(1)}, f32[4,32,512]{2,1,0:T(8,128)S(1)}, u32[]{:S(2)}, u32[]{:S(2)}) %collective-permute-start) | collective-permute-done | bytes 262176 | tf_op jit(solution)/shard_map/ppermute | solution.py:494
  16.6 2.6 %collective-permute-start.2 = (bf16[32,512]{1,0:T(8,128)(2,1)S(1)}, bf16[32,512]{1,0:T(8,128)(2,1)S(1)}, u32[]{:S(2)}, u32[]{:S(2)}) collective-permute-start(bf16[32,512]{1,0:T(8,128)(2,1)S(1)} %get-tuple-element.30), channel_id=1, source_target_pairs={{0,4},{1,5},{2,6},{3,7},{4,0},{5,1},{6,2},{7,3},{8,12},{9,13},{10,... | collective-permute-start | bytes 98312 | tf_op jit(solution)/shard_map/ppermute | solution.py:491
  19.2 1.1 %collective-permute-done.1.a = bf16[32,512]{1,0:T(8,128)(2,1)S(1)} collective-permute-done((bf16[32,512]{1,0:T(8,128)(2,1)S(1)}, bf16[32,512]{1,0:T(8,128)(2,1)S(1)}, u32[]{:S(2)}, u32[]{:S(2)}) %collective-permute-start.1) | collective-permute-done | bytes 32800 | tf_op jit(solution)/shard_map/ppermute | solution.py:491
  20.3 1.7 %collective-permute-done.2.b = bf16[32,512]{1,0:T(8,128)(2,1)S(1)} collective-permute-done((bf16[32,512]{1,0:T(8,128)(2,1)S(1)}, bf16[32,512]{1,0:T(8,128)(2,1)S(1)}, u32[]{:S(2)}, u32[]{:S(2)}) %collective-permute-start.2) | collective-permute-done | bytes 32800 | tf_op jit(solution)/shard_map/ppermute | solution.py:491
  22.1 2.3 %collective-permute-done.3.c = bf16[32,512]{1,0:T(8,128)(2,1)S(1)} collective-permute-done((bf16[32,512]{1,0:T(8,128)(2,1)S(1)}, bf16[32,512]{1,0:T(8,128)(2,1)S(1)}, u32[]{:S(2)}, u32[]{:S(2)}) %collective-permute-start.3) | collective-permute-done | bytes 32800 | tf_op jit(solution)/shard_map/ppermute | solution.py:491
  24.4 3.9 %collective-permute-start.4 = (bf16[32,512]{1,0:T(8,128)(2,1)S(1)}, bf16[32,512]{1,0:T(8,128)(2,1)S(1)}, u32[]{:S(2)}, u32[]{:S(2)}) collective-permute-start(bf16[32,512]{1,0:T(8,128)(2,1)S(1)} %share_sum.1.share), channel_id=1, source_target_pairs={{0,8},{16,24},{32,40},{48,56},{64,72},{80,88},{96,104},{112,120},{... | collective-permute-start | bytes 98312 | tf_op jit(solution)/shard_map/ppermute | solution.py:516
  28.3 1.3 %collective-permute-start.15 = (bf16[6,2,128,128]{3,2,1,0:T(8,128)(2,1)S(1)}, bf16[6,2,128,128]{3,2,1,0:T(8,128)(2,1)S(1)}, u32[]{:S(2)}, u32[]{:S(2)}) collective-permute-start(bf16[6,2,128,128]{3,2,1,0:T(8,128)(2,1)S(1)} %collective-permute-done.14), channel_id=1, source_target_pairs={{0,48},{16,0},{32,16},{48,32},{64,112},{80,64},{96,80},{112,96},{1... | collective-permute-start | bytes 1179656 | tf_op jit(solution)/shard_map/ppermute | solution.py:517
  29.8 2.8 %collective-permute-start.17 = (bf16[12,2,128,128]{3,2,1,0:T(8,128)(2,1)S(1)}, bf16[12,2,128,128]{3,2,1,0:T(8,128)(2,1)S(1)}, u32[]{:S(2)}, u32[]{:S(2)}) collective-permute-start(bf16[12,2,128,128]{3,2,1,0:T(8,128)(2,1)S(1)} %get-tuple-element.46), channel_id=1, source_target_pairs={{0,16},{8,24},{16,32},{24,40},{32,48},{40,56},{56,72},{64,80},{72,... | collective-permute-start | bytes 2359304 | tf_op jit(solution)/shard_map/ppermute | solution.py:524
  32.6 1.5 %collective-permute-done.4.m0 = bf16[32,512]{1,0:T(8,128)(2,1)S(1)} collective-permute-done((bf16[32,512]{1,0:T(8,128)(2,1)S(1)}, bf16[32,512]{1,0:T(8,128)(2,1)S(1)}, u32[]{:S(2)}, u32[]{:S(2)}) %collective-permute-start.4) | collective-permute-done | bytes 32800 | tf_op jit(solution)/shard_map/ppermute | solution.py:516
  34.1 1.3 %collective-permute-start.18 = (bf16[12,2,128,128]{3,2,1,0:T(8,128)(2,1)S(1)}, bf16[12,2,128,128]{3,2,1,0:T(8,128)(2,1)S(1)}, u32[]{:S(2)}, u32[]{:S(2)}) collective-permute-start(bf16[12,2,128,128]{3,2,1,0:T(8,128)(2,1)S(1)} %get-tuple-element.46), channel_id=1, source_target_pairs={{48,64},{112,128},{176,192},{240,0},{49,65},{113,129},{177,193},{2... | collective-permute-start | bytes 2359304 | tf_op jit(solution)/shard_map/ppermute | solution.py:526
  35.4 0.8 %collective-permute-start.6 = (bf16[32,512]{1,0:T(8,128)(2,1)S(1)}, bf16[32,512]{1,0:T(8,128)(2,1)S(1)}, u32[]{:S(2)}, u32[]{:S(2)}) collective-permute-start(bf16[32,512]{1,0:T(8,128)(2,1)S(1)} %collective-permute-done.4.m0), channel_id=1, source_target_pairs={{0,2},{1,3},{2,4},{3,5},{4,6},{5,7},{6,0},{7,1},{8,10},{9,11},{10,... | collective-permute-start | bytes 98312 | tf_op jit(solution)/shard_map/ppermute | solution.py:491
  36.1 0.9 %collective-permute-start.7 = (bf16[32,512]{1,0:T(8,128)(2,1)S(1)}, bf16[32,512]{1,0:T(8,128)(2,1)S(1)}, u32[]{:S(2)}, u32[]{:S(2)}) collective-permute-start(bf16[32,512]{1,0:T(8,128)(2,1)S(1)} %collective-permute-done.4.m0), channel_id=1, source_target_pairs={{0,4},{1,5},{2,6},{3,7},{4,0},{5,1},{6,2},{7,3},{8,12},{9,13},{10,... | collective-permute-start | bytes 98312 | tf_op jit(solution)/shard_map/ppermute | solution.py:491
  37.0 0.8 %collective-permute-done.15 = bf16[6,2,128,128]{3,2,1,0:T(8,128)(2,1)S(1)} collective-permute-done((bf16[6,2,128,128]{3,2,1,0:T(8,128)(2,1)S(1)}, bf16[6,2,128,128]{3,2,1,0:T(8,128)(2,1)S(1)}, u32[]{:S(2)}, u32[]{:S(2)}) %collective-permute-start.15) | collective-permute-done | bytes 393248 | tf_op jit(solution)/shard_map/ppermute | solution.py:517
  37.8 1.6 %collective-permute-done.6.m1 = bf16[32,512]{1,0:T(8,128)(2,1)S(1)} collective-permute-done((bf16[32,512]{1,0:T(8,128)(2,1)S(1)}, bf16[32,512]{1,0:T(8,128)(2,1)S(1)}, u32[]{:S(2)}, u32[]{:S(2)}) %collective-permute-start.6) | collective-permute-done | bytes 32800 | tf_op jit(solution)/shard_map/ppermute | solution.py:491
  39.4 2.2 %collective-permute-done.7.m2 = bf16[32,512]{1,0:T(8,128)(2,1)S(1)} collective-permute-done((bf16[32,512]{1,0:T(8,128)(2,1)S(1)}, bf16[32,512]{1,0:T(8,128)(2,1)S(1)}, u32[]{:S(2)}, u32[]{:S(2)}) %collective-permute-start.7) | collective-permute-done | bytes 32800 | tf_op jit(solution)/shard_map/ppermute | solution.py:491
  41.6 1.4 %collective-permute-done.8.m3 = bf16[32,512]{1,0:T(8,128)(2,1)S(1)} collective-permute-done((bf16[32,512]{1,0:T(8,128)(2,1)S(1)}, bf16[32,512]{1,0:T(8,128)(2,1)S(1)}, u32[]{:S(2)}, u32[]{:S(2)}) %collective-permute-start.8) | collective-permute-done | bytes 32800 | tf_op jit(solution)/shard_map/ppermute | solution.py:491
  42.9 4.6 %collective-permute-start.16 = (bf16[6,2,128,128]{3,2,1,0:T(8,128)(2,1)S(1)}, bf16[6,2,128,128]{3,2,1,0:T(8,128)(2,1)S(1)}, u32[]{:S(2)}, u32[]{:S(2)}) collective-permute-start(bf16[6,2,128,128]{3,2,1,0:T(8,128)(2,1)S(1)} %collective-permute-done.15), channel_id=1, source_target_pairs={{0,48},{16,64},{32,16},{48,32},{64,112},{80,128},{96,80},{112,96},... | collective-permute-start | bytes 1179656 | tf_op jit(solution)/shard_map/ppermute | solution.py:530
  52.1 1.3 %collective-permute-done.16.back = bf16[6,2,128,128]{3,2,1,0:T(8,128)(2,1)S(1)} collective-permute-done((bf16[6,2,128,128]{3,2,1,0:T(8,128)(2,1)S(1)}, bf16[6,2,128,128]{3,2,1,0:T(8,128)(2,1)S(1)}, u32[]{:S(2)}, u32[]{:S(2)}) %collective-permute-start.16) | collective-permute-done | bytes 393248 | tf_op jit(solution)/shard_map/ppermute | solution.py:530
  53.4 3.5 %collective-permute-done.18.late = bf16[12,2,128,128]{3,2,1,0:T(8,128)(2,1)S(1)} collective-permute-done((bf16[12,2,128,128]{3,2,1,0:T(8,128)(2,1)S(1)}, bf16[12,2,128,128]{3,2,1,0:T(8,128)(2,1)S(1)}, u32[]{:S(2)}, u32[]{:S(2)}) %collective-permute-start.18) | collective-permute-done | bytes 786464 | tf_op jit(solution)/shard_map/ppermute | solution.py:526
  56.9 2.1 %patch.1 = bf16[32,2,128,128]{3,2,1,0:T(8,128)(2,1)} custom-call(bf16[16,256]{1,0:T(8,128)(2,1)S(1)} %collective-permute-done.13.moved, bf16[6,2,128,128]{3,2,1,0:T(8,128)(2,1)S(1)} %collective-permute-done.16.back, bf16[14,2,128,128]{3,2,1,0:T(8,128)(2,1)S(1)} %collective-permute-done.5.ahead, bf16[12,2,128,128]{3,2,1,0:T(8,128)(2,1)S(1)} %collective-permute-done.17.soon, ...), custom_call_target="tpu_custom_call" | custom-call | tf_op jit(solution)/shard_map/patch/pallas_call | solution.py:461
  (30 shorter events, 5.3 us)
Async XLA Ops:
  0.6 7.6 %copy-start = (bf16[1,128,2,128,128]{4,3,2,1,0:T(8,128)(2,1)S(1)}, bf16[1,128,2,128,128]{4,3,2,1,0:T(8,128)(2,1)}, u32[]{:S(2)}) copy-start(bf16[1,128,2,128,128]{4,3,2,1,0:T(8,128)(2,1)} %param.13) | copy-start | bytes 25165828
  3.6 30.5 %collective-permute-start.5 = (bf16[14,2,128,128]{3,2,1,0:T(8,128)(2,1)S(1)}, bf16[14,2,128,128]{3,2,1,0:T(8,128)(2,1)S(1)}, u32[]{:S(2)}, u32[]{:S(2)}) collective-permute-start(bf16[14,2,128,128]{3,2,1,0:T(8,128)(2,1)S(1)} %get-tuple-element.33), channel_id=1, source_target_pairs={{0,16},{16,32},{32,48},{48,64},{64,80},{80,96},{96,112},{112,128},... | collective-permute-start | bytes 2752520 | tf_op jit(solution)/shard_map/ppermute | solution.py:500
  5.1 23.2 %collective-permute-start.14 = (bf16[6,2,128,128]{3,2,1,0:T(8,128)(2,1)S(1)}, bf16[6,2,128,128]{3,2,1,0:T(8,128)(2,1)S(1)}, u32[]{:S(2)}, u32[]{:S(2)}) collective-permute-start(bf16[6,2,128,128]{3,2,1,0:T(8,128)(2,1)S(1)} %get-tuple-element.41), channel_id=1, source_target_pairs={{0,48},{16,0},{32,16},{48,32},{64,112},{80,64},{96,80},{112,96},{1... | collective-permute-start | bytes 1179656 | tf_op jit(solution)/shard_map/ppermute | solution.py:507
  8.2 8.1 %copy-start.1 = (bf16[32,512]{1,0:T(8,128)(2,1)S(1)}, bf16[32,512]{1,0:T(8,128)(2,1)}, u32[]{:S(2)}) copy-start(bf16[32,512]{1,0:T(8,128)(2,1)} %residual.1) | copy-start | bytes 98308
  8.2 21.3 %copy-start.3 = (bf16[4096,2,128]{2,1,0:T(2,128)(2,1)S(1)}, bf16[4096,2,128]{2,1,0:T(2,128)(2,1)}, u32[]{:S(2)}) copy-start(bf16[4096,2,128]{2,1,0:T(2,128)(2,1)} %param.18) | copy-start | bytes 6291460
  14.7 35.4 %copy-start.2 = (f32[4096]{0:T(1024)S(1)}, f32[4096]{0:T(1024)}, u32[]{:S(2)}) copy-start(f32[4096]{0:T(1024)} %gain.1) | copy-start | bytes 49156
  14.7 1.6 %collective-permute-start = (f32[4,32,512]{2,1,0:T(8,128)S(1)}, f32[4,32,512]{2,1,0:T(8,128)S(1)}, u32[]{:S(2)}, u32[]{:S(2)}) collective-permute-start(f32[4,32,512]{2,1,0:T(8,128)S(1)} %get-tuple-element.27), channel_id=1, source_target_pairs={{0,1},{1,0},{2,3},{3,2},{4,5},{5,4},{6,7},{7,6},{8,9},{9,8},{10,11... | collective-permute-start | bytes 786440 | tf_op jit(solution)/shard_map/ppermute | solution.py:494
  16.3 4.0 %collective-permute-start.1 = (bf16[32,512]{1,0:T(8,128)(2,1)S(1)}, bf16[32,512]{1,0:T(8,128)(2,1)S(1)}, u32[]{:S(2)}, u32[]{:S(2)}) collective-permute-start(bf16[32,512]{1,0:T(8,128)(2,1)S(1)} %get-tuple-element.29), channel_id=1, source_target_pairs={{0,2},{1,3},{2,4},{3,5},{4,6},{5,7},{6,0},{7,1},{8,10},{9,11},{10,... | collective-permute-start | bytes 98312 | tf_op jit(solution)/shard_map/ppermute | solution.py:491
  16.6 5.4 %collective-permute-start.2 = (bf16[32,512]{1,0:T(8,128)(2,1)S(1)}, bf16[32,512]{1,0:T(8,128)(2,1)S(1)}, u32[]{:S(2)}, u32[]{:S(2)}) collective-permute-start(bf16[32,512]{1,0:T(8,128)(2,1)S(1)} %get-tuple-element.30), channel_id=1, source_target_pairs={{0,4},{1,5},{2,6},{3,7},{4,0},{5,1},{6,2},{7,3},{8,12},{9,13},{10,... | collective-permute-start | bytes 98312 | tf_op jit(solution)/shard_map/ppermute | solution.py:491
  19.2 5.1 %collective-permute-start.3 = (bf16[32,512]{1,0:T(8,128)(2,1)S(1)}, bf16[32,512]{1,0:T(8,128)(2,1)S(1)}, u32[]{:S(2)}, u32[]{:S(2)}) collective-permute-start(bf16[32,512]{1,0:T(8,128)(2,1)S(1)} %get-tuple-element.31), channel_id=1, source_target_pairs={{0,6},{1,7},{2,0},{3,1},{4,2},{5,3},{6,4},{7,5},{8,14},{9,15},{10,... | collective-permute-start | bytes 98312 | tf_op jit(solution)/shard_map/ppermute | solution.py:491
  24.4 9.7 %collective-permute-start.4 = (bf16[32,512]{1,0:T(8,128)(2,1)S(1)}, bf16[32,512]{1,0:T(8,128)(2,1)S(1)}, u32[]{:S(2)}, u32[]{:S(2)}) collective-permute-start(bf16[32,512]{1,0:T(8,128)(2,1)S(1)} %share_sum.1.share), channel_id=1, source_target_pairs={{0,8},{16,24},{32,40},{48,56},{64,72},{80,88},{96,104},{112,120},{... | collective-permute-start | bytes 98312 | tf_op jit(solution)/shard_map/ppermute | solution.py:516
  28.3 9.5 %collective-permute-start.15 = (bf16[6,2,128,128]{3,2,1,0:T(8,128)(2,1)S(1)}, bf16[6,2,128,128]{3,2,1,0:T(8,128)(2,1)S(1)}, u32[]{:S(2)}, u32[]{:S(2)}) collective-permute-start(bf16[6,2,128,128]{3,2,1,0:T(8,128)(2,1)S(1)} %collective-permute-done.14), channel_id=1, source_target_pairs={{0,48},{16,0},{32,16},{48,32},{64,112},{80,64},{96,80},{112,96},{1... | collective-permute-start | bytes 1179656 | tf_op jit(solution)/shard_map/ppermute | solution.py:517
  29.8 22.3 %collective-permute-start.17 = (bf16[12,2,128,128]{3,2,1,0:T(8,128)(2,1)S(1)}, bf16[12,2,128,128]{3,2,1,0:T(8,128)(2,1)S(1)}, u32[]{:S(2)}, u32[]{:S(2)}) collective-permute-start(bf16[12,2,128,128]{3,2,1,0:T(8,128)(2,1)S(1)} %get-tuple-element.46), channel_id=1, source_target_pairs={{0,16},{8,24},{16,32},{24,40},{32,48},{40,56},{56,72},{64,80},{72,... | collective-permute-start | bytes 2359304 | tf_op jit(solution)/shard_map/ppermute | solution.py:524
  34.1 22.8 %collective-permute-start.18 = (bf16[12,2,128,128]{3,2,1,0:T(8,128)(2,1)S(1)}, bf16[12,2,128,128]{3,2,1,0:T(8,128)(2,1)S(1)}, u32[]{:S(2)}, u32[]{:S(2)}) collective-permute-start(bf16[12,2,128,128]{3,2,1,0:T(8,128)(2,1)S(1)} %get-tuple-element.46), channel_id=1, source_target_pairs={{48,64},{112,128},{176,192},{240,0},{49,65},{113,129},{177,193},{2... | collective-permute-start | bytes 2359304 | tf_op jit(solution)/shard_map/ppermute | solution.py:526
  35.4 4.0 %collective-permute-start.6 = (bf16[32,512]{1,0:T(8,128)(2,1)S(1)}, bf16[32,512]{1,0:T(8,128)(2,1)S(1)}, u32[]{:S(2)}, u32[]{:S(2)}) collective-permute-start(bf16[32,512]{1,0:T(8,128)(2,1)S(1)} %collective-permute-done.4.m0), channel_id=1, source_target_pairs={{0,2},{1,3},{2,4},{3,5},{4,6},{5,7},{6,0},{7,1},{8,10},{9,11},{10,... | collective-permute-start | bytes 98312 | tf_op jit(solution)/shard_map/ppermute | solution.py:491
  36.1 5.4 %collective-permute-start.7 = (bf16[32,512]{1,0:T(8,128)(2,1)S(1)}, bf16[32,512]{1,0:T(8,128)(2,1)S(1)}, u32[]{:S(2)}, u32[]{:S(2)}) collective-permute-start(bf16[32,512]{1,0:T(8,128)(2,1)S(1)} %collective-permute-done.4.m0), channel_id=1, source_target_pairs={{0,4},{1,5},{2,6},{3,7},{4,0},{5,1},{6,2},{7,3},{8,12},{9,13},{10,... | collective-permute-start | bytes 98312 | tf_op jit(solution)/shard_map/ppermute | solution.py:491
  37.8 5.1 %collective-permute-start.8 = (bf16[32,512]{1,0:T(8,128)(2,1)S(1)}, bf16[32,512]{1,0:T(8,128)(2,1)S(1)}, u32[]{:S(2)}, u32[]{:S(2)}) collective-permute-start(bf16[32,512]{1,0:T(8,128)(2,1)S(1)} %collective-permute-done.4.m0), channel_id=1, source_target_pairs={{0,6},{1,7},{2,0},{3,1},{4,2},{5,3},{6,4},{7,5},{8,14},{9,15},{10,... | collective-permute-start | bytes 98312 | tf_op jit(solution)/shard_map/ppermute | solution.py:491
  42.9 10.5 %collective-permute-start.16 = (bf16[6,2,128,128]{3,2,1,0:T(8,128)(2,1)S(1)}, bf16[6,2,128,128]{3,2,1,0:T(8,128)(2,1)S(1)}, u32[]{:S(2)}, u32[]{:S(2)}) collective-permute-start(bf16[6,2,128,128]{3,2,1,0:T(8,128)(2,1)S(1)} %collective-permute-done.15), channel_id=1, source_target_pairs={{0,48},{16,64},{32,16},{48,32},{64,112},{80,128},{96,80},{112,96},... | collective-permute-start | bytes 1179656 | tf_op jit(solution)/shard_map/ppermute | solution.py:530
  47.5 1.2 %collective-permute-start.9 = (bf16[32,512]{1,0:T(8,128)(2,1)S(1)}, bf16[32,512]{1,0:T(8,128)(2,1)S(1)}, u32[]{:S(2)}, u32[]{:S(2)}) collective-permute-start(bf16[32,512]{1,0:T(8,128)(2,1)S(1)} %collective-permute-done.4.m0), channel_id=1, source_target_pairs={{0,1},{1,0},{2,3},{3,2},{4,5},{5,4},{6,7},{7,6},{8,9},{9,8},{10,11... | collective-permute-start | bytes 98312 | tf_op jit(solution)/shard_map/ppermute | solution.py:494
  47.5 1.4 %collective-permute-start.10 = (bf16[32,512]{1,0:T(8,128)(2,1)S(1)}, bf16[32,512]{1,0:T(8,128)(2,1)S(1)}, u32[]{:S(2)}, u32[]{:S(2)}) collective-permute-start(bf16[32,512]{1,0:T(8,128)(2,1)S(1)} %collective-permute-done.6.m1), channel_id=1, source_target_pairs={{0,1},{1,0},{2,3},{3,2},{4,5},{5,4},{6,7},{7,6},{8,9},{9,8},{10,11... | collective-permute-start | bytes 98312 | tf_op jit(solution)/shard_map/ppermute | solution.py:494
  48.7 1.2 %collective-permute-start.11 = (bf16[32,512]{1,0:T(8,128)(2,1)S(1)}, bf16[32,512]{1,0:T(8,128)(2,1)S(1)}, u32[]{:S(2)}, u32[]{:S(2)}) collective-permute-start(bf16[32,512]{1,0:T(8,128)(2,1)S(1)} %collective-permute-done.7.m2), channel_id=1, source_target_pairs={{0,1},{1,0},{2,3},{3,2},{4,5},{5,4},{6,7},{7,6},{8,9},{9,8},{10,11... | collective-permute-start | bytes 98312 | tf_op jit(solution)/shard_map/ppermute | solution.py:494
  48.9 1.2 %collective-permute-start.12 = (bf16[32,512]{1,0:T(8,128)(2,1)S(1)}, bf16[32,512]{1,0:T(8,128)(2,1)S(1)}, u32[]{:S(2)}, u32[]{:S(2)}) collective-permute-start(bf16[32,512]{1,0:T(8,128)(2,1)S(1)} %collective-permute-done.8.m3), channel_id=1, source_target_pairs={{0,1},{1,0},{2,3},{3,2},{4,5},{5,4},{6,7},{7,6},{8,9},{9,8},{10,11... | collective-permute-start | bytes 98312 | tf_op jit(solution)/shard_map/ppermute | solution.py:494
  50.8 1.3 %collective-permute-start.13 = (bf16[16,256]{1,0:T(8,128)(2,1)S(1)}, bf16[16,256]{1,0:T(8,128)(2,1)S(1)}, u32[]{:S(2)}, u32[]{:S(2)}) collective-permute-start(bf16[16,256]{1,0:T(8,128)(2,1)S(1)} %get-tuple-element.40), channel_id=1, source_target_pairs={{8,24},{24,40},{40,56},{56,72},{72,88},{88,104},{104,120},{120,136... | collective-permute-start | bytes 24584 | tf_op jit(solution)/shard_map/ppermute | solution.py:534

commit v4 on v3

--- a/solution.py
+++ b/solution.py
@@ -522,8 +522,8 @@
     turns = [(a, b) for a, b in steps if a % 8 == 6]
     later = after(later, share)
     soon = lax.ppermute(later, ("inst", "section"), [p for p in steps if p not in turns])
+    late = lax.ppermute(after(later, arrived), ("inst", "section"), turns)
     arrived = after(arrived, flat_kv, ahead)
-    late = lax.ppermute(after(later, arrived), ("inst", "section"), turns)
 
     mine = [arrived] + [across(arrived, k) for k in (1, 2, 3)]
     other = [to_twin(after(arrived, mine[1]))] + [to_twin(m) for m in mine[1:]]

time: 59.4 us -> 59.4 us (level)
    ppermute x1, waiting for transfers between devices: 1.29 us -> 0.01 us  [local(): back = lax.ppermute(after(back, *mine), 'inst', turn)]
    ppermute x1, waiting for transfers between devices: 3.5 us -> 4.62 us  [local(): late = lax.ppermute(after(later, arrived), ('inst', 'section'), turns)]
  transfers between devices with their start and end apart: 19 -> 19, of which waited for: 14 -> 13; matrix products, arithmetic and copies ran while one was open for 0% -> 0% of each run, Pallas kernels for 13% -> 13%
where the time goes in v4:
time: 59.4 us; the launch traced here: 59.2 us
  starting transfers between devices  25 us (42%)
  waiting for transfers between devices  20.2 us (34%)
  Pallas kernels  12.8 us (22%)
  between operations  0.95 us (2%)
    ppermute x6, waiting for transfers between devices, across(): lax.ppermute(value, 'tensor', [(i, (i + 2 * by) % 8) for i in range(8)])  10.2 us
    pallas_call x1, Pallas kernels, first_layer(): pl.pallas_call(first_kernel, out_shape=(jax.ShapeDtypeStruct((REQ, WIDTH)...  6.43 us
    ppermute x1, starting transfers between devices, local(): back = lax.ppermute(after(back, *mine), 'inst', turn)  4.76 us
    ppermute x1, waiting for transfers between devices, local(): late = lax.ppermute(after(later, arrived), ('inst', 'section'), turns)  4.62 us
    ppermute x6, starting transfers between devices, across(): lax.ppermute(value, 'tensor', [(i, (i + 2 * by) % 8) for i in range(8)])  4.55 us
    ppermute x1, starting transfers between devices, local(): arrived = lax.ppermute(share, ('inst', 'section'), across_z)  3.87 us
    ppermute x1, starting transfers between devices, local(): back = lax.ppermute(back, 'inst', down)  3.15 us
    ppermute x5, waiting for transfers between devices, to_twin(): return lax.ppermute(value, 'tensor', [(i, i ^ 1) for i in range(8)])  3.08 us
  transfers between devices with their start and end apart: 19, of which 13 were waited for; matrix products, arithmetic and copies ran while one was open for 0% of the time, Pallas kernels for 13%

profile of v4, /device:TPU:24, one launch (start us, length us, event | category | flops | bytes accessed | tf_op | source)
XLA Modules:
  0.0 59.2 jit_solution(12286172064093482455)
XLA Ops:
  0.6 2.9 %gather_pages.1 = (bf16[6,2,128,128]{3,2,1,0:T(8,128)(2,1)S(1)}, bf16[14,2,128,128]{3,2,1,0:T(8,128)(2,1)S(1)}, bf16[12,2,128,128]{3,2,1,0:T(8,128)(2,1)S(1)}) custom-call(s32[4,32]{1,0:T(4,128)} %bitcast.17, s32[32]{0:T(128)} %lengths_in.7, s32[8]{0:T(128)} %ids_in.3, bf16[32,2,128]{2,1,0:T(2,128)(2,1)} %fresh_in.3, bf16[128,2,128,128]{3,2,1,0:T(8,128)(2,1)} %bitcast.9), custom_call_target="tpu_custom_call" | custom-call | tf_op jit(solution)/shard_map/gather_pages/pallas_call | solution.py:186
  3.6 1.6 %collective-permute-start.5 = (bf16[14,2,128,128]{3,2,1,0:T(8,128)(2,1)S(1)}, bf16[14,2,128,128]{3,2,1,0:T(8,128)(2,1)S(1)}, u32[]{:S(2)}, u32[]{:S(2)}) collective-permute-start(bf16[14,2,128,128]{3,2,1,0:T(8,128)(2,1)S(1)} %get-tuple-element.33), channel_id=1, source_target_pairs={{0,16},{16,32},{32,48},{48,64},{64,80},{80,96},{96,112},{112,128},... | collective-permute-start | bytes 2752520 | tf_op jit(solution)/shard_map/ppermute | solution.py:500
  5.2 3.1 %collective-permute-start.14 = (bf16[6,2,128,128]{3,2,1,0:T(8,128)(2,1)S(1)}, bf16[6,2,128,128]{3,2,1,0:T(8,128)(2,1)S(1)}, u32[]{:S(2)}, u32[]{:S(2)}) collective-permute-start(bf16[6,2,128,128]{3,2,1,0:T(8,128)(2,1)S(1)} %get-tuple-element.41), channel_id=1, source_target_pairs={{0,48},{16,0},{32,16},{48,32},{64,112},{80,64},{96,80},{112,96},{1... | collective-permute-start | bytes 1179656 | tf_op jit(solution)/shard_map/ppermute | solution.py:507
  8.3 6.4 %first_layer.1 = (bf16[32,512]{1,0:T(8,128)(2,1)S(1)}, f32[4,32,512]{2,1,0:T(8,128)S(1)}, f32[4,32,512]{2,1,0:T(8,128)S(1)}, bf16[4096,512]{1,0:T(8,128)(2,1)S(1)}) custom-call(s32[4,32]{1,0:T(4,128)} %bitcast.18, s32[32]{0:T(128)} %lengths_in.7, bf16[32,512]{1,0:T(8,128)(2,1)} %query_in.1, bf16[32,2,128]{2,1,0:T(2,128)(2,1)} %fresh_in.3, ...), custom_call_target="tpu_custom_call" | custom-call | tf_op jit(solution)/shard_map/first_layer/pallas_call | solution.py:254
  14.9 1.5 %collective-permute-done.got = f32[4,32,512]{2,1,0:T(8,128)S(1)} collective-permute-done((f32[4,32,512]{2,1,0:T(8,128)S(1)}, f32[4,32,512]{2,1,0:T(8,128)S(1)}, u32[]{:S(2)}, u32[]{:S(2)}) %collective-permute-start) | collective-permute-done | bytes 262176 | tf_op jit(solution)/shard_map/ppermute | solution.py:494
  16.7 2.6 %collective-permute-start.2 = (bf16[32,512]{1,0:T(8,128)(2,1)S(1)}, bf16[32,512]{1,0:T(8,128)(2,1)S(1)}, u32[]{:S(2)}, u32[]{:S(2)}) collective-permute-start(bf16[32,512]{1,0:T(8,128)(2,1)S(1)} %get-tuple-element.30), channel_id=1, source_target_pairs={{0,4},{1,5},{2,6},{3,7},{4,0},{5,1},{6,2},{7,3},{8,12},{9,13},{10,... | collective-permute-start | bytes 98312 | tf_op jit(solution)/shard_map/ppermute | solution.py:491
  19.3 1.1 %collective-permute-done.1.a = bf16[32,512]{1,0:T(8,128)(2,1)S(1)} collective-permute-done((bf16[32,512]{1,0:T(8,128)(2,1)S(1)}, bf16[32,512]{1,0:T(8,128)(2,1)S(1)}, u32[]{:S(2)}, u32[]{:S(2)}) %collective-permute-start.1) | collective-permute-done | bytes 32800 | tf_op jit(solution)/shard_map/ppermute | solution.py:491
  20.4 1.7 %collective-permute-done.2.b = bf16[32,512]{1,0:T(8,128)(2,1)S(1)} collective-permute-done((bf16[32,512]{1,0:T(8,128)(2,1)S(1)}, bf16[32,512]{1,0:T(8,128)(2,1)S(1)}, u32[]{:S(2)}, u32[]{:S(2)}) %collective-permute-start.2) | collective-permute-done | bytes 32800 | tf_op jit(solution)/shard_map/ppermute | solution.py:491
  22.1 2.3 %collective-permute-done.3.c = bf16[32,512]{1,0:T(8,128)(2,1)S(1)} collective-permute-done((bf16[32,512]{1,0:T(8,128)(2,1)S(1)}, bf16[32,512]{1,0:T(8,128)(2,1)S(1)}, u32[]{:S(2)}, u32[]{:S(2)}) %collective-permute-start.3) | collective-permute-done | bytes 32800 | tf_op jit(solution)/shard_map/ppermute | solution.py:491
  24.5 3.9 %collective-permute-start.4 = (bf16[32,512]{1,0:T(8,128)(2,1)S(1)}, bf16[32,512]{1,0:T(8,128)(2,1)S(1)}, u32[]{:S(2)}, u32[]{:S(2)}) collective-permute-start(bf16[32,512]{1,0:T(8,128)(2,1)S(1)} %share_sum.1.share), channel_id=1, source_target_pairs={{0,8},{16,24},{32,40},{48,56},{64,72},{80,88},{96,104},{112,120},{... | collective-permute-start | bytes 98312 | tf_op jit(solution)/shard_map/ppermute | solution.py:516
  28.3 1.1 %collective-permute-start.15 = (bf16[6,2,128,128]{3,2,1,0:T(8,128)(2,1)S(1)}, bf16[6,2,128,128]{3,2,1,0:T(8,128)(2,1)S(1)}, u32[]{:S(2)}, u32[]{:S(2)}) collective-permute-start(bf16[6,2,128,128]{3,2,1,0:T(8,128)(2,1)S(1)} %collective-permute-done.14), channel_id=1, source_target_pairs={{0,48},{16,0},{32,16},{48,32},{64,112},{80,64},{96,80},{112,96},{1... | collective-permute-start | bytes 1179656 | tf_op jit(solution)/shard_map/ppermute | solution.py:517
  29.4 3.0 %collective-permute-start.17 = (bf16[12,2,128,128]{3,2,1,0:T(8,128)(2,1)S(1)}, bf16[12,2,128,128]{3,2,1,0:T(8,128)(2,1)S(1)}, u32[]{:S(2)}, u32[]{:S(2)}) collective-permute-start(bf16[12,2,128,128]{3,2,1,0:T(8,128)(2,1)S(1)} %get-tuple-element.46), channel_id=1, source_target_pairs={{0,16},{8,24},{16,32},{24,40},{32,48},{40,56},{56,72},{64,80},{72,... | collective-permute-start | bytes 2359304 | tf_op jit(solution)/shard_map/ppermute | solution.py:524
  32.4 1.8 %collective-permute-done.4.m0 = bf16[32,512]{1,0:T(8,128)(2,1)S(1)} collective-permute-done((bf16[32,512]{1,0:T(8,128)(2,1)S(1)}, bf16[32,512]{1,0:T(8,128)(2,1)S(1)}, u32[]{:S(2)}, u32[]{:S(2)}) %collective-permute-start.4) | collective-permute-done | bytes 32800 | tf_op jit(solution)/shard_map/ppermute | solution.py:516
  34.2 1.3 %collective-permute-start.18 = (bf16[12,2,128,128]{3,2,1,0:T(8,128)(2,1)S(1)}, bf16[12,2,128,128]{3,2,1,0:T(8,128)(2,1)S(1)}, u32[]{:S(2)}, u32[]{:S(2)}) collective-permute-start(bf16[12,2,128,128]{3,2,1,0:T(8,128)(2,1)S(1)} %get-tuple-element.46), channel_id=1, source_target_pairs={{48,64},{112,128},{176,192},{240,0},{49,65},{113,129},{177,193},{2... | collective-permute-start | bytes 2359304 | tf_op jit(solution)/shard_map/ppermute | solution.py:525
  35.8 0.8 %collective-permute-start.6 = (bf16[32,512]{1,0:T(8,128)(2,1)S(1)}, bf16[32,512]{1,0:T(8,128)(2,1)S(1)}, u32[]{:S(2)}, u32[]{:S(2)}) collective-permute-start(bf16[32,512]{1,0:T(8,128)(2,1)S(1)} %collective-permute-done.4.m0), channel_id=1, source_target_pairs={{0,2},{1,3},{2,4},{3,5},{4,6},{5,7},{6,0},{7,1},{8,10},{9,11},{10,... | collective-permute-start | bytes 98312 | tf_op jit(solution)/shard_map/ppermute | solution.py:491
  36.5 0.9 %collective-permute-start.7 = (bf16[32,512]{1,0:T(8,128)(2,1)S(1)}, bf16[32,512]{1,0:T(8,128)(2,1)S(1)}, u32[]{:S(2)}, u32[]{:S(2)}) collective-permute-start(bf16[32,512]{1,0:T(8,128)(2,1)S(1)} %collective-permute-done.4.m0), channel_id=1, source_target_pairs={{0,4},{1,5},{2,6},{3,7},{4,0},{5,1},{6,2},{7,3},{8,12},{9,13},{10,... | collective-permute-start | bytes 98312 | tf_op jit(solution)/shard_map/ppermute | solution.py:491
  37.9 1.9 %collective-permute-done.6.m1 = bf16[32,512]{1,0:T(8,128)(2,1)S(1)} collective-permute-done((bf16[32,512]{1,0:T(8,128)(2,1)S(1)}, bf16[32,512]{1,0:T(8,128)(2,1)S(1)}, u32[]{:S(2)}, u32[]{:S(2)}) %collective-permute-start.6) | collective-permute-done | bytes 32800 | tf_op jit(solution)/shard_map/ppermute | solution.py:491
  39.8 2.2 %collective-permute-done.7.m2 = bf16[32,512]{1,0:T(8,128)(2,1)S(1)} collective-permute-done((bf16[32,512]{1,0:T(8,128)(2,1)S(1)}, bf16[32,512]{1,0:T(8,128)(2,1)S(1)}, u32[]{:S(2)}, u32[]{:S(2)}) %collective-permute-start.7) | collective-permute-done | bytes 32800 | tf_op jit(solution)/shard_map/ppermute | solution.py:491
  41.9 1.1 %collective-permute-done.8.m3 = bf16[32,512]{1,0:T(8,128)(2,1)S(1)} collective-permute-done((bf16[32,512]{1,0:T(8,128)(2,1)S(1)}, bf16[32,512]{1,0:T(8,128)(2,1)S(1)}, u32[]{:S(2)}, u32[]{:S(2)}) %collective-permute-start.8) | collective-permute-done | bytes 32800 | tf_op jit(solution)/shard_map/ppermute | solution.py:491
  43.0 4.8 %collective-permute-start.16 = (bf16[6,2,128,128]{3,2,1,0:T(8,128)(2,1)S(1)}, bf16[6,2,128,128]{3,2,1,0:T(8,128)(2,1)S(1)}, u32[]{:S(2)}, u32[]{:S(2)}) collective-permute-start(bf16[6,2,128,128]{3,2,1,0:T(8,128)(2,1)S(1)} %collective-permute-done.15), channel_id=1, source_target_pairs={{0,48},{16,64},{32,16},{48,32},{64,112},{80,128},{96,80},{112,96},... | collective-permute-start | bytes 1179656 | tf_op jit(solution)/shard_map/ppermute | solution.py:530
  48.3 0.7 %collective-permute-done.9.n0 = bf16[32,512]{1,0:T(8,128)(2,1)S(1)} collective-permute-done((bf16[32,512]{1,0:T(8,128)(2,1)S(1)}, bf16[32,512]{1,0:T(8,128)(2,1)S(1)}, u32[]{:S(2)}, u32[]{:S(2)}) %collective-permute-start.9) | collective-permute-done | bytes 32800 | tf_op jit(solution)/shard_map/ppermute | solution.py:494
  49.5 0.7 %collective-permute-done.11.n2 = bf16[32,512]{1,0:T(8,128)(2,1)S(1)} collective-permute-done((bf16[32,512]{1,0:T(8,128)(2,1)S(1)}, bf16[32,512]{1,0:T(8,128)(2,1)S(1)}, u32[]{:S(2)}, u32[]{:S(2)}) %collective-permute-start.11) | collective-permute-done | bytes 32800 | tf_op jit(solution)/shard_map/ppermute | solution.py:494
  52.4 4.6 %collective-permute-done.18.late = bf16[12,2,128,128]{3,2,1,0:T(8,128)(2,1)S(1)} collective-permute-done((bf16[12,2,128,128]{3,2,1,0:T(8,128)(2,1)S(1)}, bf16[12,2,128,128]{3,2,1,0:T(8,128)(2,1)S(1)}, u32[]{:S(2)}, u32[]{:S(2)}) %collective-permute-start.18) | collective-permute-done | bytes 786464 | tf_op jit(solution)/shard_map/ppermute | solution.py:525
  57.0 2.1 %patch.1 = bf16[32,2,128,128]{3,2,1,0:T(8,128)(2,1)} custom-call(bf16[16,256]{1,0:T(8,128)(2,1)S(1)} %collective-permute-done.13.moved, bf16[6,2,128,128]{3,2,1,0:T(8,128)(2,1)S(1)} %collective-permute-done.16.back, bf16[14,2,128,128]{3,2,1,0:T(8,128)(2,1)S(1)} %collective-permute-done.5.ahead, bf16[12,2,128,128]{3,2,1,0:T(8,128)(2,1)S(1)} %collective-permute-done.17.soon, ...), custom_call_target="tpu_custom_call" | custom-call | tf_op jit(solution)/shard_map/patch/pallas_call | solution.py:461
  (30 shorter events, 4.4 us)
Async XLA Ops:
  0.6 7.7 %copy-start = (bf16[1,128,2,128,128]{4,3,2,1,0:T(8,128)(2,1)S(1)}, bf16[1,128,2,128,128]{4,3,2,1,0:T(8,128)(2,1)}, u32[]{:S(2)}) copy-start(bf16[1,128,2,128,128]{4,3,2,1,0:T(8,128)(2,1)} %param.13) | copy-start | bytes 25165828
  3.6 32.2 %collective-permute-start.5 = (bf16[14,2,128,128]{3,2,1,0:T(8,128)(2,1)S(1)}, bf16[14,2,128,128]{3,2,1,0:T(8,128)(2,1)S(1)}, u32[]{:S(2)}, u32[]{:S(2)}) collective-permute-start(bf16[14,2,128,128]{3,2,1,0:T(8,128)(2,1)S(1)} %get-tuple-element.33), channel_id=1, source_target_pairs={{0,16},{16,32},{32,48},{48,64},{64,80},{80,96},{96,112},{112,128},... | collective-permute-start | bytes 2752520 | tf_op jit(solution)/shard_map/ppermute | solution.py:500
  5.2 23.2 %collective-permute-start.14 = (bf16[6,2,128,128]{3,2,1,0:T(8,128)(2,1)S(1)}, bf16[6,2,128,128]{3,2,1,0:T(8,128)(2,1)S(1)}, u32[]{:S(2)}, u32[]{:S(2)}) collective-permute-start(bf16[6,2,128,128]{3,2,1,0:T(8,128)(2,1)S(1)} %get-tuple-element.41), channel_id=1, source_target_pairs={{0,48},{16,0},{32,16},{48,32},{64,112},{80,64},{96,80},{112,96},{1... | collective-permute-start | bytes 1179656 | tf_op jit(solution)/shard_map/ppermute | solution.py:507
  8.3 8.1 %copy-start.1 = (bf16[32,512]{1,0:T(8,128)(2,1)S(1)}, bf16[32,512]{1,0:T(8,128)(2,1)}, u32[]{:S(2)}) copy-start(bf16[32,512]{1,0:T(8,128)(2,1)} %residual.1) | copy-start | bytes 98308
  8.3 27.2 %copy-start.3 = (bf16[4096,2,128]{2,1,0:T(2,128)(2,1)S(1)}, bf16[4096,2,128]{2,1,0:T(2,128)(2,1)}, u32[]{:S(2)}) copy-start(bf16[4096,2,128]{2,1,0:T(2,128)(2,1)} %param.18) | copy-start | bytes 6291460
  14.7 35.6 %copy-start.2 = (f32[4096]{0:T(1024)S(1)}, f32[4096]{0:T(1024)}, u32[]{:S(2)}) copy-start(f32[4096]{0:T(1024)} %gain.1) | copy-start | bytes 49156
  14.8 1.6 %collective-permute-start = (f32[4,32,512]{2,1,0:T(8,128)S(1)}, f32[4,32,512]{2,1,0:T(8,128)S(1)}, u32[]{:S(2)}, u32[]{:S(2)}) collective-permute-start(f32[4,32,512]{2,1,0:T(8,128)S(1)} %get-tuple-element.27), channel_id=1, source_target_pairs={{0,1},{1,0},{2,3},{3,2},{4,5},{5,4},{6,7},{7,6},{8,9},{9,8},{10,11... | collective-permute-start | bytes 786440 | tf_op jit(solution)/shard_map/ppermute | solution.py:494
  16.4 4.0 %collective-permute-start.1 = (bf16[32,512]{1,0:T(8,128)(2,1)S(1)}, bf16[32,512]{1,0:T(8,128)(2,1)S(1)}, u32[]{:S(2)}, u32[]{:S(2)}) collective-permute-start(bf16[32,512]{1,0:T(8,128)(2,1)S(1)} %get-tuple-element.29), channel_id=1, source_target_pairs={{0,2},{1,3},{2,4},{3,5},{4,6},{5,7},{6,0},{7,1},{8,10},{9,11},{10,... | collective-permute-start | bytes 98312 | tf_op jit(solution)/shard_map/ppermute | solution.py:491
  16.7 5.4 %collective-permute-start.2 = (bf16[32,512]{1,0:T(8,128)(2,1)S(1)}, bf16[32,512]{1,0:T(8,128)(2,1)S(1)}, u32[]{:S(2)}, u32[]{:S(2)}) collective-permute-start(bf16[32,512]{1,0:T(8,128)(2,1)S(1)} %get-tuple-element.30), channel_id=1, source_target_pairs={{0,4},{1,5},{2,6},{3,7},{4,0},{5,1},{6,2},{7,3},{8,12},{9,13},{10,... | collective-permute-start | bytes 98312 | tf_op jit(solution)/shard_map/ppermute | solution.py:491
  19.3 5.1 %collective-permute-start.3 = (bf16[32,512]{1,0:T(8,128)(2,1)S(1)}, bf16[32,512]{1,0:T(8,128)(2,1)S(1)}, u32[]{:S(2)}, u32[]{:S(2)}) collective-permute-start(bf16[32,512]{1,0:T(8,128)(2,1)S(1)} %get-tuple-element.31), channel_id=1, source_target_pairs={{0,6},{1,7},{2,0},{3,1},{4,2},{5,3},{6,4},{7,5},{8,14},{9,15},{10,... | collective-permute-start | bytes 98312 | tf_op jit(solution)/shard_map/ppermute | solution.py:491
  24.5 9.7 %collective-permute-start.4 = (bf16[32,512]{1,0:T(8,128)(2,1)S(1)}, bf16[32,512]{1,0:T(8,128)(2,1)S(1)}, u32[]{:S(2)}, u32[]{:S(2)}) collective-permute-start(bf16[32,512]{1,0:T(8,128)(2,1)S(1)} %share_sum.1.share), channel_id=1, source_target_pairs={{0,8},{16,24},{32,40},{48,56},{64,72},{80,88},{96,104},{112,120},{... | collective-permute-start | bytes 98312 | tf_op jit(solution)/shard_map/ppermute | solution.py:516
  28.3 9.5 %collective-permute-start.15 = (bf16[6,2,128,128]{3,2,1,0:T(8,128)(2,1)S(1)}, bf16[6,2,128,128]{3,2,1,0:T(8,128)(2,1)S(1)}, u32[]{:S(2)}, u32[]{:S(2)}) collective-permute-start(bf16[6,2,128,128]{3,2,1,0:T(8,128)(2,1)S(1)} %collective-permute-done.14), channel_id=1, source_target_pairs={{0,48},{16,0},{32,16},{48,32},{64,112},{80,64},{96,80},{112,96},{1... | collective-permute-start | bytes 1179656 | tf_op jit(solution)/shard_map/ppermute | solution.py:517
  29.4 22.9 %collective-permute-start.17 = (bf16[12,2,128,128]{3,2,1,0:T(8,128)(2,1)S(1)}, bf16[12,2,128,128]{3,2,1,0:T(8,128)(2,1)S(1)}, u32[]{:S(2)}, u32[]{:S(2)}) collective-permute-start(bf16[12,2,128,128]{3,2,1,0:T(8,128)(2,1)S(1)} %get-tuple-element.46), channel_id=1, source_target_pairs={{0,16},{8,24},{16,32},{24,40},{32,48},{40,56},{56,72},{64,80},{72,... | collective-permute-start | bytes 2359304 | tf_op jit(solution)/shard_map/ppermute | solution.py:524
  34.2 22.8 %collective-permute-start.18 = (bf16[12,2,128,128]{3,2,1,0:T(8,128)(2,1)S(1)}, bf16[12,2,128,128]{3,2,1,0:T(8,128)(2,1)S(1)}, u32[]{:S(2)}, u32[]{:S(2)}) collective-permute-start(bf16[12,2,128,128]{3,2,1,0:T(8,128)(2,1)S(1)} %get-tuple-element.46), channel_id=1, source_target_pairs={{48,64},{112,128},{176,192},{240,0},{49,65},{113,129},{177,193},{2... | collective-permute-start | bytes 2359304 | tf_op jit(solution)/shard_map/ppermute | solution.py:525
  35.8 4.0 %collective-permute-start.6 = (bf16[32,512]{1,0:T(8,128)(2,1)S(1)}, bf16[32,512]{1,0:T(8,128)(2,1)S(1)}, u32[]{:S(2)}, u32[]{:S(2)}) collective-permute-start(bf16[32,512]{1,0:T(8,128)(2,1)S(1)} %collective-permute-done.4.m0), channel_id=1, source_target_pairs={{0,2},{1,3},{2,4},{3,5},{4,6},{5,7},{6,0},{7,1},{8,10},{9,11},{10,... | collective-permute-start | bytes 98312 | tf_op jit(solution)/shard_map/ppermute | solution.py:491
  36.5 5.4 %collective-permute-start.7 = (bf16[32,512]{1,0:T(8,128)(2,1)S(1)}, bf16[32,512]{1,0:T(8,128)(2,1)S(1)}, u32[]{:S(2)}, u32[]{:S(2)}) collective-permute-start(bf16[32,512]{1,0:T(8,128)(2,1)S(1)} %collective-permute-done.4.m0), channel_id=1, source_target_pairs={{0,4},{1,5},{2,6},{3,7},{4,0},{5,1},{6,2},{7,3},{8,12},{9,13},{10,... | collective-permute-start | bytes 98312 | tf_op jit(solution)/shard_map/ppermute | solution.py:491
  37.9 5.1 %collective-permute-start.8 = (bf16[32,512]{1,0:T(8,128)(2,1)S(1)}, bf16[32,512]{1,0:T(8,128)(2,1)S(1)}, u32[]{:S(2)}, u32[]{:S(2)}) collective-permute-start(bf16[32,512]{1,0:T(8,128)(2,1)S(1)} %collective-permute-done.4.m0), channel_id=1, source_target_pairs={{0,6},{1,7},{2,0},{3,1},{4,2},{5,3},{6,4},{7,5},{8,14},{9,15},{10,... | collective-permute-start | bytes 98312 | tf_op jit(solution)/shard_map/ppermute | solution.py:491
  43.0 14.0 %collective-permute-start.16 = (bf16[6,2,128,128]{3,2,1,0:T(8,128)(2,1)S(1)}, bf16[6,2,128,128]{3,2,1,0:T(8,128)(2,1)S(1)}, u32[]{:S(2)}, u32[]{:S(2)}) collective-permute-start(bf16[6,2,128,128]{3,2,1,0:T(8,128)(2,1)S(1)} %collective-permute-done.15), channel_id=1, source_target_pairs={{0,48},{16,64},{32,16},{48,32},{64,112},{80,128},{96,80},{112,96},... | collective-permute-start | bytes 1179656 | tf_op jit(solution)/shard_map/ppermute | solution.py:530
  47.8 1.2 %collective-permute-start.9 = (bf16[32,512]{1,0:T(8,128)(2,1)S(1)}, bf16[32,512]{1,0:T(8,128)(2,1)S(1)}, u32[]{:S(2)}, u32[]{:S(2)}) collective-permute-start(bf16[32,512]{1,0:T(8,128)(2,1)S(1)} %collective-permute-done.4.m0), channel_id=1, source_target_pairs={{0,1},{1,0},{2,3},{3,2},{4,5},{5,4},{6,7},{7,6},{8,9},{9,8},{10,11... | collective-permute-start | bytes 98312 | tf_op jit(solution)/shard_map/ppermute | solution.py:494
  47.8 1.4 %collective-permute-start.10 = (bf16[32,512]{1,0:T(8,128)(2,1)S(1)}, bf16[32,512]{1,0:T(8,128)(2,1)S(1)}, u32[]{:S(2)}, u32[]{:S(2)}) collective-permute-start(bf16[32,512]{1,0:T(8,128)(2,1)S(1)} %collective-permute-done.6.m1), channel_id=1, source_target_pairs={{0,1},{1,0},{2,3},{3,2},{4,5},{5,4},{6,7},{7,6},{8,9},{9,8},{10,11... | collective-permute-start | bytes 98312 | tf_op jit(solution)/shard_map/ppermute | solution.py:494
  49.0 1.2 %collective-permute-start.11 = (bf16[32,512]{1,0:T(8,128)(2,1)S(1)}, bf16[32,512]{1,0:T(8,128)(2,1)S(1)}, u32[]{:S(2)}, u32[]{:S(2)}) collective-permute-start(bf16[32,512]{1,0:T(8,128)(2,1)S(1)} %collective-permute-done.7.m2), channel_id=1, source_target_pairs={{0,1},{1,0},{2,3},{3,2},{4,5},{5,4},{6,7},{7,6},{8,9},{9,8},{10,11... | collective-permute-start | bytes 98312 | tf_op jit(solution)/shard_map/ppermute | solution.py:494
  49.1 1.2 %collective-permute-start.12 = (bf16[32,512]{1,0:T(8,128)(2,1)S(1)}, bf16[32,512]{1,0:T(8,128)(2,1)S(1)}, u32[]{:S(2)}, u32[]{:S(2)}) collective-permute-start(bf16[32,512]{1,0:T(8,128)(2,1)S(1)} %collective-permute-done.8.m3), channel_id=1, source_target_pairs={{0,1},{1,0},{2,3},{3,2},{4,5},{5,4},{6,7},{7,6},{8,9},{9,8},{10,11... | collective-permute-start | bytes 98312 | tf_op jit(solution)/shard_map/ppermute | solution.py:494
  51.0 1.3 %collective-permute-start.13 = (bf16[16,256]{1,0:T(8,128)(2,1)S(1)}, bf16[16,256]{1,0:T(8,128)(2,1)S(1)}, u32[]{:S(2)}, u32[]{:S(2)}) collective-permute-start(bf16[16,256]{1,0:T(8,128)(2,1)S(1)} %get-tuple-element.40), channel_id=1, source_target_pairs={{8,24},{24,40},{40,56},{56,72},{72,88},{88,104},{104,120},{120,136... | collective-permute-start | bytes 24584 | tf_op jit(solution)/shard_map/ppermute | solution.py:534

commit v5 on v4

--- a/solution.py
+++ b/solution.py
@@ -20,7 +20,7 @@
 SENT = 2 * MIG
 GROUP = 16
 PAD = 8
-PARTS = (6, 14, 12)
+PARTS = (6, 15, 11)
 SCALE = HDIM ** (-0.5)
 F32 = jnp.float32
 BF16 = jnp.bfloat16

time: 59.4 us -> 58.6 us (0.987)
  waiting for transfers between devices: 20.2 us -> 17.8 us
  starting transfers between devices: 25 us -> 26.5 us
    ppermute x1, waiting for transfers between devices: 4.62 us -> 3.02 us  [local(): late = lax.ppermute(after(later, arrived), ('inst', 'section'), turns)]
    ppermute x1, starting transfers between devices: 1.07 us -> 0.09 us  [local(): back = lax.ppermute(after(back, share), 'inst', down)]
    ppermute x1, starting transfers between devices: 4.76 us -> 5.72 us  [local(): back = lax.ppermute(after(back, *mine), 'inst', turn)]
    ppermute x1, starting transfers between devices: 3.87 us -> 4.74 us  [local(): arrived = lax.ppermute(share, ('inst', 'section'), across_z)]
  transfers between devices with their start and end apart: 19 -> 19, of which waited for: 13 -> 12; matrix products, arithmetic and copies ran while one was open for 0% -> 0% of each run, Pallas kernels for 13% -> 13%
where the time goes in v5:
time: 58.6 us; the launch traced here: 58.3 us
  starting transfers between devices  26.5 us (45%)
  waiting for transfers between devices  17.8 us (30%)
  Pallas kernels  12.8 us (22%)
  between operations  0.94 us (2%)
    ppermute x6, waiting for transfers between devices, across(): lax.ppermute(value, 'tensor', [(i, (i + 2 * by) % 8) for i in range(8)])  9.8 us
    pallas_call x1, Pallas kernels, first_layer(): pl.pallas_call(first_kernel, out_shape=(jax.ShapeDtypeStruct((REQ, WIDTH)...  6.43 us
    ppermute x1, starting transfers between devices, local(): back = lax.ppermute(after(back, *mine), 'inst', turn)  5.72 us
    ppermute x6, starting transfers between devices, across(): lax.ppermute(value, 'tensor', [(i, (i + 2 * by) % 8) for i in range(8)])  5 us
    ppermute x1, starting transfers between devices, local(): arrived = lax.ppermute(share, ('inst', 'section'), across_z)  4.74 us
    ppermute x1, starting transfers between devices, local(): back = lax.ppermute(back, 'inst', down)  3.19 us
    ppermute x1, starting transfers between devices, local(): lax.ppermute(later, ('inst', 'section'), [p for p in steps if p not in tu...  3.09 us
    ppermute x5, waiting for transfers between devices, to_twin(): return lax.ppermute(value, 'tensor', [(i, i ^ 1) for i in range(8)])  3.08 us
  transfers between devices with their start and end apart: 19, of which 12 were waited for; matrix products, arithmetic and copies ran while one was open for 0% of the time, Pallas kernels for 13%

profile of v5, /device:TPU:24, one launch (start us, length us, event | category | flops | bytes accessed | tf_op | source)
XLA Modules:
  0.0 58.3 jit_solution(10645624060736528149)
XLA Ops:
  0.6 2.9 %gather_pages.1 = (bf16[6,2,128,128]{3,2,1,0:T(8,128)(2,1)S(1)}, bf16[15,2,128,128]{3,2,1,0:T(8,128)(2,1)S(1)}, bf16[11,2,128,128]{3,2,1,0:T(8,128)(2,1)S(1)}) custom-call(s32[4,32]{1,0:T(4,128)} %bitcast.17, s32[32]{0:T(128)} %lengths_in.7, s32[8]{0:T(128)} %ids_in.3, bf16[32,2,128]{2,1,0:T(2,128)(2,1)} %fresh_in.3, bf16[128,2,128,128]{3,2,1,0:T(8,128)(2,1)} %bitcast.9), custom_call_target="tpu_custom_call" | custom-call | tf_op jit(solution)/shard_map/gather_pages/pallas_call | solution.py:186
  3.6 1.6 %collective-permute-start.5 = (bf16[15,2,128,128]{3,2,1,0:T(8,128)(2,1)S(1)}, bf16[15,2,128,128]{3,2,1,0:T(8,128)(2,1)S(1)}, u32[]{:S(2)}, u32[]{:S(2)}) collective-permute-start(bf16[15,2,128,128]{3,2,1,0:T(8,128)(2,1)S(1)} %get-tuple-element.33), channel_id=1, source_target_pairs={{0,16},{16,32},{32,48},{48,64},{64,80},{80,96},{96,112},{112,128},... | collective-permute-start | bytes 2949128 | tf_op jit(solution)/shard_map/ppermute | solution.py:500
  5.2 3.2 %collective-permute-start.14 = (bf16[6,2,128,128]{3,2,1,0:T(8,128)(2,1)S(1)}, bf16[6,2,128,128]{3,2,1,0:T(8,128)(2,1)S(1)}, u32[]{:S(2)}, u32[]{:S(2)}) collective-permute-start(bf16[6,2,128,128]{3,2,1,0:T(8,128)(2,1)S(1)} %get-tuple-element.41), channel_id=1, source_target_pairs={{0,48},{16,0},{32,16},{48,32},{64,112},{80,64},{96,80},{112,96},{1... | collective-permute-start | bytes 1179656 | tf_op jit(solution)/shard_map/ppermute | solution.py:507
  8.4 6.4 %first_layer.1 = (bf16[32,512]{1,0:T(8,128)(2,1)S(1)}, f32[4,32,512]{2,1,0:T(8,128)S(1)}, f32[4,32,512]{2,1,0:T(8,128)S(1)}, bf16[4096,512]{1,0:T(8,128)(2,1)S(1)}) custom-call(s32[4,32]{1,0:T(4,128)} %bitcast.18, s32[32]{0:T(128)} %lengths_in.7, bf16[32,512]{1,0:T(8,128)(2,1)} %query_in.1, bf16[32,2,128]{2,1,0:T(2,128)(2,1)} %fresh_in.3, ...), custom_call_target="tpu_custom_call" | custom-call | tf_op jit(solution)/shard_map/first_layer/pallas_call | solution.py:254
  15.0 1.5 %collective-permute-done.got = f32[4,32,512]{2,1,0:T(8,128)S(1)} collective-permute-done((f32[4,32,512]{2,1,0:T(8,128)S(1)}, f32[4,32,512]{2,1,0:T(8,128)S(1)}, u32[]{:S(2)}, u32[]{:S(2)}) %collective-permute-start) | collective-permute-done | bytes 262176 | tf_op jit(solution)/shard_map/ppermute | solution.py:494
  16.8 2.6 %collective-permute-start.2 = (bf16[32,512]{1,0:T(8,128)(2,1)S(1)}, bf16[32,512]{1,0:T(8,128)(2,1)S(1)}, u32[]{:S(2)}, u32[]{:S(2)}) collective-permute-start(bf16[32,512]{1,0:T(8,128)(2,1)S(1)} %get-tuple-element.30), channel_id=1, source_target_pairs={{0,4},{1,5},{2,6},{3,7},{4,0},{5,1},{6,2},{7,3},{8,12},{9,13},{10,... | collective-permute-start | bytes 98312 | tf_op jit(solution)/shard_map/ppermute | solution.py:491
  19.4 1.1 %collective-permute-done.1.a = bf16[32,512]{1,0:T(8,128)(2,1)S(1)} collective-permute-done((bf16[32,512]{1,0:T(8,128)(2,1)S(1)}, bf16[32,512]{1,0:T(8,128)(2,1)S(1)}, u32[]{:S(2)}, u32[]{:S(2)}) %collective-permute-start.1) | collective-permute-done | bytes 32800 | tf_op jit(solution)/shard_map/ppermute | solution.py:491
  20.5 1.7 %collective-permute-done.2.b = bf16[32,512]{1,0:T(8,128)(2,1)S(1)} collective-permute-done((bf16[32,512]{1,0:T(8,128)(2,1)S(1)}, bf16[32,512]{1,0:T(8,128)(2,1)S(1)}, u32[]{:S(2)}, u32[]{:S(2)}) %collective-permute-start.2) | collective-permute-done | bytes 32800 | tf_op jit(solution)/shard_map/ppermute | solution.py:491
  22.2 2.3 %collective-permute-done.3.c = bf16[32,512]{1,0:T(8,128)(2,1)S(1)} collective-permute-done((bf16[32,512]{1,0:T(8,128)(2,1)S(1)}, bf16[32,512]{1,0:T(8,128)(2,1)S(1)}, u32[]{:S(2)}, u32[]{:S(2)}) %collective-permute-start.3) | collective-permute-done | bytes 32800 | tf_op jit(solution)/shard_map/ppermute | solution.py:491
  24.7 4.7 %collective-permute-start.4 = (bf16[32,512]{1,0:T(8,128)(2,1)S(1)}, bf16[32,512]{1,0:T(8,128)(2,1)S(1)}, u32[]{:S(2)}, u32[]{:S(2)}) collective-permute-start(bf16[32,512]{1,0:T(8,128)(2,1)S(1)} %share_sum.1.share), channel_id=1, source_target_pairs={{0,8},{16,24},{32,40},{48,56},{64,72},{80,88},{96,104},{112,120},{... | collective-permute-start | bytes 98312 | tf_op jit(solution)/shard_map/ppermute | solution.py:516
  29.4 3.1 %collective-permute-start.17 = (bf16[11,2,128,128]{3,2,1,0:T(8,128)(2,1)S(1)}, bf16[11,2,128,128]{3,2,1,0:T(8,128)(2,1)S(1)}, u32[]{:S(2)}, u32[]{:S(2)}) collective-permute-start(bf16[11,2,128,128]{3,2,1,0:T(8,128)(2,1)S(1)} %get-tuple-element.46), channel_id=1, source_target_pairs={{0,16},{8,24},{16,32},{24,40},{32,48},{40,56},{56,72},{64,80},{72,... | collective-permute-start | bytes 2162696 | tf_op jit(solution)/shard_map/ppermute | solution.py:524
  32.5 1.9 %collective-permute-done.4.m0 = bf16[32,512]{1,0:T(8,128)(2,1)S(1)} collective-permute-done((bf16[32,512]{1,0:T(8,128)(2,1)S(1)}, bf16[32,512]{1,0:T(8,128)(2,1)S(1)}, u32[]{:S(2)}, u32[]{:S(2)}) %collective-permute-start.4) | collective-permute-done | bytes 32800 | tf_op jit(solution)/shard_map/ppermute | solution.py:516
  34.4 1.3 %collective-permute-start.18 = (bf16[11,2,128,128]{3,2,1,0:T(8,128)(2,1)S(1)}, bf16[11,2,128,128]{3,2,1,0:T(8,128)(2,1)S(1)}, u32[]{:S(2)}, u32[]{:S(2)}) collective-permute-start(bf16[11,2,128,128]{3,2,1,0:T(8,128)(2,1)S(1)} %get-tuple-element.46), channel_id=1, source_target_pairs={{48,64},{112,128},{176,192},{240,0},{49,65},{113,129},{177,193},{2... | collective-permute-start | bytes 2162696 | tf_op jit(solution)/shard_map/ppermute | solution.py:525
  36.0 0.8 %collective-permute-start.6 = (bf16[32,512]{1,0:T(8,128)(2,1)S(1)}, bf16[32,512]{1,0:T(8,128)(2,1)S(1)}, u32[]{:S(2)}, u32[]{:S(2)}) collective-permute-start(bf16[32,512]{1,0:T(8,128)(2,1)S(1)} %collective-permute-done.4.m0), channel_id=1, source_target_pairs={{0,2},{1,3},{2,4},{3,5},{4,6},{5,7},{6,0},{7,1},{8,10},{9,11},{10,... | collective-permute-start | bytes 98312 | tf_op jit(solution)/shard_map/ppermute | solution.py:491
  36.7 0.9 %collective-permute-start.7 = (bf16[32,512]{1,0:T(8,128)(2,1)S(1)}, bf16[32,512]{1,0:T(8,128)(2,1)S(1)}, u32[]{:S(2)}, u32[]{:S(2)}) collective-permute-start(bf16[32,512]{1,0:T(8,128)(2,1)S(1)} %collective-permute-done.4.m0), channel_id=1, source_target_pairs={{0,4},{1,5},{2,6},{3,7},{4,0},{5,1},{6,2},{7,3},{8,12},{9,13},{10,... | collective-permute-start | bytes 98312 | tf_op jit(solution)/shard_map/ppermute | solution.py:491
  38.1 1.9 %collective-permute-done.6.m1 = bf16[32,512]{1,0:T(8,128)(2,1)S(1)} collective-permute-done((bf16[32,512]{1,0:T(8,128)(2,1)S(1)}, bf16[32,512]{1,0:T(8,128)(2,1)S(1)}, u32[]{:S(2)}, u32[]{:S(2)}) %collective-permute-start.6) | collective-permute-done | bytes 32800 | tf_op jit(solution)/shard_map/ppermute | solution.py:491
  40.0 2.2 %collective-permute-done.7.m2 = bf16[32,512]{1,0:T(8,128)(2,1)S(1)} collective-permute-done((bf16[32,512]{1,0:T(8,128)(2,1)S(1)}, bf16[32,512]{1,0:T(8,128)(2,1)S(1)}, u32[]{:S(2)}, u32[]{:S(2)}) %collective-permute-start.7) | collective-permute-done | bytes 32800 | tf_op jit(solution)/shard_map/ppermute | solution.py:491
  42.8 5.7 %collective-permute-start.16 = (bf16[6,2,128,128]{3,2,1,0:T(8,128)(2,1)S(1)}, bf16[6,2,128,128]{3,2,1,0:T(8,128)(2,1)S(1)}, u32[]{:S(2)}, u32[]{:S(2)}) collective-permute-start(bf16[6,2,128,128]{3,2,1,0:T(8,128)(2,1)S(1)} %collective-permute-done.15), channel_id=1, source_target_pairs={{0,48},{16,64},{32,16},{48,32},{64,112},{80,128},{96,80},{112,96},... | collective-permute-start | bytes 1179656 | tf_op jit(solution)/shard_map/ppermute | solution.py:530
  49.0 0.7 %collective-permute-done.9.n0 = bf16[32,512]{1,0:T(8,128)(2,1)S(1)} collective-permute-done((bf16[32,512]{1,0:T(8,128)(2,1)S(1)}, bf16[32,512]{1,0:T(8,128)(2,1)S(1)}, u32[]{:S(2)}, u32[]{:S(2)}) %collective-permute-start.9) | collective-permute-done | bytes 32800 | tf_op jit(solution)/shard_map/ppermute | solution.py:494
  50.2 0.7 %collective-permute-done.11.n2 = bf16[32,512]{1,0:T(8,128)(2,1)S(1)} collective-permute-done((bf16[32,512]{1,0:T(8,128)(2,1)S(1)}, bf16[32,512]{1,0:T(8,128)(2,1)S(1)}, u32[]{:S(2)}, u32[]{:S(2)}) %collective-permute-start.11) | collective-permute-done | bytes 32800 | tf_op jit(solution)/shard_map/ppermute | solution.py:494
  51.7 0.7 %collective-permute-start.13 = (bf16[16,256]{1,0:T(8,128)(2,1)S(1)}, bf16[16,256]{1,0:T(8,128)(2,1)S(1)}, u32[]{:S(2)}, u32[]{:S(2)}) collective-permute-start(bf16[16,256]{1,0:T(8,128)(2,1)S(1)} %get-tuple-element.40), channel_id=1, source_target_pairs={{8,24},{24,40},{40,56},{56,72},{72,88},{88,104},{104,120},{120,136... | collective-permute-start | bytes 24584 | tf_op jit(solution)/shard_map/ppermute | solution.py:534
  52.4 0.7 %second_layer.1 = bf16[32,512]{1,0:T(8,128)(2,1)} custom-call(s32[4,32]{1,0:T(4,128)} %bitcast.19, s32[32]{0:T(128)} %lengths_in.7, bf16[32,512]{1,0:T(8,128)(2,1)S(1)} %get-tuple-element.25.first_attn, bf16[32,512]{1,0:T(8,128)(2,1)S(1)} %get-tuple-element.37.query, f32[32,256]{1,0:T(8,128)S(1)} %get-tuple-element.38.fresh, ...), custom_call_target="tpu_custom_call" | custom-call | flops 1073741824 | bytes 16777216 | tf_op jit(solution)/shard_map/second_layer/pallas_call | solution.py:405
  53.1 3.0 %collective-permute-done.18.late = bf16[11,2,128,128]{3,2,1,0:T(8,128)(2,1)S(1)} collective-permute-done((bf16[11,2,128,128]{3,2,1,0:T(8,128)(2,1)S(1)}, bf16[11,2,128,128]{3,2,1,0:T(8,128)(2,1)S(1)}, u32[]{:S(2)}, u32[]{:S(2)}) %collective-permute-start.18) | collective-permute-done | bytes 720928 | tf_op jit(solution)/shard_map/ppermute | solution.py:525
  56.1 2.1 %patch.1 = bf16[32,2,128,128]{3,2,1,0:T(8,128)(2,1)} custom-call(bf16[16,256]{1,0:T(8,128)(2,1)S(1)} %collective-permute-done.13.moved, bf16[6,2,128,128]{3,2,1,0:T(8,128)(2,1)S(1)} %collective-permute-done.16.back, bf16[15,2,128,128]{3,2,1,0:T(8,128)(2,1)S(1)} %collective-permute-done.5.ahead, bf16[11,2,128,128]{3,2,1,0:T(8,128)(2,1)S(1)} %collective-permute-done.17.soon, ...), custom_call_target="tpu_custom_call" | custom-call | tf_op jit(solution)/shard_map/patch/pallas_call | solution.py:461
  (30 shorter events, 3.7 us)
Async XLA Ops:
  0.6 7.8 %copy-start = (bf16[1,128,2,128,128]{4,3,2,1,0:T(8,128)(2,1)S(1)}, bf16[1,128,2,128,128]{4,3,2,1,0:T(8,128)(2,1)}, u32[]{:S(2)}) copy-start(bf16[1,128,2,128,128]{4,3,2,1,0:T(8,128)(2,1)} %param.13) | copy-start | bytes 25165828
  3.6 32.4 %collective-permute-start.5 = (bf16[15,2,128,128]{3,2,1,0:T(8,128)(2,1)S(1)}, bf16[15,2,128,128]{3,2,1,0:T(8,128)(2,1)S(1)}, u32[]{:S(2)}, u32[]{:S(2)}) collective-permute-start(bf16[15,2,128,128]{3,2,1,0:T(8,128)(2,1)S(1)} %get-tuple-element.33), channel_id=1, source_target_pairs={{0,16},{16,32},{32,48},{48,64},{64,80},{80,96},{96,112},{112,128},... | collective-permute-start | bytes 2949128 | tf_op jit(solution)/shard_map/ppermute | solution.py:500
  5.2 19.4 %collective-permute-start.14 = (bf16[6,2,128,128]{3,2,1,0:T(8,128)(2,1)S(1)}, bf16[6,2,128,128]{3,2,1,0:T(8,128)(2,1)S(1)}, u32[]{:S(2)}, u32[]{:S(2)}) collective-permute-start(bf16[6,2,128,128]{3,2,1,0:T(8,128)(2,1)S(1)} %get-tuple-element.41), channel_id=1, source_target_pairs={{0,48},{16,0},{32,16},{48,32},{64,112},{80,64},{96,80},{112,96},{1... | collective-permute-start | bytes 1179656 | tf_op jit(solution)/shard_map/ppermute | solution.py:507
  8.4 8.1 %copy-start.1 = (bf16[32,512]{1,0:T(8,128)(2,1)S(1)}, bf16[32,512]{1,0:T(8,128)(2,1)}, u32[]{:S(2)}) copy-start(bf16[32,512]{1,0:T(8,128)(2,1)} %residual.1) | copy-start | bytes 98308
  8.4 27.3 %copy-start.3 = (bf16[4096,2,128]{2,1,0:T(2,128)(2,1)S(1)}, bf16[4096,2,128]{2,1,0:T(2,128)(2,1)}, u32[]{:S(2)}) copy-start(bf16[4096,2,128]{2,1,0:T(2,128)(2,1)} %param.18) | copy-start | bytes 6291460
  14.9 36.2 %copy-start.2 = (f32[4096]{0:T(1024)S(1)}, f32[4096]{0:T(1024)}, u32[]{:S(2)}) copy-start(f32[4096]{0:T(1024)} %gain.1) | copy-start | bytes 49156
  14.9 1.6 %collective-permute-start = (f32[4,32,512]{2,1,0:T(8,128)S(1)}, f32[4,32,512]{2,1,0:T(8,128)S(1)}, u32[]{:S(2)}, u32[]{:S(2)}) collective-permute-start(f32[4,32,512]{2,1,0:T(8,128)S(1)} %get-tuple-element.27), channel_id=1, source_target_pairs={{0,1},{1,0},{2,3},{3,2},{4,5},{5,4},{6,7},{7,6},{8,9},{9,8},{10,11... | collective-permute-start | bytes 786440 | tf_op jit(solution)/shard_map/ppermute | solution.py:494
  16.5 4.0 %collective-permute-start.1 = (bf16[32,512]{1,0:T(8,128)(2,1)S(1)}, bf16[32,512]{1,0:T(8,128)(2,1)S(1)}, u32[]{:S(2)}, u32[]{:S(2)}) collective-permute-start(bf16[32,512]{1,0:T(8,128)(2,1)S(1)} %get-tuple-element.29), channel_id=1, source_target_pairs={{0,2},{1,3},{2,4},{3,5},{4,6},{5,7},{6,0},{7,1},{8,10},{9,11},{10,... | collective-permute-start | bytes 98312 | tf_op jit(solution)/shard_map/ppermute | solution.py:491
  16.8 5.4 %collective-permute-start.2 = (bf16[32,512]{1,0:T(8,128)(2,1)S(1)}, bf16[32,512]{1,0:T(8,128)(2,1)S(1)}, u32[]{:S(2)}, u32[]{:S(2)}) collective-permute-start(bf16[32,512]{1,0:T(8,128)(2,1)S(1)} %get-tuple-element.30), channel_id=1, source_target_pairs={{0,4},{1,5},{2,6},{3,7},{4,0},{5,1},{6,2},{7,3},{8,12},{9,13},{10,... | collective-permute-start | bytes 98312 | tf_op jit(solution)/shard_map/ppermute | solution.py:491
  19.4 5.1 %collective-permute-start.3 = (bf16[32,512]{1,0:T(8,128)(2,1)S(1)}, bf16[32,512]{1,0:T(8,128)(2,1)S(1)}, u32[]{:S(2)}, u32[]{:S(2)}) collective-permute-start(bf16[32,512]{1,0:T(8,128)(2,1)S(1)} %get-tuple-element.31), channel_id=1, source_target_pairs={{0,6},{1,7},{2,0},{3,1},{4,2},{5,3},{6,4},{7,5},{8,14},{9,15},{10,... | collective-permute-start | bytes 98312 | tf_op jit(solution)/shard_map/ppermute | solution.py:491
  24.6 13.1 %collective-permute-start.15 = (bf16[6,2,128,128]{3,2,1,0:T(8,128)(2,1)S(1)}, bf16[6,2,128,128]{3,2,1,0:T(8,128)(2,1)S(1)}, u32[]{:S(2)}, u32[]{:S(2)}) collective-permute-start(bf16[6,2,128,128]{3,2,1,0:T(8,128)(2,1)S(1)} %collective-permute-done.14), channel_id=1, source_target_pairs={{0,48},{16,0},{32,16},{48,32},{64,112},{80,64},{96,80},{112,96},{1... | collective-permute-start | bytes 1179656 | tf_op jit(solution)/shard_map/ppermute | solution.py:517
  24.7 9.7 %collective-permute-start.4 = (bf16[32,512]{1,0:T(8,128)(2,1)S(1)}, bf16[32,512]{1,0:T(8,128)(2,1)S(1)}, u32[]{:S(2)}, u32[]{:S(2)}) collective-permute-start(bf16[32,512]{1,0:T(8,128)(2,1)S(1)} %share_sum.1.share), channel_id=1, source_target_pairs={{0,8},{16,24},{32,40},{48,56},{64,72},{80,88},{96,104},{112,120},{... | collective-permute-start | bytes 98312 | tf_op jit(solution)/shard_map/ppermute | solution.py:516
  29.4 23.6 %collective-permute-start.17 = (bf16[11,2,128,128]{3,2,1,0:T(8,128)(2,1)S(1)}, bf16[11,2,128,128]{3,2,1,0:T(8,128)(2,1)S(1)}, u32[]{:S(2)}, u32[]{:S(2)}) collective-permute-start(bf16[11,2,128,128]{3,2,1,0:T(8,128)(2,1)S(1)} %get-tuple-element.46), channel_id=1, source_target_pairs={{0,16},{8,24},{16,32},{24,40},{32,48},{40,56},{56,72},{64,80},{72,... | collective-permute-start | bytes 2162696 | tf_op jit(solution)/shard_map/ppermute | solution.py:524
  34.4 21.7 %collective-permute-start.18 = (bf16[11,2,128,128]{3,2,1,0:T(8,128)(2,1)S(1)}, bf16[11,2,128,128]{3,2,1,0:T(8,128)(2,1)S(1)}, u32[]{:S(2)}, u32[]{:S(2)}) collective-permute-start(bf16[11,2,128,128]{3,2,1,0:T(8,128)(2,1)S(1)} %get-tuple-element.46), channel_id=1, source_target_pairs={{48,64},{112,128},{176,192},{240,0},{49,65},{113,129},{177,193},{2... | collective-permute-start | bytes 2162696 | tf_op jit(solution)/shard_map/ppermute | solution.py:525
  36.0 4.0 %collective-permute-start.6 = (bf16[32,512]{1,0:T(8,128)(2,1)S(1)}, bf16[32,512]{1,0:T(8,128)(2,1)S(1)}, u32[]{:S(2)}, u32[]{:S(2)}) collective-permute-start(bf16[32,512]{1,0:T(8,128)(2,1)S(1)} %collective-permute-done.4.m0), channel_id=1, source_target_pairs={{0,2},{1,3},{2,4},{3,5},{4,6},{5,7},{6,0},{7,1},{8,10},{9,11},{10,... | collective-permute-start | bytes 98312 | tf_op jit(solution)/shard_map/ppermute | solution.py:491
  36.7 5.4 %collective-permute-start.7 = (bf16[32,512]{1,0:T(8,128)(2,1)S(1)}, bf16[32,512]{1,0:T(8,128)(2,1)S(1)}, u32[]{:S(2)}, u32[]{:S(2)}) collective-permute-start(bf16[32,512]{1,0:T(8,128)(2,1)S(1)} %collective-permute-done.4.m0), channel_id=1, source_target_pairs={{0,4},{1,5},{2,6},{3,7},{4,0},{5,1},{6,2},{7,3},{8,12},{9,13},{10,... | collective-permute-start | bytes 98312 | tf_op jit(solution)/shard_map/ppermute | solution.py:491
  37.6 5.1 %collective-permute-start.8 = (bf16[32,512]{1,0:T(8,128)(2,1)S(1)}, bf16[32,512]{1,0:T(8,128)(2,1)S(1)}, u32[]{:S(2)}, u32[]{:S(2)}) collective-permute-start(bf16[32,512]{1,0:T(8,128)(2,1)S(1)} %collective-permute-done.4.m0), channel_id=1, source_target_pairs={{0,6},{1,7},{2,0},{3,1},{4,2},{5,3},{6,4},{7,5},{8,14},{9,15},{10,... | collective-permute-start | bytes 98312 | tf_op jit(solution)/shard_map/ppermute | solution.py:491
  42.8 13.3 %collective-permute-start.16 = (bf16[6,2,128,128]{3,2,1,0:T(8,128)(2,1)S(1)}, bf16[6,2,128,128]{3,2,1,0:T(8,128)(2,1)S(1)}, u32[]{:S(2)}, u32[]{:S(2)}) collective-permute-start(bf16[6,2,128,128]{3,2,1,0:T(8,128)(2,1)S(1)} %collective-permute-done.15), channel_id=1, source_target_pairs={{0,48},{16,64},{32,16},{48,32},{64,112},{80,128},{96,80},{112,96},... | collective-permute-start | bytes 1179656 | tf_op jit(solution)/shard_map/ppermute | solution.py:530
  48.5 1.2 %collective-permute-start.9 = (bf16[32,512]{1,0:T(8,128)(2,1)S(1)}, bf16[32,512]{1,0:T(8,128)(2,1)S(1)}, u32[]{:S(2)}, u32[]{:S(2)}) collective-permute-start(bf16[32,512]{1,0:T(8,128)(2,1)S(1)} %collective-permute-done.4.m0), channel_id=1, source_target_pairs={{0,1},{1,0},{2,3},{3,2},{4,5},{5,4},{6,7},{7,6},{8,9},{9,8},{10,11... | collective-permute-start | bytes 98312 | tf_op jit(solution)/shard_map/ppermute | solution.py:494
  48.5 1.4 %collective-permute-start.10 = (bf16[32,512]{1,0:T(8,128)(2,1)S(1)}, bf16[32,512]{1,0:T(8,128)(2,1)S(1)}, u32[]{:S(2)}, u32[]{:S(2)}) collective-permute-start(bf16[32,512]{1,0:T(8,128)(2,1)S(1)} %collective-permute-done.6.m1), channel_id=1, source_target_pairs={{0,1},{1,0},{2,3},{3,2},{4,5},{5,4},{6,7},{7,6},{8,9},{9,8},{10,11... | collective-permute-start | bytes 98312 | tf_op jit(solution)/shard_map/ppermute | solution.py:494
  49.7 1.2 %collective-permute-start.11 = (bf16[32,512]{1,0:T(8,128)(2,1)S(1)}, bf16[32,512]{1,0:T(8,128)(2,1)S(1)}, u32[]{:S(2)}, u32[]{:S(2)}) collective-permute-start(bf16[32,512]{1,0:T(8,128)(2,1)S(1)} %collective-permute-done.7.m2), channel_id=1, source_target_pairs={{0,1},{1,0},{2,3},{3,2},{4,5},{5,4},{6,7},{7,6},{8,9},{9,8},{10,11... | collective-permute-start | bytes 98312 | tf_op jit(solution)/shard_map/ppermute | solution.py:494
  49.9 1.2 %collective-permute-start.12 = (bf16[32,512]{1,0:T(8,128)(2,1)S(1)}, bf16[32,512]{1,0:T(8,128)(2,1)S(1)}, u32[]{:S(2)}, u32[]{:S(2)}) collective-permute-start(bf16[32,512]{1,0:T(8,128)(2,1)S(1)} %collective-permute-done.8.m3), channel_id=1, source_target_pairs={{0,1},{1,0},{2,3},{3,2},{4,5},{5,4},{6,7},{7,6},{8,9},{9,8},{10,11... | collective-permute-start | bytes 98312 | tf_op jit(solution)/shard_map/ppermute | solution.py:494
  51.7 4.4 %collective-permute-start.13 = (bf16[16,256]{1,0:T(8,128)(2,1)S(1)}, bf16[16,256]{1,0:T(8,128)(2,1)S(1)}, u32[]{:S(2)}, u32[]{:S(2)}) collective-permute-start(bf16[16,256]{1,0:T(8,128)(2,1)S(1)} %get-tuple-element.40), channel_id=1, source_target_pairs={{8,24},{24,40},{40,56},{56,72},{72,88},{88,104},{104,120},{120,136... | collective-permute-start | bytes 24584 | tf_op jit(solution)/shard_map/ppermute | solution.py:534
